TPU v7x, 32 devices: a whole 2x2x4 slice. The times are simulated.
32 devices in a mesh: dp: 16 (over z, x, core), seq: 2 (over y).
Axes of the slice: x: 2, y: 2, z: 4, core: 2. Of those that a mesh axis runs over, the one named last changes fastest.
Arguments:
- tokens: bfloat16 [64, 512, 768], P('dp', 'seq'), may hold values from -6 to 6
- weight_in: bfloat16 [768, 3072], P(('dp', 'seq')), may hold values from -0.21875 to 0.21875
- bias_in: bfloat16 [3072], P(('dp', 'seq')), may hold values from -3 to 3
- weight_out: bfloat16 [3072, 768], P(('dp', 'seq')), may hold values from -0.15625 to 0.15625
- bias_out: bfloat16 [768], P(('dp', 'seq')), may hold values from -2 to 2
- gain_mix: bfloat16 [768], P(('dp', 'seq')), may hold values from 0.099609375 to 1.8984375
- shift_mix: bfloat16 [768], P(('dp', 'seq')), may hold values from -2 to 2
- gain_ffn: bfloat16 [768], P(('dp', 'seq')), may hold values from 0.099609375 to 1.8984375
- shift_ffn: bfloat16 [768], P(('dp', 'seq')), may hold values from -2 to 2
- cotangent: bfloat16 [64, 512, 768], P('dp', 'seq'), may hold values from -6 to 6
Outputs:
- output: bfloat16 [64, 512, 768], P('dp', 'seq')
- grad_tokens: float32 [64, 512, 768], P('dp', 'seq')
- grad_weight_in: float32 [768, 3072], P(('dp', 'seq'))
- grad_bias_in: float32 [3072], P(('dp', 'seq'))
- grad_weight_out: float32 [3072, 768], P(('dp', 'seq'))
- grad_bias_out: float32 [768], P(('dp', 'seq'))
- grad_gain_mix: float32 [768], P(('dp', 'seq'))
- grad_shift_mix: float32 [768], P(('dp', 'seq'))
- grad_gain_ffn: float32 [768], P(('dp', 'seq'))
- grad_shift_ffn: float32 [768], P(('dp', 'seq'))
All inputs are finite; a program needn't handle non-finite values.
Results may differ from a plain program's by a relative error of at most 0.0074.
Values may be sent and summed in bfloat16 or wider, within the bound.
No kernel may reach another device: no remote copies, remote signals or barrier semaphores. Data moves between devices by JAX's collectives and lax.ppermute only.
A program may use at most 192 MiB of HBM per device.

v0:
```python
import functools
import math

import jax
import jax.numpy as jnp
import numpy as np
from jax import lax
from jax.experimental import pallas as pl
from jax.experimental.pallas import tpu as pltpu
from jax.sharding import PartitionSpec as P

EPS = 1e-12
AXES = ("dp", "seq")
BF16 = jnp.bfloat16
F32 = jnp.float32
MIB = 1 << 20
LANES = 128
ERF_T = 0.3275911
ERF_P = (0.254829592, -0.284496736, 1.421413741, -1.453152027, 1.061405429)


def dft_tables(length):
    index = np.arange(length, dtype=np.int64)
    angle = (index[:, None] * index[None, :] % length).astype(np.float64) * (2.0 * math.pi / length)
    scale = length ** (-0.5)
    return np.cos(angle) * scale, np.sin(angle) * scale


def table(values):
    return jnp.asarray(values.astype(np.float32)).astype(BF16)


class Grid:
    def __init__(self, mesh):
        self.dp = mesh.shape["dp"]
        self.seq = mesh.shape["seq"]
        chips = self.dp // 2
        self.low = min(2, chips)
        self.high = chips // self.low
        self.shifts = [
            self.perm(lambda z, x, c, y: ((z + step) % self.high, x, c, y)) for step in range(4)
        ]
        self.ring = self.shifts[1]
        self.across = self.perm(lambda z, x, c, y: (z, (x + 1) % self.low, c, y))
        self.corner = self.perm(
            lambda z, x, c, y: (z, (x + 1) % self.low, c, (y + 1) % self.seq)
        )
        self.cores = self.perm(lambda z, x, c, y: (z, x, 1 - c, y))
        self.blocks = self.perm(lambda z, x, c, y: (z, x, c, (y + 1) % self.seq))
        self.across_0 = self.perm(
            lambda z, x, c, y: (z, (x + 1 - c) % self.low, c, (y + c) % self.seq)
        )
        self.across_1 = self.perm(
            lambda z, x, c, y: (z, (x + c) % self.low, c, (y + 1 - c) % self.seq)
        )
        self.chained = self.high == 4 and self.low == 2 and self.seq == 2

    def index(self, z, x, c, y):
        return ((z * self.low + x) * 2 + c) * self.seq + y

    def perm(self, move):
        return [
            (self.index(z, x, c, y), self.index(*move(z, x, c, y)))
            for z in range(self.high)
            for x in range(self.low)
            for c in range(2)
            for y in range(self.seq)
        ]

    def place(self):
        dp = lax.axis_index("dp")
        return dp // (2 * self.low), dp // 2 % self.low, dp % 2, lax.axis_index("seq")


def send(value, perm):
    return lax.ppermute(value, AXES, perm)


def pick(value, index):
    zero = jnp.uint32(0)
    starts = (index,) + (zero,) * (value.ndim - 1)
    return lax.dynamic_slice(value, starts, (1,) + value.shape[1:])[0]


def dot(a, b):
    return jnp.dot(a, b, preferred_element_type=F32)


def dot_nt(a, b):
    return lax.dot_general(a, b, (((1,), (1,)), ((), ())), preferred_element_type=F32)


def dot_tn(a, b):
    return lax.dot_general(a, b, (((0,), (0,)), ((), ())), preferred_element_type=F32)


def params(mib):
    return pltpu.CompilerParams(vmem_limit_bytes=mib * MIB)


def cost(flops, bytes_accessed, transcendentals=0):
    return pl.CostEstimate(
        flops=int(flops), bytes_accessed=int(bytes_accessed), transcendentals=int(transcendentals)
    )


def row_sum(values):
    return jnp.sum(values, axis=0, keepdims=True)


def after(value, *others):
    return lax.optimization_barrier((value,) + others)[0]


def together(*values):
    return lax.optimization_barrier(values)


def device_number(place, distance, flip_x, flip_y, other_core):
    z, x, c, y = place
    zz = lax.rem(z - distance + 4, 4)
    cc = 1 - c if other_core else c
    xx = x + flip_x - 2 * x * flip_x
    yy = y + flip_y - 2 * y * flip_y
    return ((zz * 2 + xx) * 2 + cc) * 2 + yy


def column_slab(part, index, core):
    group = part + index // 4
    flip_x, flip_y = ((0, 0), (1 - core, core), (core, 1 - core), (1, 1))[group]
    return index % 4, flip_x, flip_y


def pair_slab(part, index, core):
    return part // 2, index, part % 2


def put_slabs(place, refs, slab_of, put):
    for part, ref in enumerate(refs):
        own = len(refs) // 2
        for i in range(ref.shape[0]):
            core = 1 - place[2] if part >= own else place[2]
            where = slab_of(part % own, i, core)
            put(ref, i, device_number(place, *where, part >= own))


def vmem_call(kernel, name, out_shape, mib, work, scratch_shapes=(), places=0, anywhere=0, outside=False, aliases=None):
    def call(*operands):
        here = len(operands) - places - anywhere
        return pl.pallas_call(
            kernel,
            name=name,
            in_specs=[pl.BlockSpec(memory_space=pltpu.SMEM)] * places
            + [pl.BlockSpec(memory_space=pltpu.VMEM)] * here
            + [pl.BlockSpec(memory_space=pl.ANY)] * anywhere,
            out_specs=[pl.BlockSpec(memory_space=pl.ANY if outside else pltpu.VMEM)] * len(out_shape),
            out_shape=[jax.ShapeDtypeStruct(*each) for each in out_shape],
            scratch_shapes=list(scratch_shapes),
            input_output_aliases=aliases or {},
            compiler_params=params(mib),
            cost_estimate=work,
        )(*operands)

    return call


def tile_rows(index, size):
    return pl.ds(pl.multiple_of(index * size, size), size)


def assemble(place, groups, split):
    _, rows, columns = groups[0].shape
    slabs = sum(group.shape[0] for group in groups)
    return vmem_call(
        functools.partial(assemble_kernel, count=len(groups), split=split),
        "assemble_w_in",
        [((slabs * rows, split), BF16), ((slabs, rows, LANES), BF16)],
        2,
        cost(0, 4 * slabs * rows * columns),
        [pltpu.SemaphoreType.DMA((2 * slabs,))],
        places=1,
        anywhere=len(groups),
    )(place, *groups)


def spread_matrix(size, start, total):
    lane = lax.broadcasted_iota(jnp.int32, (LANES, total), 0)
    column = lax.broadcasted_iota(jnp.int32, (LANES, total), 1)
    return lane == start + lax.rem(column, size)


def owner_mask(owners, total):
    owner = lax.broadcasted_iota(jnp.int32, (owners, total), 0)
    column = lax.broadcasted_iota(jnp.int32, (owners, total), 1)
    return lax.div(column, total // owners) == owner


def first_weight_kernel(place_ref, xhat_ref, *refs, count, split):
    groups = refs[:count]
    full_ref, bias_ref, vec_ref, low_ref, low_t_ref, extra_ref = refs[count:]
    rows = groups[0].shape[1]
    place = tuple(place_ref[i] for i in range(4))

    def put(ref, i, at):
        full_ref[tile_rows(at, rows), :] = ref[i, :, :split]
        extra_ref[at] = ref[i, :, split:]

    put_slabs(place, groups, column_slab, put)
    owners, width = extra_ref.shape[0], vec_ref.shape[1]
    line = extra_ref[:, 0, :]
    wide = dot(line, spread_matrix(split // owners, 0, split).astype(BF16))
    bias_ref[...] = row_sum(jnp.where(owner_mask(owners, split), wide, 0.0))
    line = extra_ref[:, 1, :]
    mask = owner_mask(owners, width)
    size = width // owners
    vec_ref[...] = jnp.zeros_like(vec_ref)
    for i in range(5):
        wide = dot(line, spread_matrix(size, i * size, width).astype(BF16))
        vec_ref[i : i + 1, :] = row_sum(jnp.where(mask, wide, 0.0))
    low = (xhat_ref[...] * vec_ref[1:2, :] + vec_ref[2:3, :]).astype(BF16)
    low_ref[...] = low
    low_t_ref[...] = low.T


def first_weight(place, xhat, groups, split):
    _, rows, columns = groups[0].shape
    slabs = sum(group.shape[0] for group in groups)
    count, width = xhat.shape
    return vmem_call(
        functools.partial(first_weight_kernel, count=len(groups), split=split),
        "first_weight",
        [
            ((slabs * rows, split), BF16),
            ((1, split), F32),
            ((8, width), F32),
            ((count, width), BF16),
            ((width, count), BF16),
        ],
        10,
        cost(2 * count * width, 4 * slabs * rows * columns),
        [pltpu.VMEM((slabs, rows, LANES), BF16)],
        places=1,
    )(place, xhat, *groups)


def mix_kernel(place_ref, mine_ref, other_ref, seq_ref, hid_hbm, xhat_ref, rstd_ref, row_ref, hid_ref, sem):
    half, block, width = other_ref.shape
    length = 2 * block
    y = place_ref[3]
    copy = pltpu.make_async_copy(hid_hbm, hid_ref, sem)
    copy.start()

    def spectra(r, part):
        at = part * block
        tokens = row_ref[...]
        cos_part = dot(seq_ref[at : at + block, :], tokens).astype(BF16)
        return cos_part, dot(seq_ref[length + at : length + at + block, :], tokens).astype(BF16)

    for r in range(half):
        row_ref[tile_rows(y, block), :] = mine_ref[half * y + r]
        row_ref[tile_rows(1 - y, block), :] = other_ref[r]
        for part in range(2):
            cos_part, sin_part = spectra(r, part)
            if r == 0 and part == 0:
                copy.wait()
            mixed = dot(cos_part, hid_ref[:width, :]) + dot(sin_part, hid_ref[width:, :])
            resid = row_ref[part * block : (part + 1) * block, :].astype(F32) + mixed
            center = resid - jnp.mean(resid, axis=-1, keepdims=True)
            rstd = lax.rsqrt(jnp.mean(center * center, axis=-1, keepdims=True) + EPS)
            at = (2 * r + part) * block
            xhat_ref[at : at + block, :] = center * rstd
            rstd_ref[at : at + block, :] = rstd


def mix(place, tokens, other, seq_table, hid_table):
    half, block, width = other.shape
    length = 2 * block
    count = half * length
    return vmem_call(
        mix_kernel,
        "mix_norm",
        [((count, width), F32), ((count, 1), F32)],
        14,
        cost(4 * count * width * (length + width), 10 * count * width),
        [
            pltpu.VMEM((length, width), BF16),
            pltpu.VMEM((2 * width, width), BF16),
            pltpu.SemaphoreType.DMA(()),
        ],
        places=1,
        anywhere=1,
    )(place, tokens, other, seq_table, pltpu.with_memory_space_constraint(hid_table, pltpu.HBM))


def gelu_both(values):
    size = jnp.abs(values)
    t = 1.0 / (1.0 + (ERF_T / math.sqrt(2.0)) * size)
    bell = jnp.exp(-0.5 * (values * values))
    poly = 0.5 * ERF_P[4]
    for term in ERF_P[3::-1]:
        poly = 0.5 * term + t * poly
    tail = t * poly * bell
    phi = jnp.where(values > 0, 1.0 - tail, tail)
    return values * phi, phi + values * (bell * (1.0 / math.sqrt(2.0 * math.pi)))


def ffn_low_kernel(xhat_ref, vec_ref, low_ref, low_t_ref):
    low = (xhat_ref[...] * vec_ref[1:2, :] + vec_ref[2:3, :]).astype(BF16)
    low_ref[...] = low
    low_t_ref[...] = low.T


def ffn_low(xhat, vectors):
    count, width = xhat.shape
    return vmem_call(
        ffn_low_kernel,
        "normed_low",
        [((count, width), BF16), ((width, count), BF16)],
        8,
        cost(2 * count * width, 8 * count * width),
    )(xhat, vectors)


def ffn_in_tiles(low_ref, w_ref, bias_ref, act_ref, slope_ref, at, tile, columns):
    tiles = low_ref.shape[0] // tile

    def step(j, carry):
        rows = tile_rows(lax.rem(j, tiles), tile)
        part = j // tiles * columns
        cut = pl.ds(pl.multiple_of(part, LANES), columns)
        full = pl.ds(pl.multiple_of(at + part, LANES), columns)
        act, slope = gelu_both(dot(low_ref[rows, :], w_ref[:, full]) + bias_ref[:, full])
        act_ref[rows, cut] = act.astype(BF16)
        slope_ref[rows, cut] = slope.astype(BF16)
        return carry

    lax.fori_loop(0, tiles * (act_ref.shape[1] // columns), step, 0)


def ffn_in_kernel(low_ref, w_ref, bias_ref, act_ref, slope_ref, *, at, tile, columns):
    ffn_in_tiles(low_ref, w_ref, bias_ref, act_ref, slope_ref, at, tile, columns)


def ffn_in(low, w_in, bias, part, parts, columns=768, tile=512):
    count, width = low.shape
    hidden = w_in.shape[1] // parts
    return vmem_call(
        functools.partial(ffn_in_kernel, at=part * hidden, tile=tile, columns=columns),
        "ffn_in_gelu",
        [((count, hidden), BF16)] * 2,
        14,
        cost(2 * count * width * hidden, 4 * count * hidden, 2 * count * hidden),
    )(low, w_in, bias)


def hidden_block(refs, rows, block):
    width = refs[0].shape[1] // 2
    cut = pl.ds(pl.multiple_of(lax.rem(block, 2) * width, width), width)
    return jnp.where(block >= 2, refs[1][rows, cut], refs[0][rows, cut])


def place_pairs(place_ref, groups, w_ref, first):
    place = tuple(place_ref[i] for i in range(4))
    rows = groups[0].shape[1]

    def put(ref, i, at):
        w_ref[tile_rows(at, rows), :] = ref[i]

    put_slabs(place, groups, lambda part, index, core: pair_slab(part + first, index, core), put)


def ffn_in_last_kernel(place_ref, low_ref, w_in_ref, bias_ref, act_0_ref, *refs, count, at, tile, columns, step):
    groups, (act_1_ref, slope_ref, w_ref, branch_ref) = refs[:count], refs[count:]
    place_pairs(place_ref, groups, w_ref, 0)
    ffn_in_tiles(low_ref, w_in_ref, bias_ref, act_1_ref, slope_ref, at, tile, columns)
    size = w_ref.shape[0] // 4

    def multiply(i, carry):
        rows = tile_rows(i, step)
        total = None
        for distance in range(3):
            block = lax.rem(place_ref[0] + 4 - distance, 4)
            part = hidden_block((act_0_ref, act_1_ref), rows, block)
            part = dot(part, w_ref[tile_rows(block, size), :])
            total = part if total is None else total + part
        branch_ref[rows, :] = total
        return carry

    lax.fori_loop(0, branch_ref.shape[0] // step, multiply, 0)


def ffn_in_last(place, low, w_in, bias, act_0, groups, columns=768, tile=512, step=512):
    count, width = low.shape
    hidden = act_0.shape[1]
    return vmem_call(
        functools.partial(
            ffn_in_last_kernel, count=len(groups), at=hidden, tile=tile, columns=columns, step=step
        ),
        "ffn_in_out",
        [((count, hidden), BF16)] * 2 + [((2 * hidden, width), BF16), ((count, width), F32)],
        14,
        cost(5 * count * width * hidden, 8 * count * hidden, 2 * count * hidden),
        places=1,
    )(place, low, w_in, bias, act_0, *groups)


def ffn_out_kernel(place_ref, *refs, count):
    if count:
        act_0_ref, act_1_ref, _, *refs = refs
    branch_ref, xhat_ref, mine_ref, other_ref, vec_ref, *refs = refs
    groups, refs = refs[:count], refs[count:]
    if count:
        w_ref, *refs = refs
    send_ref, keep_ref, resid_ref, low_ref, sums_ref, part_ref = refs
    half, block, _ = other_ref.shape
    y = place_ref[3]
    if count:
        place_pairs(place_ref, groups, w_ref, 6)
    sums_ref[...] = jnp.zeros_like(sums_ref)
    gain_mix = vec_ref[1:2, :]
    shift_mix = vec_ref[2:3, :] + vec_ref[0:1, :]
    gain, shift = vec_ref[3:4, :], vec_ref[4:5, :]

    def rows_of(step):
        away, r = step < half, step % half
        return tile_rows(2 * r + (1 - y if away else y), block)

    def multiply(step):
        rows = rows_of(step)
        if not count:
            return branch_ref[rows, :]
        last = lax.rem(place_ref[0] + 1, 4)
        part = hidden_block((act_0_ref, act_1_ref), rows, last)
        return branch_ref[rows, :] + dot(part, w_ref[tile_rows(last, w_ref.shape[0] // 4), :])

    def finish(step, branch):
        away, r = step < half, step % half
        rows = rows_of(step)
        value = xhat_ref[rows, :] * gain_mix + (branch + shift_mix)
        center = value - jnp.mean(value, axis=-1, keepdims=True)
        rstd = lax.rsqrt(jnp.mean(center * center, axis=-1, keepdims=True) + EPS)
        xhat = center * rstd
        result = (xhat * gain + shift).astype(BF16)
        if away:
            send_ref[r] = result
            cot = other_ref[r].astype(F32)
        else:
            keep_ref[r] = result
            cot = mine_ref[half * y + r].astype(F32)
        d_xhat = cot * gain
        d_resid = rstd * (
            d_xhat
            - jnp.mean(d_xhat, axis=-1, keepdims=True)
            - xhat * jnp.mean(d_xhat * xhat, axis=-1, keepdims=True)
        )
        d_low = d_resid.astype(BF16)
        resid_ref[rows, :] = d_resid
        low_ref[rows, :] = d_low
        sums_ref[0:1, :] += row_sum(d_low.astype(F32))
        sums_ref[1:2, :] += row_sum(cot * xhat)
        sums_ref[2:3, :] += row_sum(cot)

    part_ref[0] = multiply(0)
    for step in range(2 * half):
        if step + 1 < 2 * half:
            part_ref[(step + 1) % 2] = multiply(step + 1)
        finish(step, part_ref[step % 2])


def ffn_out(place, branch, xhat, cotangent, cot_other, vectors, acts=(), w_out=None, groups=()):
    count, width = xhat.shape
    half, block, _ = cot_other.shape
    hidden = 2 * acts[0].shape[1] if groups else 0
    before = [*acts, w_out] if groups else []
    out_shape = [((hidden, width), BF16)] if groups else []
    out_shape += [
        ((half, block, width), BF16),
        ((half, block, width), BF16),
        ((count, width), F32),
        ((count, width), BF16),
        ((8, width), F32),
    ]
    return vmem_call(
        functools.partial(ffn_out_kernel, count=len(groups)),
        "ffn_out_norm",
        out_shape,
        10,
        cost(count * hidden * width // 2, 30 * count * width),
        [pltpu.VMEM((2, block, width), F32)],
        places=1,
        aliases={3: 0} if groups else None,
    )(place, *before, branch, xhat, cotangent, cot_other, vectors, *groups)


def slot(place_ref, xx, yy, core):
    same_x = jnp.where(place_ref[1] == xx, 1, 0)
    same_y = jnp.where(place_ref[3] == yy, 1, 0)
    return jnp.where(core == 0, same_y, same_x), jnp.where(core == 0, same_x, same_y)


def grad_out_kernel(place_ref, act_0_ref, act_1_ref, low_ref, _, send_ref, keep_ref, *, first):
    c = place_ref[2]
    rows = send_ref.shape[2]
    columns = 8 * rows

    def group(xx, yy):
        return jnp.where(place_ref[3] == yy, 0, 1) + jnp.where(place_ref[1] == xx, 0, 2)

    def step(j, carry):
        t, xx = j // 2, lax.rem(j, 2)
        block = lax.rem(place_ref[0] + 7 - first - t, 4)
        cut = pl.ds(pl.multiple_of(lax.rem(block, 2) * columns + xx * (columns // 2), LANES), columns // 2)
        act = jnp.where(block >= 2, act_1_ref[:, cut], act_0_ref[:, cut])
        total = dot_tn(act, low_ref[...])
        for yy in range(2):
            one = total[yy * rows : (yy + 1) * rows]
            two = total[(2 + yy) * rows : (3 + yy) * rows]
            send_ref[t, group(xx, yy)] = jnp.where(c == 0, two, one).astype(BF16)
            keep_ref[t, group(xx, yy)] = jnp.where(c == 0, one, two)
        return carry

    lax.fori_loop(0, 2 * send_ref.shape[0], step, 0)


def grad_out(place, acts, d_low, nearby, rows, first, steps):
    count, width = d_low.shape
    shape = (steps, 4, rows, width)
    return vmem_call(
        functools.partial(grad_out_kernel, first=first),
        "grad_w_out",
        [(shape, BF16), (shape, F32)],
        6,
        cost(16 * steps * count * rows * width, 16 * steps * count * rows),
        places=1,
    )(place, *acts, d_low, nearby)


def ffn_back_kernel(place_ref, low_ref, resid_ref, slope_0_ref, slope_1_ref, w_out_ref, w_in_ref, xhat_ref, rstd_ref, vec_ref, low_t_ref, two_ref, *refs, tile, columns):
    if len(refs) == 7:
        mix_ref, one_ref, send_ref, keep_ref, pre_ref, bias_ref, sums_ref = refs
    else:
        mix_ref, one_ref, pre_ref, bias_ref, sums_ref = refs
    hidden = pre_ref.shape[1]
    share = slope_0_ref.shape[1]
    bias_ref[...] = jnp.zeros_like(bias_ref)
    sums_ref[...] = jnp.zeros_like(sums_ref)

    def step(i, carry):
        rows = tile_rows(i, tile)
        d_low = low_ref[rows, :]
        d_normed = resid_ref[rows, :]
        for part in range(0, hidden, columns):
            cut = slice(part, part + columns)
            slope_ref = (slope_0_ref, slope_1_ref)[part // share]
            slope = slope_ref[rows, part % share : part % share + columns].astype(F32)
            d_pre = (dot_nt(d_low, w_out_ref[cut, :]) * slope).astype(BF16)
            pre_ref[rows, cut] = d_pre
            bias_ref[0:1, cut] += row_sum(d_pre.astype(F32))
            d_normed += dot_nt(d_pre, w_in_ref[:, cut])
        xhat = xhat_ref[rows, :]
        sums_ref[0:1, :] += row_sum(d_normed * xhat)
        sums_ref[1:2, :] += row_sum(d_normed)
        d_xhat = d_normed * vec_ref[1:2, :]
        d_one = rstd_ref[rows, :] * (
            d_xhat
            - jnp.mean(d_xhat, axis=-1, keepdims=True)
            - xhat * jnp.mean(d_xhat * xhat, axis=-1, keepdims=True)
        )
        one_ref[rows, :] = d_one
        mix_ref[rows, :] = d_one.astype(BF16)
        return carry

    lax.fori_loop(0, low_ref.shape[0] // tile, step, 0)
    if len(refs) == 7:
        grad_in_part(place_ref, low_t_ref, pre_ref, bias_ref, two_ref, sums_ref, send_ref, keep_ref)


def grad_in_part(place_ref, low_ref, pre_ref, bias_ref, two_ref, one_ref, send_ref, keep_ref):
    c = place_ref[2]
    split = pre_ref.shape[1]
    owners, width = 32, low_ref.shape[0]
    size = width // owners

    def gathered(values, first, part):
        total = values.shape[1]
        high = values.astype(BF16)
        rest = values - high.astype(F32)
        middle = rest.astype(BF16)
        lowest = (rest - middle.astype(F32)).astype(BF16)
        matrix = spread_matrix(part, first, total).astype(BF16)
        mask = owner_mask(total // part, total)
        return sum(dot_nt(jnp.where(mask, piece, 0.0).astype(BF16), matrix) for piece in (high, middle, lowest))

    line_0 = gathered(bias_ref[0:1, :], 0, 4 * size)
    line_1 = jnp.zeros((owners, LANES), F32)
    for i, (ref, row) in enumerate(
        ((two_ref, 0), (one_ref, 0), (one_ref, 1), (two_ref, 1), (two_ref, 2))
    ):
        line_1 += gathered(ref[row : row + 1, :], i * size, size)
    send_ref[:, :, :, :, split:] = jnp.zeros(send_ref.shape[:4] + (LANES,), BF16)
    keep_ref[:, :, :, :, split:] = jnp.zeros(keep_ref.shape[:4] + (LANES,), F32)
    rows = send_ref.shape[3]
    columns = split // 2
    for z in range(4):
        for cut in (slice(0, columns), slice(columns, split)):
            total = dot(low_ref[8 * z * rows : 8 * (z + 1) * rows, :], pre_ref[:, cut])
            for xx in range(2):
                for yy in range(2):
                    at = (4 * xx + yy) * rows
                    first, second = total[at : at + rows], total[at + 2 * rows : at + 3 * rows]
                    away, stay = slot(place_ref, xx, yy, 1 - c), slot(place_ref, xx, yy, c)
                    send_ref[away[0], z, away[1], :, cut] = jnp.where(c == 0, second, first).astype(BF16)
                    keep_ref[stay[0], z, stay[1], :, cut] = jnp.where(c == 0, first, second)
        for xx in range(2):
            for yy in range(2):
                at = 8 * z + 4 * xx + yy
                away, stay = slot(place_ref, xx, yy, 1 - c), slot(place_ref, xx, yy, c)
                for row, line in enumerate((line_0, line_1)):
                    first, second = line[at : at + 1], line[at + 2 : at + 3]
                    side = jnp.where(c == 0, second, first)
                    send_ref[away[0], z, away[1], row : row + 1, split:] = side.astype(BF16)
                    side = jnp.where(c == 0, first, second)
                    keep_ref[stay[0], z, stay[1], row : row + 1, split:] = side


def ffn_back(place, d_low, d_resid, slopes, w_out, w_in, norm, low_t, sums_two, chained, tile=512, columns=768):
    count, width = d_low.shape
    hidden = 2 * slopes[0].shape[1]
    out_shape = [((count, width), BF16), ((count, width), F32)]
    backs = [((count, hidden), BF16), ((8, hidden), F32), ((8, width), F32)]
    scratch_shapes = []
    if chained:
        shape = (2, 4, 2, width // 32, hidden + LANES)
        out_shape += [(shape, BF16), (shape, F32)]
        scratch_shapes = [pltpu.VMEM(*each) for each in backs]
    else:
        out_shape += backs
    return vmem_call(
        functools.partial(ffn_back_kernel, tile=tile, columns=columns),
        "ffn_back",
        out_shape,
        12 if chained else 10,
        cost(6 * count * hidden * width, 6 * count * hidden + 4 * hidden * width),
        scratch_shapes,
        places=1,
    )(place, d_low, d_resid, *slopes, w_out, w_in, *norm, low_t, sums_two)


def mix_back_kernel(place_ref, low_ref, one_ref, hid_ref, seq_ref, send_ref, keep_ref, spec_ref):
    width = low_ref.shape[1]
    length = seq_ref.shape[0]
    block = length // 2
    y = place_ref[3]

    def step(r, carry):
        for part in range(2):
            cut = slice(part * width, (part + 1) * width)
            spec = dot(low_ref[tile_rows(r, length), :], hid_ref[:, cut])
            spec_ref[part * length : (part + 1) * length, :] = spec.astype(BF16)
        for spot, away in ((1 - y, True), (y, False)):
            total = dot(seq_ref[tile_rows(spot, block), :], spec_ref[...])
            total += one_ref[tile_rows(2 * r + spot, block), :]
            if away:
                send_ref[r] = total.astype(BF16)
            else:
                keep_ref[r] = total
        return carry

    lax.fori_loop(0, low_ref.shape[0] // length, step, 0)


def mix_back(place, d_low, d_one, hid_table, seq_table):
    count, width = d_low.shape
    length = seq_table.shape[0]
    half, block = count // length, length // 2
    return vmem_call(
        mix_back_kernel,
        "mix_back",
        [((half, block, width), BF16), ((half, block, width), F32)],
        14,
        cost(4 * count * width * (length + width), 10 * count * width),
        [pltpu.VMEM((2 * length, width), BF16)],
        places=1,
    )(place, d_low, d_one, hid_table, seq_table)


def join_kernel(place_ref, keep_ref, *refs):
    *others, out_ref, wide_ref, sem = refs
    y = place_ref[3]
    half = keep_ref.shape[0]
    copies = [pltpu.make_async_copy(keep_ref, out_ref.at[pl.ds(half * y, half)], sem.at[0])]
    copies[0].start()
    at = half * (1 - y)
    for i, ref in enumerate(others):
        rows = ref.shape[0]
        if ref.dtype == keep_ref.dtype:
            source = ref
        else:
            source = wide_ref.at[pl.ds(i * rows, rows)]
            wide_ref[i * rows : (i + 1) * rows] = ref[...].astype(wide_ref.dtype)
        copies.append(
            pltpu.make_async_copy(source, out_ref.at[pl.ds(at + i * rows, rows)], sem.at[i + 1])
        )
        copies[-1].start()
    for copy in copies:
        copy.wait()


def join(place, keep, *others):
    half, block, width = keep.shape
    wide = keep.shape if others[0].dtype != keep.dtype else (1, 8, LANES)
    return vmem_call(
        join_kernel,
        "join_rows",
        [((2 * half, block, width), keep.dtype)],
        4,
        cost(0, 16 * half * block * width),
        [pltpu.VMEM(wide, keep.dtype), pltpu.SemaphoreType.DMA((1 + len(others),))],
        places=1,
        outside=True,
    )(place, keep, *others)[0]


def finish_kernel(own_ref, *refs, spots):
    parts, (w_ref, *smalls) = refs[:3], refs[3:]
    split = w_ref.shape[1]
    total = own_ref[...]
    for ref in parts:
        total += ref[...].astype(F32)
    w_ref[...] = total[:, :split]
    for ref, (line, at) in zip(smalls, spots):
        ref[...] = total[line : line + 1, split + at : split + at + ref.shape[1]]


def finish(own, parts, split, sizes, spots):
    rows, _ = own.shape
    return vmem_call(
        functools.partial(finish_kernel, spots=spots),
        "finish_w_in",
        [((rows, split), F32)] + [((1, size), F32) for size in sizes],
        4,
        cost(3 * rows * split, 14 * rows * split),
    )(own, *parts)


def add_up(keep, other):
    return keep + other.astype(F32)


def per_device(grid, tokens, weight_in, bias_in, weight_out, bias_out, gain_mix, shift_mix, gain_ffn, shift_ffn, cotangent):
    rows, block, width = tokens.shape
    part_in, hidden = weight_in.shape
    part_out = weight_out.shape[0]
    half = rows // 2
    length = 2 * block
    devices = grid.dp * grid.seq
    z, x, c, y = grid.place()
    place = jnp.stack([z, x, c, y]).astype(jnp.int32)
    zero = jnp.uint32(0)
    across = ((1 - y) * half).astype(jnp.uint32)
    ahead = [((z + step) % 4).astype(jnp.uint32) for step in range(4)]
    place, across, ahead, weight_in = together(place, across, ahead, weight_in)
    chained = grid.chained and part_in % 8 == 0

    def other_rows(value):
        return lax.dynamic_slice(value, (across, zero, zero), (half,) + value.shape[1:])

    def join_rows(keep, other):
        other = other.astype(keep.dtype)
        return jnp.where(
            y == 0, jnp.concatenate([keep, other], 0), jnp.concatenate([other, keep], 0)
        )

    def core(value):
        return send(value, grid.cores)

    smalls = (bias_in, bias_out, gain_mix, shift_mix, gain_ffn, shift_ffn)
    sizes = [v.shape[0] for v in smalls]
    spots = [(0, 0)] + [(1, i * sizes[1]) for i in range(5)]
    lines = [0, 0]
    for value, (line, at) in zip(smalls, spots):
        lines[line] += jnp.pad(value, (at, LANES - at - value.shape[0]))
    strip = jnp.pad(jnp.stack(lines), ((0, part_in - 2), (0, 0)))
    tok_other = send(other_rows(tokens), grid.blocks)

    cos_seq, sin_seq = dft_tables(length)
    cos_hid, sin_hid = dft_tables(width)
    mix_tables = (
        table(np.concatenate([cos_seq, sin_seq], 0)),
        table(np.concatenate([cos_hid, -sin_hid], 0)),
    )
    if chained:
        packed = jnp.concatenate([weight_in, strip], axis=1)
        packed, shard_out = together(packed, weight_out)
        *pieces, near_out, tok_other = together(
            *(send(packed, grid.shifts[step]) for step in range(1, 4)),
            send(shard_out, grid.across),
            tok_other,
        )
        pair = jnp.stack([shard_out, near_out])
        column = jnp.stack([packed] + pieces)
        column, pair, tok_other = together(column, pair, tok_other)
        near, ring_pair, far_pair, (xhat, rstd) = together(
            send(column, grid.across_0),
            send(pair, grid.ring),
            send(pair, grid.blocks),
            mix(place, tokens, tok_other, *mix_tables),
        )
        pairs = [pair, far_pair]
        both = jnp.concatenate([column, near], axis=0)
        both, ring_pair, far_pair = together(both, ring_pair, far_pair)
        pairs.append(ring_pair)
        groups = [column, near, send(both, grid.across_1)]
        twins = [core(column), core(near)]
        groups[2], twins, ring_far, ring_pair_2 = together(
            groups[2], twins, send(far_pair, grid.ring), send(ring_pair, grid.ring)
        )
        ring_far_2, ring_pair_3 = send(ring_far, grid.ring), send(ring_pair_2, grid.ring)
        cot_other = send(after(other_rows(cotangent), groups[2]), grid.blocks)
        w_in, bias, vectors, low, low_t = first_weight(
            place, xhat, groups + twins + [core(groups[2])], hidden
        )
    else:
        cot_other = send(other_rows(cotangent), grid.blocks)
        xhat, rstd = mix(place, tokens, tok_other, *mix_tables)
        w_in = lax.all_gather(weight_in, AXES, axis=0, tiled=True)
        w_out = lax.all_gather(weight_out, AXES, axis=0, tiled=True)
        extra = lax.all_gather(strip, AXES, axis=0)[:, :2]
        bias, *vectors = [
            extra[:, line, at : at + size].reshape(1, -1).astype(F32)
            for size, (line, at) in zip(sizes, spots)
        ]
        vectors = jnp.concatenate(vectors + [jnp.zeros((3, width), F32)], axis=0)
        low, low_t = ffn_low(xhat, vectors)
    act_0, slope_0 = ffn_in(low, w_in, bias, 0, 2)
    if chained:
        act_0, slope_0, low, ring_far_2, ring_pair_3 = together(
            act_0, slope_0, low, ring_far_2, ring_pair_3
        )
        ring_far_3 = send(ring_far_2, grid.ring)
    if chained:
        pairs = [pair, far_pair, ring_pair, ring_far, ring_pair_2, ring_far_2]
        pairs += [core(p) for p in pairs]
        act_1, slope_1, w_out, branch = ffn_in_last(place, low, w_in, bias, act_0, pairs)
        ring_far_3, cot_other, branch = together(ring_far_3, cot_other, branch)
    else:
        act_1, slope_1 = ffn_in(low, w_in, bias, 1, 2)
    acts, slopes = [act_0, act_1], [slope_0, slope_1]
    if chained:
        last = [ring_pair_3, ring_far_3]
        w_out, out_send, out_keep, d_resid, d_low, sums_two = ffn_out(
            place, branch, xhat, cotangent, cot_other, vectors, acts, w_out, last + [core(p) for p in last]
        )
    else:
        branch = dot(act_0, w_out[: hidden // 2]) + dot(act_1, w_out[hidden // 2 :])
        out_send, out_keep, d_resid, d_low, sums_two = ffn_out(
            place, branch, xhat, cotangent, cot_other, vectors
        )

    norm = (xhat, rstd, vectors)
    back_tables = (
        table(np.concatenate([cos_hid, -sin_hid], 1)),
        table(np.concatenate([cos_seq, sin_seq], 1)),
    )

    def pack_small(bias_sum, norm_sum):
        grads = (bias_sum, sums_two[0], norm_sum[0], norm_sum[1], sums_two[1], sums_two[2])
        lines = [0, 0]
        for value, (line, at) in zip(grads, spots):
            value = value.reshape(devices, -1)
            lines[line] += jnp.pad(value, ((0, 0), (at, LANES - at - value.shape[1])))
        return jnp.pad(jnp.stack(lines, axis=1), ((0, 0), (0, part_in - 2), (0, 0)))

    def low_send(value, perm):
        return send(value.astype(BF16), perm)

    if chained:
        (away_a, keep_a), start = together(grad_out(place, acts, d_low, w_out, part_out, 0, 1), d_low)
        twin_a, (away_b, keep_b) = together(core(away_a), grad_out(place, acts, start, w_out, part_out, 1, 3))
        quad = add_up(keep_a[0], twin_a[0])
        start, away_b, quad, out_send = together(start, away_b, quad, out_send)
        twin_b, ring, out_other, (d_mix, d_one, away, keep) = together(
            core(away_b),
            low_send(quad, grid.ring),
            send(out_send, grid.blocks),
            ffn_back(place, start, d_resid, slopes, w_out, w_in, norm, low_t, sums_two, True),
        )
        quad = add_up(add_up(keep_b[0], twin_b[0]), ring)
        twin, (gt_send, gt_keep), quad = together(
            core(away), mix_back(place, d_mix, d_one, *back_tables), quad
        )
        first, ring, output = together(
            low_send(add_up(keep[0], twin[0]), grid.across_1),
            low_send(quad, grid.ring),
            join(place, out_keep, out_other),
        )
        pair = add_up(add_up(keep[1], twin[1]), first)
        quad = add_up(add_up(keep_b[1], twin_b[1]), ring)
        second, ring, gt_0 = together(
            low_send(pair[:, 0], grid.across_0),
            low_send(quad, grid.ring),
            send(gt_send[:1], grid.blocks),
        )
        column = add_up(pair[:, 1], second)
        quad = add_up(add_up(keep_b[2], twin_b[2]), ring)
        gt_1 = send(after(gt_send[1:], quad), grid.blocks)
        parts, far = together(
            [low_send(pick(column, ahead[step]), grid.shifts[step]) for step in range(1, 4)],
            low_send(quad[2:], grid.across),
        )
        quad = add_up(quad[:2], far)
        passed, gt_1 = together(quad[1].astype(BF16), gt_1)
        my_w_out = add_up(quad[0], send(passed, grid.blocks))
        grad_tokens = join(place, gt_keep, gt_0, gt_1)
        my_w_in, *my_small = finish(pick(column, ahead[0]), parts, hidden, sizes, spots)
        my_small = [v.reshape(-1) for v in my_small]
    else:
        output = join_rows(out_keep, send(out_send, grid.blocks))
        grad_w_out = jnp.concatenate([dot_tn(act, d_low) for act in acts], axis=0)
        my_w_out = lax.psum_scatter(grad_w_out, AXES, scatter_dimension=0, tiled=True)
        d_mix, d_one, pre, bias_sum, norm_sum = ffn_back(
            place, d_low, d_resid, slopes, w_out, w_in, norm, low_t, sums_two, False
        )
        gt_send, gt_keep = mix_back(place, d_mix, d_one, *back_tables)
        grad_tokens = join_rows(gt_keep, send(gt_send, grid.blocks))
        my_w_in = lax.psum_scatter(dot(low_t, pre), AXES, scatter_dimension=0, tiled=True)
        strips = pack_small(bias_sum[0], norm_sum)
        my_strip = lax.psum_scatter(strips, AXES, scatter_dimension=0, tiled=True)[0, :2]
        my_small = [my_strip[line, at : at + size] for size, (line, at) in zip(sizes, spots)]
    return (
        output,
        grad_tokens,
        my_w_in,
        my_small[0],
        my_w_out,
        my_small[1],
        my_small[2],
        my_small[3],
        my_small[4],
        my_small[5],
    )


def solution(mesh):
    grid = Grid(mesh)
    cut, cut2 = P(AXES), P(AXES, None)
    block = P("dp", "seq", None)
    in_specs = (block, cut2, cut, cut2, cut, cut, cut, cut, cut, block)
    out_specs = (block, block, cut2, cut, cut2, cut, cut, cut, cut, cut)

    def program(*arrays):
        return per_device(grid, *arrays)

    return jax.shard_map(
        program, mesh=mesh, in_specs=in_specs, out_specs=out_specs, check_vma=False
    )
```

profile of v0, /device:TPU:0, one launch (start us, length us, event | category | flops | bytes accessed | tf_op | source)
XLA Modules:
  0.0 195.1 jit_solution(11256989030688094416)
XLA Ops:
  2.2 3.0 %collective-permute-start.4 = (bf16[2,256,768]{2,1,0:T(8,128)(2,1)S(1)}, bf16[2,256,768]{2,1,0:T(8,128)(2,1)S(1)}, u32[]{:S(2)}, u32[]{:S(2)}) collective-permute-start(bf16[2,256,768]{2,1,0:T(8,128)(2,1)S(1)} %constant_dynamic-slice_fusion.1), channel_id=1, source_target_pairs={{0,1},{1,0},{2,3},{3,2},{4,5},{5,4},{6,7},{7,6},{8,9},{9,8},{10,11... | collective-permute-start | bytes 2359304 | tf_op jit(solution)/shard_map/ppermute | solution.py:76
  5.4 3.7 %collective-permute-start.2 = (bf16[24,3200]{1,0:T(8,128)(2,1)S(1)}, bf16[24,3200]{1,0:T(8,128)(2,1)S(1)}, u32[]{:S(2)}, u32[]{:S(2)}) collective-permute-start(bf16[24,3200]{1,0:T(8,128)(2,1)S(1)} %pad_maximum_fusion.3), channel_id=1, source_target_pairs={{0,24},{1,25},{2,26},{3,27},{4,28},{5,29},{6,30},{7,31},{8,0},{9,1... | collective-permute-start | bytes 460808 | tf_op jit(solution)/shard_map/ppermute | solution.py:76
  11.6 3.7 %collective-permute-done.3 = bf16[96,768]{1,0:T(8,128)(2,1)S(1)} collective-permute-done((bf16[96,768]{1,0:T(8,128)(2,1)S(1)}, bf16[96,768]{1,0:T(8,128)(2,1)S(1)}, u32[]{:S(2)}, u32[]{:S(2)}) %collective-permute-start.3) | collective-permute-done | bytes 147488 | tf_op jit(solution)/shard_map/ppermute | solution.py:76
  15.3 6.6 %collective-permute-done.1 = bf16[24,3200]{1,0:T(8,128)(2,1)S(1)} collective-permute-done((bf16[24,3200]{1,0:T(8,128)(2,1)S(1)}, bf16[24,3200]{1,0:T(8,128)(2,1)S(1)}, u32[]{:S(2)}, u32[]{:S(2)}) %collective-permute-start.1) | collective-permute-done | bytes 153632 | tf_op jit(solution)/shard_map/ppermute | solution.py:76
  23.0 1.8 collective-permute-start.5
  27.8 6.7 %mix_norm.1 = (f32[1024,768]{1,0:T(8,128)S(1)}, f32[1024,1]{1,0:T(8,128)S(1)}) custom-call(s32[4]{0:T(128)S(1)} %pad_add_fusion.place_ref, bf16[4,256,768]{2,1,0:T(8,128)(2,1)S(1)} %copy-done.1, bf16[2,256,768]{2,1,0:T(8,128)(2,1)S(1)} %collective-permute-done.4.other_ref, bf16[1024,512]{1,0:T(8,128)(2,1)S(1)} %copy-done.6, bf16[1536,768]{1,0:T(8,128)(2,1)} %constant.108.hid_hbm), custom_call_target="tpu_custom_call" | custom-call | flops 4026531840 | bytes 7864320 | tf_op jit(solution)/shard_map/mix_norm/pallas_call | solution.py:150
  36.4 2.5 %collective-permute-start.9 = (bf16[4,24,3200]{2,1,0:T(8,128)(2,1)S(1)}, bf16[4,24,3200]{2,1,0:T(8,128)(2,1)S(1)}, u32[]{:S(2)}, u32[]{:S(2)}) collective-permute-start(bf16[4,24,3200]{2,1,0:T(8,128)(2,1)S(1)} %pad_maximum_fusion.1.refs_0_), channel_id=1, source_target_pairs={{0,2},{1,3},{2,0},{3,1},{4,6},{5,7},{6,4},{7,5},{8,10},{9,11},{10,... | collective-permute-start | bytes 1843208 | tf_op jit(solution)/shard_map/ppermute | solution.py:76
  38.9 2.0 %collective-permute-start.11 = (bf16[2,96,768]{2,1,0:T(8,128)(2,1)S(1)}, bf16[2,96,768]{2,1,0:T(8,128)(2,1)S(1)}, u32[]{:S(2)}, u32[]{:S(2)}) collective-permute-start(bf16[2,96,768]{2,1,0:T(8,128)(2,1)S(1)} %collective-permute-done.7.refs_1_), channel_id=1, source_target_pairs={{0,8},{1,9},{2,10},{3,11},{4,12},{5,13},{6,14},{7,15},{8,16},{9,17... | collective-permute-start | bytes 884744 | tf_op jit(solution)/shard_map/ppermute | solution.py:76
  42.5 8.3 %collective-permute-done.11.refs_3_ = bf16[2,96,768]{2,1,0:T(8,128)(2,1)S(1)} collective-permute-done((bf16[2,96,768]{2,1,0:T(8,128)(2,1)S(1)}, bf16[2,96,768]{2,1,0:T(8,128)(2,1)S(1)}, u32[]{:S(2)}, u32[]{:S(2)}) %collective-permute-start.11) | collective-permute-done | bytes 294944 | tf_op jit(solution)/shard_map/ppermute | solution.py:76
  50.8 6.1 %collective-permute-done.12.refs_4_ = bf16[2,96,768]{2,1,0:T(8,128)(2,1)S(1)} collective-permute-done((bf16[2,96,768]{2,1,0:T(8,128)(2,1)S(1)}, bf16[2,96,768]{2,1,0:T(8,128)(2,1)S(1)}, u32[]{:S(2)}, u32[]{:S(2)}) %collective-permute-start.12) | collective-permute-done | bytes 294944 | tf_op jit(solution)/shard_map/ppermute | solution.py:76
  60.0 2.4 %first_weight.1 = (bf16[768,3072]{1,0:T(8,128)(2,1)S(1)}, f32[1,3072]{1,0:T(1,128)S(1)}, f32[8,768]{1,0:T(8,128)S(1)}, bf16[1024,768]{1,0:T(8,128)(2,1)S(1)}, bf16[768,1024]{1,0:T(8,128)(2,1)S(1)}) custom-call(s32[4]{0:T(128)S(1)} %pad_add_fusion.place_ref, f32[1024,768]{1,0:T(8,128)S(1)} %get-tuple-element.134.xhat_ref.refs_4_, ...), custom_call_target="tpu_custom_call" | custom-call | flops 1572864 | bytes 9830400 | tf_op jit(solution)/shard_map/first_weight/pallas_call | solution.py:150
  62.5 7.7 %ffn_in_gelu.1 = (bf16[1024,1536]{1,0:T(8,128)(2,1)S(1)}, bf16[1024,1536]{1,0:T(8,128)(2,1)S(1)}) custom-call(bf16[1024,768]{1,0:T(8,128)(2,1)S(1)} %get-tuple-element.152.low_ref, bf16[768,3072]{1,0:T(8,128)(2,1)S(1)} %get-tuple-element.145.w_ref.w_in_ref, f32[1,3072]{1,0:T(1,128)S(1)} %get-tuple-element.146.bias_ref), custom_call_target="tpu_custom_call" | custom-call | flops 2415919104 | bytes 6291456 | tf_op jit(solution)/shard_map/ffn_in_gelu/pallas_call | solution.py:150
  72.2 2.3 %collective-permute-done.15.refs_8_ = bf16[2,96,768]{2,1,0:T(8,128)(2,1)S(1)} collective-permute-done((bf16[2,96,768]{2,1,0:T(8,128)(2,1)S(1)}, bf16[2,96,768]{2,1,0:T(8,128)(2,1)S(1)}, u32[]{:S(2)}, u32[]{:S(2)}) %collective-permute-start.15) | collective-permute-done | bytes 294944 | tf_op jit(solution)/shard_map/ppermute | solution.py:76
  76.8 12.7 %ffn_in_out.1 = (bf16[1024,1536]{1,0:T(8,128)(2,1)S(1)}, bf16[1024,1536]{1,0:T(8,128)(2,1)S(1)}, bf16[3072,768]{1,0:T(8,128)(2,1)S(1)}, f32[1024,768]{1,0:T(8,128)S(1)}) custom-call(s32[4]{0:T(128)S(1)} %pad_add_fusion.place_ref, bf16[1024,768]{1,0:T(8,128)(2,1)S(1)} %get-tuple-element.152.low_ref, bf16[768,3072]{1,0:T(8,128)(2,1)S(1)} %get-tuple-element.145.w_ref.w_in_ref, ...), custom_call_target="tpu_custom_call" | custom-call | flops 6039797760 | bytes 12582912 | tf_op jit(solution)/shard_map/ffn_in_out/pallas_call | solution.py:150
  89.5 1.7 copy-done.9
  91.1 3.5 %collective-permute-done.23.refs_6_ = bf16[2,256,768]{2,1,0:T(8,128)(2,1)S(1)} collective-permute-done((bf16[2,256,768]{2,1,0:T(8,128)(2,1)S(1)}, bf16[2,256,768]{2,1,0:T(8,128)(2,1)S(1)}, u32[]{:S(2)}, u32[]{:S(2)}) %collective-permute-start.23) | collective-permute-done | bytes 786464 | tf_op jit(solution)/shard_map/ppermute | solution.py:76
  96.2 4.8 %ffn_out_norm.1 = (bf16[3072,768]{1,0:T(8,128)(2,1)S(1)}, bf16[2,256,768]{2,1,0:T(8,128)(2,1)S(1)}, bf16[2,256,768]{2,1,0:T(8,128)(2,1)S(1)}, f32[1024,768]{1,0:...) custom-call(s32[4]{0:T(128)S(1)} %pad_add_fusion.place_ref, ...), custom_call_target="tpu_custom_call", output_to_operand_aliasing={{0}: (3, {})} | custom-call | flops 1207959552 | bytes 23592960 | tf_op jit(solution)/shard_map/ffn_out_norm/pallas_call | solution.py:150
  101.0 2.3 %grad_w_out.2 = (bf16[1,4,96,768]{3,2,1,0:T(8,128)(2,1)S(1)}, f32[1,4,96,768]{3,2,1,0:T(8,128)S(1)}) custom-call(s32[4]{0:T(128)S(1)} %pad_add_fusion.place_ref, bf16[1024,1536]{1,0:T(8,128)(2,1)S(1)} %get-tuple-element.151.act_0_ref.refs_0_, bf16[1024,1536]{1,0:T(8,128)(2,1)S(1)} %get-tuple-element.154.refs_1_.act_1_ref, ...), custom_call_target="tpu_custom_call" | custom-call | flops 1207959552 | bytes 1572864 | tf_op jit(solution)/shard_map/grad_w_out/pallas_call | solution.py:150
  103.6 5.9 %grad_w_out.3 = (bf16[3,4,96,768]{3,2,1,0:T(8,128)(2,1)S(1)}, f32[3,4,96,768]{3,2,1,0:T(8,128)S(1)}) custom-call(s32[4]{0:T(128)S(1)} %pad_add_fusion.place_ref, bf16[1024,1536]{1,0:T(8,128)(2,1)S(1)} %get-tuple-element.151.act_0_ref.refs_0_, bf16[1024,1536]{1,0:T(8,128)(2,1)S(1)} %get-tuple-element.154.refs_1_.act_1_ref, ...), custom_call_target="tpu_custom_call" | custom-call | flops 3623878656 | bytes 4718592 | tf_op jit(solution)/shard_map/grad_w_out/pallas_call | solution.py:150
  111.6 19.0 %ffn_back.1 = (bf16[1024,768]{1,0:T(8,128)(2,1)S(1)}, f32[1024,768]{1,0:T(8,128)S(1)}, bf16[2,4,2,24,3200]{4,3,2,1,0:T(8,128)(2,1)S(1)}, f32[2,4,2,24,3200]{4,3,2,1,0:T(8,128)S(1)}) custom-call(s32[4]{0:T(128)S(1)} %pad_add_fusion.place_ref, bf16[1024,768]{1,0:T(8,128)(2,1)S(1)} %get-tuple-element.178.low_ref, f32[1024,768]{1,0:T(8,128)S(1)} %copy-done.3, ...), custom_call_target="tpu_custom_call" | custom-call | flops 14495514624 | bytes 28311552 | tf_op jit(solution)/shard_map/ffn_back/pallas_call | solution.py:150
  133.3 5.2 %mix_back.1 = (bf16[2,256,768]{2,1,0:T(8,128)(2,1)S(1)}, f32[2,256,768]{2,1,0:T(8,128)S(1)}) custom-call(s32[4]{0:T(128)S(1)} %pad_add_fusion.place_ref, bf16[1024,768]{1,0:T(8,128)(2,1)S(1)} %get-tuple-element.191.low_ref, f32[1024,768]{1,0:T(8,128)S(1)} %get-tuple-element.192.one_ref, bf16[768,1536]{1,0:T(8,128)(2,1)S(1)} %copy-done.4, ...), custom_call_target="tpu_custom_call" | custom-call | flops 4026531840 | bytes 7864320 | tf_op jit(solution)/shard_map/mix_back/pallas_call | solution.py:150
  139.7 1.7 join_rows.2
  141.4 14.6 %collective-permute-done.32 = bf16[4,96,768]{2,1,0:T(8,128)(2,1)S(1)} collective-permute-done((bf16[4,96,768]{2,1,0:T(8,128)(2,1)S(1)}, bf16[4,96,768]{2,1,0:T(8,128)(2,1)S(1)}, u32[]{:S(2)}, u32[]{:S(2)}) %collective-permute-start.32) | collective-permute-done | bytes 589856 | tf_op jit(solution)/shard_map/ppermute | solution.py:76
  156.8 1.7 collective-permute-start.33
  159.2 11.5 %collective-permute-done.35.refs_0_ = bf16[1,256,768]{2,1,0:T(8,128)(2,1)S(1)} collective-permute-done((bf16[1,256,768]{2,1,0:T(8,128)(2,1)S(1)}, bf16[1,256,768]{2,1,0:T(8,128)(2,1)S(1)}, u32[]{:S(2)}, u32[]{:S(2)}) %collective-permute-start.35) | collective-permute-done | bytes 393248 | tf_op jit(solution)/shard_map/ppermute | solution.py:76
  170.7 1.8 collective-permute-done.34
  172.9 2.8 %collective-permute-start.39 = (bf16[2,96,768]{2,1,0:T(8,128)(2,1)S(1)}, bf16[2,96,768]{2,1,0:T(8,128)(2,1)S(1)}, u32[]{:S(2)}, u32[]{:S(2)}) collective-permute-start(bf16[2,96,768]{2,1,0:T(8,128)(2,1)S(1)} %slice.115), channel_id=1, source_target_pairs={{0,4},{1,5},{2,6},{3,7},{4,0},{5,1},{6,2},{7,3},{8,12},{9,13},{10,... | collective-permute-start | bytes 884744 | tf_op jit(solution)/shard_map/ppermute | solution.py:76
  176.0 1.9 collective-permute-start.36
  178.1 5.6 %collective-permute-done.38.refs_2_ = bf16[24,3200]{1,0:T(8,128)(2,1)S(1)} collective-permute-done((bf16[24,3200]{1,0:T(8,128)(2,1)S(1)}, bf16[24,3200]{1,0:T(8,128)(2,1)S(1)}, u32[]{:S(2)}, u32[]{:S(2)}) %collective-permute-start.38) | collective-permute-done | bytes 153632 | tf_op jit(solution)/shard_map/ppermute | solution.py:76
  183.7 4.7 %collective-permute-done.36.refs_0_ = bf16[24,3200]{1,0:T(8,128)(2,1)S(1)} collective-permute-done((bf16[24,3200]{1,0:T(8,128)(2,1)S(1)}, bf16[24,3200]{1,0:T(8,128)(2,1)S(1)}, u32[]{:S(2)}, u32[]{:S(2)}) %collective-permute-start.36) | collective-permute-done | bytes 153632 | tf_op jit(solution)/shard_map/ppermute | solution.py:76
  189.7 2.2 %join_rows.3 = f32[4,256,768]{2,1,0:T(8,128)} custom-call(s32[4]{0:T(128)S(1)} %pad_add_fusion.place_ref, f32[2,256,768]{2,1,0:T(8,128)S(1)} %get-tuple-element.203.keep_ref, bf16[1,256,768]{2,1,0:T(8,128)(2,1)S(1)} %collective-permute-done.35.refs_0_, bf16[1,256,768]{2,1,0:T(8,128)(2,1)S(1)} %collective-permute-done.40.refs_1_), custom_call_target="tpu_custom_call" | custom-call | bytes 6291456 | tf_op jit(solution)/shard_map/join_rows/pallas_call | solution.py:150
  191.9 2.5 %collective-permute-done.41 = bf16[96,768]{1,0:T(8,128)(2,1)S(1)} collective-permute-done((bf16[96,768]{1,0:T(8,128)(2,1)S(1)}, bf16[96,768]{1,0:T(8,128)(2,1)S(1)}, u32[]{:S(2)}, u32[]{:S(2)}) %collective-permute-start.41) | collective-permute-done | bytes 147488 | tf_op jit(solution)/shard_map/ppermute | solution.py:76
  (131 shorter events, 30.9 us)
Async XLA Ops:
  2.2 20.6 %collective-permute-start.4 = (bf16[2,256,768]{2,1,0:T(8,128)(2,1)S(1)}, bf16[2,256,768]{2,1,0:T(8,128)(2,1)S(1)}, u32[]{:S(2)}, u32[]{:S(2)}) collective-permute-start(bf16[2,256,768]{2,1,0:T(8,128)(2,1)S(1)} %constant_dynamic-slice_fusion.1), channel_id=1, source_target_pairs={{0,1},{1,0},{2,3},{3,2},{4,5},{5,4},{6,7},{7,6},{8,9},{9,8},{10,11... | collective-permute-start | bytes 2359304 | tf_op jit(solution)/shard_map/ppermute | solution.py:76
  5.4 9.8 %collective-permute-start.2 = (bf16[24,3200]{1,0:T(8,128)(2,1)S(1)}, bf16[24,3200]{1,0:T(8,128)(2,1)S(1)}, u32[]{:S(2)}, u32[]{:S(2)}) collective-permute-start(bf16[24,3200]{1,0:T(8,128)(2,1)S(1)} %pad_maximum_fusion.3), channel_id=1, source_target_pairs={{0,24},{1,25},{2,26},{3,27},{4,28},{5,29},{6,30},{7,31},{8,0},{9,1... | collective-permute-start | bytes 460808 | tf_op jit(solution)/shard_map/ppermute | solution.py:76
  9.1 12.7 %collective-permute-start.1 = (bf16[24,3200]{1,0:T(8,128)(2,1)S(1)}, bf16[24,3200]{1,0:T(8,128)(2,1)S(1)}, u32[]{:S(2)}, u32[]{:S(2)}) collective-permute-start(bf16[24,3200]{1,0:T(8,128)(2,1)S(1)} %pad_maximum_fusion.3), channel_id=1, source_target_pairs={{0,16},{1,17},{2,18},{3,19},{4,20},{5,21},{6,22},{7,23},{8,24},{9,... | collective-permute-start | bytes 460808 | tf_op jit(solution)/shard_map/ppermute | solution.py:76
  9.1 12.7 %collective-permute-start = (bf16[24,3200]{1,0:T(8,128)(2,1)S(1)}, bf16[24,3200]{1,0:T(8,128)(2,1)S(1)}, u32[]{:S(2)}, u32[]{:S(2)}) collective-permute-start(bf16[24,3200]{1,0:T(8,128)(2,1)S(1)} %pad_maximum_fusion.3), channel_id=1, source_target_pairs={{0,8},{1,9},{2,10},{3,11},{4,12},{5,13},{6,14},{7,15},{8,16},{9,17... | collective-permute-start | bytes 460808 | tf_op jit(solution)/shard_map/ppermute | solution.py:76
  23.0 11.8 %collective-permute-start.5 = (bf16[4,24,3200]{2,1,0:T(8,128)(2,1)S(1)}, bf16[4,24,3200]{2,1,0:T(8,128)(2,1)S(1)}, u32[]{:S(2)}, u32[]{:S(2)}) collective-permute-start(bf16[4,24,3200]{2,1,0:T(8,128)(2,1)S(1)} %pad_maximum_fusion.1.refs_0_), channel_id=1, source_target_pairs={{0,4},{1,5},{2,3},{3,2},{4,0},{5,1},{6,7},{7,6},{8,12},{9,13},{10,... | collective-permute-start | bytes 1843208 | tf_op jit(solution)/shard_map/ppermute | solution.py:76
  24.7 9.9 %collective-permute-start.7 = (bf16[2,96,768]{2,1,0:T(8,128)(2,1)S(1)}, bf16[2,96,768]{2,1,0:T(8,128)(2,1)S(1)}, u32[]{:S(2)}, u32[]{:S(2)}) collective-permute-start(bf16[2,96,768]{2,1,0:T(8,128)(2,1)S(1)} %pad_maximum_fusion.2.refs_0_), channel_id=1, source_target_pairs={{0,1},{1,0},{2,3},{3,2},{4,5},{5,4},{6,7},{7,6},{8,9},{9,8},{10,11... | collective-permute-start | bytes 884744 | tf_op jit(solution)/shard_map/ppermute | solution.py:76
  26.3 8.5 %collective-permute-start.6 = (bf16[2,96,768]{2,1,0:T(8,128)(2,1)S(1)}, bf16[2,96,768]{2,1,0:T(8,128)(2,1)S(1)}, u32[]{:S(2)}, u32[]{:S(2)}) collective-permute-start(bf16[2,96,768]{2,1,0:T(8,128)(2,1)S(1)} %pad_maximum_fusion.2.refs_0_), channel_id=1, source_target_pairs={{0,8},{1,9},{2,10},{3,11},{4,12},{5,13},{6,14},{7,15},{8,16},{9,17... | collective-permute-start | bytes 884744 | tf_op jit(solution)/shard_map/ppermute | solution.py:76
  34.9 22.1 %collective-permute-start.8 = (bf16[8,24,3200]{2,1,0:T(8,128)(2,1)S(1)}, bf16[8,24,3200]{2,1,0:T(8,128)(2,1)S(1)}, u32[]{:S(2)}, u32[]{:S(2)}) collective-permute-start(bf16[8,24,3200]{2,1,0:T(8,128)(2,1)S(1)} %pad_maximum_fusion), channel_id=1, source_target_pairs={{0,1},{1,0},{2,6},{3,7},{4,5},{5,4},{6,2},{7,3},{8,9},{9,8},{10,14... | collective-permute-start | bytes 3686408 | tf_op jit(solution)/shard_map/ppermute | solution.py:76
  38.9 18.0 %collective-permute-start.10 = (bf16[4,24,3200]{2,1,0:T(8,128)(2,1)S(1)}, bf16[4,24,3200]{2,1,0:T(8,128)(2,1)S(1)}, u32[]{:S(2)}, u32[]{:S(2)}) collective-permute-start(bf16[4,24,3200]{2,1,0:T(8,128)(2,1)S(1)} %collective-permute-done.5.refs_1_), channel_id=1, source_target_pairs={{0,2},{1,3},{2,0},{3,1},{4,6},{5,7},{6,4},{7,5},{8,10},{9,11},{10,... | collective-permute-start | bytes 1843208 | tf_op jit(solution)/shard_map/ppermute | solution.py:76
  38.9 11.9 %collective-permute-start.11 = (bf16[2,96,768]{2,1,0:T(8,128)(2,1)S(1)}, bf16[2,96,768]{2,1,0:T(8,128)(2,1)S(1)}, u32[]{:S(2)}, u32[]{:S(2)}) collective-permute-start(bf16[2,96,768]{2,1,0:T(8,128)(2,1)S(1)} %collective-permute-done.7.refs_1_), channel_id=1, source_target_pairs={{0,8},{1,9},{2,10},{3,11},{4,12},{5,13},{6,14},{7,15},{8,16},{9,17... | collective-permute-start | bytes 884744 | tf_op jit(solution)/shard_map/ppermute | solution.py:76
  41.0 16.0 %collective-permute-start.12 = (bf16[2,96,768]{2,1,0:T(8,128)(2,1)S(1)}, bf16[2,96,768]{2,1,0:T(8,128)(2,1)S(1)}, u32[]{:S(2)}, u32[]{:S(2)}) collective-permute-start(bf16[2,96,768]{2,1,0:T(8,128)(2,1)S(1)} %collective-permute-done.6.refs_2_), channel_id=1, source_target_pairs={{0,8},{1,9},{2,10},{3,11},{4,12},{5,13},{6,14},{7,15},{8,16},{9,17... | collective-permute-start | bytes 884744 | tf_op jit(solution)/shard_map/ppermute | solution.py:76
  57.0 14.8 %collective-permute-start.14 = (bf16[2,96,768]{2,1,0:T(8,128)(2,1)S(1)}, bf16[2,96,768]{2,1,0:T(8,128)(2,1)S(1)}, u32[]{:S(2)}, u32[]{:S(2)}) collective-permute-start(bf16[2,96,768]{2,1,0:T(8,128)(2,1)S(1)} %collective-permute-done.11.refs_3_), channel_id=1, source_target_pairs={{0,8},{1,9},{2,10},{3,11},{4,12},{5,13},{6,14},{7,15},{8,16},{9,17... | collective-permute-start | bytes 884744 | tf_op jit(solution)/shard_map/ppermute | solution.py:76
  57.1 17.5 %collective-permute-start.15 = (bf16[2,96,768]{2,1,0:T(8,128)(2,1)S(1)}, bf16[2,96,768]{2,1,0:T(8,128)(2,1)S(1)}, u32[]{:S(2)}, u32[]{:S(2)}) collective-permute-start(bf16[2,96,768]{2,1,0:T(8,128)(2,1)S(1)} %collective-permute-done.12.refs_4_), channel_id=1, source_target_pairs={{0,8},{1,9},{2,10},{3,11},{4,12},{5,13},{6,14},{7,15},{8,16},{9,17... | collective-permute-start | bytes 884744 | tf_op jit(solution)/shard_map/ppermute | solution.py:76
  58.3 16.2 %collective-permute-start.16 = (bf16[2,96,768]{2,1,0:T(8,128)(2,1)S(1)}, bf16[2,96,768]{2,1,0:T(8,128)(2,1)S(1)}, u32[]{:S(2)}, u32[]{:S(2)}) collective-permute-start(bf16[2,96,768]{2,1,0:T(8,128)(2,1)S(1)} %pad_maximum_fusion.2.refs_0_), channel_id=1, source_target_pairs={{0,2},{1,3},{2,0},{3,1},{4,6},{5,7},{6,4},{7,5},{8,10},{9,11},{10,... | collective-permute-start | bytes 884744 | tf_op jit(solution)/shard_map/ppermute | solution.py:76
  58.3 16.8 %collective-permute-start.17 = (bf16[2,96,768]{2,1,0:T(8,128)(2,1)S(1)}, bf16[2,96,768]{2,1,0:T(8,128)(2,1)S(1)}, u32[]{:S(2)}, u32[]{:S(2)}) collective-permute-start(bf16[2,96,768]{2,1,0:T(8,128)(2,1)S(1)} %collective-permute-done.7.refs_1_), channel_id=1, source_target_pairs={{0,2},{1,3},{2,0},{3,1},{4,6},{5,7},{6,4},{7,5},{8,10},{9,11},{10,... | collective-permute-start | bytes 884744 | tf_op jit(solution)/shard_map/ppermute | solution.py:76
  59.9 16.8 %collective-permute-start.18 = (bf16[2,96,768]{2,1,0:T(8,128)(2,1)S(1)}, bf16[2,96,768]{2,1,0:T(8,128)(2,1)S(1)}, u32[]{:S(2)}, u32[]{:S(2)}) collective-permute-start(bf16[2,96,768]{2,1,0:T(8,128)(2,1)S(1)} %collective-permute-done.6.refs_2_), channel_id=1, source_target_pairs={{0,2},{1,3},{2,0},{3,1},{4,6},{5,7},{6,4},{7,5},{8,10},{9,11},{10,... | collective-permute-start | bytes 884744 | tf_op jit(solution)/shard_map/ppermute | solution.py:76
  75.1 19.5 %collective-permute-start.23 = (bf16[2,256,768]{2,1,0:T(8,128)(2,1)S(1)}, bf16[2,256,768]{2,1,0:T(8,128)(2,1)S(1)}, u32[]{:S(2)}, u32[]{:S(2)}) collective-permute-start(bf16[2,256,768]{2,1,0:T(8,128)(2,1)S(1)} %constant_dynamic-slice_fusion), channel_id=1, source_target_pairs={{0,1},{1,0},{2,3},{3,2},{4,5},{5,4},{6,7},{7,6},{8,9},{9,8},{10,11... | collective-permute-start | bytes 2359304 | tf_op jit(solution)/shard_map/ppermute | solution.py:76
  76.7 17.9 %collective-permute-start.22 = (bf16[2,96,768]{2,1,0:T(8,128)(2,1)S(1)}, bf16[2,96,768]{2,1,0:T(8,128)(2,1)S(1)}, u32[]{:S(2)}, u32[]{:S(2)}) collective-permute-start(bf16[2,96,768]{2,1,0:T(8,128)(2,1)S(1)} %collective-permute-done.14.refs_5_), channel_id=1, source_target_pairs={{0,8},{1,9},{2,10},{3,11},{4,12},{5,13},{6,14},{7,15},{8,16},{9,17... | collective-permute-start | bytes 884744 | tf_op jit(solution)/shard_map/ppermute | solution.py:76
  76.7 17.9 %collective-permute-start.24 = (bf16[2,96,768]{2,1,0:T(8,128)(2,1)S(1)}, bf16[2,96,768]{2,1,0:T(8,128)(2,1)S(1)}, u32[]{:S(2)}, u32[]{:S(2)}) collective-permute-start(bf16[2,96,768]{2,1,0:T(8,128)(2,1)S(1)} %collective-permute-done.15.refs_8_), channel_id=1, source_target_pairs={{0,2},{1,3},{2,0},{3,1},{4,6},{5,7},{6,4},{7,5},{8,10},{9,11},{10,... | collective-permute-start | bytes 884744 | tf_op jit(solution)/shard_map/ppermute | solution.py:76
  109.7 21.0 %collective-permute-start.27 = (bf16[3,4,96,768]{3,2,1,0:T(8,128)(2,1)S(1)}, bf16[3,4,96,768]{3,2,1,0:T(8,128)(2,1)S(1)}, u32[]{:S(2)}, u32[]{:S(2)}) collective-permute-start(bf16[3,4,96,768]{3,2,1,0:T(8,128)(2,1)S(1)} %get-tuple-element.175), channel_id=1, source_target_pairs={{0,2},{1,3},{2,0},{3,1},{4,6},{5,7},{6,4},{7,5},{8,10},{9,11},{10,... | collective-permute-start | bytes 5308424 | tf_op jit(solution)/shard_map/ppermute | solution.py:76
  110.1 20.5 %collective-permute-start.28 = (bf16[4,96,768]{2,1,0:T(8,128)(2,1)S(1)}, bf16[4,96,768]{2,1,0:T(8,128)(2,1)S(1)}, u32[]{:S(2)}, u32[]{:S(2)}) collective-permute-start(bf16[4,96,768]{2,1,0:T(8,128)(2,1)S(1)} %add_bitcast_fusion), channel_id=1, source_target_pairs={{0,8},{1,9},{2,10},{3,11},{4,12},{5,13},{6,14},{7,15},{8,16},{9,17... | collective-permute-start | bytes 1769480 | tf_op jit(solution)/shard_map/ppermute | solution.py:76
  110.1 20.5 %collective-permute-start.29 = (bf16[2,256,768]{2,1,0:T(8,128)(2,1)S(1)}, bf16[2,256,768]{2,1,0:T(8,128)(2,1)S(1)}, u32[]{:S(2)}, u32[]{:S(2)}) collective-permute-start(bf16[2,256,768]{2,1,0:T(8,128)(2,1)S(1)} %get-tuple-element.177), channel_id=1, source_target_pairs={{0,1},{1,0},{2,3},{3,2},{4,5},{5,4},{6,7},{7,6},{8,9},{9,8},{10,11... | collective-permute-start | bytes 2359304 | tf_op jit(solution)/shard_map/ppermute | solution.py:76
  138.8 17.3 %collective-permute-start.31 = (bf16[4,2,24,3200]{3,2,0,1:T(8,128)(2,1)S(1)}, bf16[4,2,24,3200]{3,2,0,1:T(8,128)(2,1)S(1)}, u32[]{:S(2)}, u32[]{:S(2)}) collective-permute-start(bf16[4,2,24,3200]{3,2,0,1:T(8,128)(2,1)S(1)} %fusion.3), channel_id=1, source_target_pairs={{0,1},{1,0},{2,6},{3,7},{4,5},{5,4},{6,2},{7,3},{8,9},{9,8},{10,14... | collective-permute-start | bytes 3686408 | tf_op jit(solution)/shard_map/ppermute | solution.py:76
  139.6 16.4 %collective-permute-start.32 = (bf16[4,96,768]{2,1,0:T(8,128)(2,1)S(1)}, bf16[4,96,768]{2,1,0:T(8,128)(2,1)S(1)}, u32[]{:S(2)}, u32[]{:S(2)}) collective-permute-start(bf16[4,96,768]{2,1,0:T(8,128)(2,1)S(1)} %bitcast_add_fusion.2), channel_id=1, source_target_pairs={{0,8},{1,9},{2,10},{3,11},{4,12},{5,13},{6,14},{7,15},{8,16},{9,17... | collective-permute-start | bytes 1769480 | tf_op jit(solution)/shard_map/ppermute | solution.py:76
  156.7 15.8 %collective-permute-start.34 = (bf16[4,96,768]{2,1,0:T(8,128)(2,1)S(1)}, bf16[4,96,768]{2,1,0:T(8,128)(2,1)S(1)}, u32[]{:S(2)}, u32[]{:S(2)}) collective-permute-start(bf16[4,96,768]{2,1,0:T(8,128)(2,1)S(1)} %fusion.5), channel_id=1, source_target_pairs={{0,8},{1,9},{2,10},{3,11},{4,12},{5,13},{6,14},{7,15},{8,16},{9,17... | collective-permute-start | bytes 1769480 | tf_op jit(solution)/shard_map/ppermute | solution.py:76
  156.8 15.7 %collective-permute-start.33 = (bf16[4,24,3200]{2,1,0:T(8,128)(2,1)S(1)}, bf16[4,24,3200]{2,1,0:T(8,128)(2,1)S(1)}, u32[]{:S(2)}, u32[]{:S(2)}) collective-permute-start(bf16[4,24,3200]{2,1,0:T(8,128)(2,1)S(1)} %fusion.6), channel_id=1, source_target_pairs={{0,4},{1,5},{2,3},{3,2},{4,0},{5,1},{6,7},{7,6},{8,12},{9,13},{10,... | collective-permute-start | bytes 1843208 | tf_op jit(solution)/shard_map/ppermute | solution.py:76
  158.6 12.1 %collective-permute-start.35 = (bf16[1,256,768]{2,1,0:T(8,128)(2,1)S(1)}, bf16[1,256,768]{2,1,0:T(8,128)(2,1)S(1)}, u32[]{:S(2)}, u32[]{:S(2)}) collective-permute-start(bf16[1,256,768]{2,1,0:T(8,128)(2,1)S(1)} %get-tuple-element.232), channel_id=1, source_target_pairs={{0,1},{1,0},{2,3},{3,2},{4,5},{5,4},{6,7},{7,6},{8,9},{9,8},{10,11... | collective-permute-start | bytes 1179656 | tf_op jit(solution)/shard_map/ppermute | solution.py:76
  172.9 15.4 %collective-permute-start.39 = (bf16[2,96,768]{2,1,0:T(8,128)(2,1)S(1)}, bf16[2,96,768]{2,1,0:T(8,128)(2,1)S(1)}, u32[]{:S(2)}, u32[]{:S(2)}) collective-permute-start(bf16[2,96,768]{2,1,0:T(8,128)(2,1)S(1)} %slice.115), channel_id=1, source_target_pairs={{0,4},{1,5},{2,6},{3,7},{4,0},{5,1},{6,2},{7,3},{8,12},{9,13},{10,... | collective-permute-start | bytes 884744 | tf_op jit(solution)/shard_map/ppermute | solution.py:76
  175.8 7.9 %collective-permute-start.38 = (bf16[24,3200]{1,0:T(8,128)(2,1)S(1)}, bf16[24,3200]{1,0:T(8,128)(2,1)S(1)}, u32[]{:S(2)}, u32[]{:S(2)}) collective-permute-start(bf16[24,3200]{1,0:T(8,128)(2,1)S(1)} %get-tuple-element.228), channel_id=1, source_target_pairs={{0,24},{1,25},{2,26},{3,27},{4,28},{5,29},{6,30},{7,31},{8,0},{9,1... | collective-permute-start | bytes 460808 | tf_op jit(solution)/shard_map/ppermute | solution.py:76
  175.9 7.8 %collective-permute-start.37 = (bf16[24,3200]{1,0:T(8,128)(2,1)S(1)}, bf16[24,3200]{1,0:T(8,128)(2,1)S(1)}, u32[]{:S(2)}, u32[]{:S(2)}) collective-permute-start(bf16[24,3200]{1,0:T(8,128)(2,1)S(1)} %get-tuple-element.229), channel_id=1, source_target_pairs={{0,16},{1,17},{2,18},{3,19},{4,20},{5,21},{6,22},{7,23},{8,24},{9,... | collective-permute-start | bytes 460808 | tf_op jit(solution)/shard_map/ppermute | solution.py:76
  176.0 12.4 %collective-permute-start.36 = (bf16[24,3200]{1,0:T(8,128)(2,1)S(1)}, bf16[24,3200]{1,0:T(8,128)(2,1)S(1)}, u32[]{:S(2)}, u32[]{:S(2)}) collective-permute-start(bf16[24,3200]{1,0:T(8,128)(2,1)S(1)} %get-tuple-element.230), channel_id=1, source_target_pairs={{0,8},{1,9},{2,10},{3,11},{4,12},{5,13},{6,14},{7,15},{8,16},{9,17... | collective-permute-start | bytes 460808 | tf_op jit(solution)/shard_map/ppermute | solution.py:76
  177.9 10.8 %collective-permute-start.40 = (bf16[1,256,768]{2,1,0:T(8,128)(2,1)S(1)}, bf16[1,256,768]{2,1,0:T(8,128)(2,1)S(1)}, u32[]{:S(2)}, u32[]{:S(2)}) collective-permute-start(bf16[1,256,768]{2,1,0:T(8,128)(2,1)S(1)} %get-tuple-element.214), channel_id=1, source_target_pairs={{0,1},{1,0},{2,3},{3,2},{4,5},{5,4},{6,7},{7,6},{8,9},{9,8},{10,11... | collective-permute-start | bytes 1179656 | tf_op jit(solution)/shard_map/ppermute | solution.py:76
  (31 other events, 203.4 us)
where the time goes:
time: 196 us; the launch traced here: 195 us
  waiting for transfers between devices  75.4 us (38%)
  Pallas kernels  71.4 us (36%)
  starting transfers between devices  37 us (19%)
  local copies, waits for them, and re-layouts  7.22 us (4%)
  other arithmetic  2.82 us (1%)
    ppermute x42, waiting for transfers between devices, send(): return lax.ppermute(value, AXES, perm)  75.4 us
    pallas_call x12, Pallas kernels, call(): pl.pallas_call(kernel, name=name, in_specs=[pl.BlockSpec(memory_space=plt...  71.4 us
    ppermute x42, starting transfers between devices, send(): return lax.ppermute(value, AXES, perm)  37 us
    unnamed x42, local copies, waits for them, and re-layouts  5.4 us
  transfers between devices with their start and end apart: 42, of which 18 were waited for; matrix products, arithmetic and copies ran while one was open for 0% of the time, Pallas kernels for 33%

commit v1 on v0

--- a/solution.py
+++ b/solution.py
@@ -131,15 +131,15 @@
     return index % 4, flip_x, flip_y
 
 
-def pair_slab(part, index, core):
-    return part // 2, index, part % 2
+def ring_slab(position):
+    return position // 4, position % 2, position % 4 // 2
 
 
 def put_slabs(place, refs, slab_of, put):
+    own = len(refs) // 2
     for part, ref in enumerate(refs):
-        own = len(refs) // 2
+        core = 1 - place[2] if part >= own else place[2]
         for i in range(ref.shape[0]):
-            core = 1 - place[2] if part >= own else place[2]
             where = slab_of(part % own, i, core)
             put(ref, i, device_number(place, *where, part >= own))
 
@@ -295,7 +295,7 @@
 def gelu_both(values):
     size = jnp.abs(values)
     t = 1.0 / (1.0 + (ERF_T / math.sqrt(2.0)) * size)
-    bell = jnp.exp(-0.5 * (values * values))
+    bell = jnp.exp2((values * values) * (-0.5 * math.log2(math.e)))
     poly = 0.5 * ERF_P[4]
     for term in ERF_P[3::-1]:
         poly = 0.5 * term + t * poly
@@ -348,7 +348,7 @@
         functools.partial(ffn_in_kernel, at=part * hidden, tile=tile, columns=columns),
         "ffn_in_gelu",
         [((count, hidden), BF16)] * 2,
-        14,
+        8,
         cost(2 * count * width * hidden, 4 * count * hidden, 2 * count * hidden),
     )(low, w_in, bias)
 
@@ -359,19 +359,22 @@
     return jnp.where(block >= 2, refs[1][rows, cut], refs[0][rows, cut])
 
 
-def place_pairs(place_ref, groups, w_ref, first):
+def place_rows(place_ref, groups, w_ref, first):
     place = tuple(place_ref[i] for i in range(4))
     rows = groups[0].shape[1]
+    starts = [first]
+    for group in groups[: len(groups) // 2]:
+        starts.append(starts[-1] + group.shape[0])
 
     def put(ref, i, at):
         w_ref[tile_rows(at, rows), :] = ref[i]
 
-    put_slabs(place, groups, lambda part, index, core: pair_slab(part + first, index, core), put)
+    put_slabs(place, groups, lambda part, index, core: ring_slab(starts[part] + index), put)
 
 
 def ffn_in_last_kernel(place_ref, low_ref, w_in_ref, bias_ref, act_0_ref, *refs, count, at, tile, columns, step):
     groups, (act_1_ref, slope_ref, w_ref, branch_ref) = refs[:count], refs[count:]
-    place_pairs(place_ref, groups, w_ref, 0)
+    place_rows(place_ref, groups, w_ref, 0)
     ffn_in_tiles(low_ref, w_in_ref, bias_ref, act_1_ref, slope_ref, at, tile, columns)
     size = w_ref.shape[0] // 4
 
@@ -398,7 +401,7 @@
         ),
         "ffn_in_out",
         [((count, hidden), BF16)] * 2 + [((2 * hidden, width), BF16), ((count, width), F32)],
-        14,
+        8,
         cost(5 * count * width * hidden, 8 * count * hidden, 2 * count * hidden),
         places=1,
     )(place, low, w_in, bias, act_0, *groups)
@@ -407,15 +410,15 @@
 def ffn_out_kernel(place_ref, *refs, count):
     if count:
         act_0_ref, act_1_ref, _, *refs = refs
-    branch_ref, xhat_ref, mine_ref, other_ref, vec_ref, *refs = refs
+    branch_ref, xhat_ref, mine_ref, other_0_ref, other_1_ref, vec_ref, *refs = refs
     groups, refs = refs[:count], refs[count:]
     if count:
         w_ref, *refs = refs
     send_ref, keep_ref, resid_ref, low_ref, sums_ref, part_ref = refs
-    half, block, _ = other_ref.shape
+    half, block = 2, other_0_ref.shape[1]
     y = place_ref[3]
     if count:
-        place_pairs(place_ref, groups, w_ref, 6)
+        place_rows(place_ref, groups, w_ref, 14)
     sums_ref[...] = jnp.zeros_like(sums_ref)
     gain_mix = vec_ref[1:2, :]
     shift_mix = vec_ref[2:3, :] + vec_ref[0:1, :]
@@ -443,7 +446,7 @@
         result = (xhat * gain + shift).astype(BF16)
         if away:
             send_ref[r] = result
-            cot = other_ref[r].astype(F32)
+            cot = (other_0_ref, other_1_ref)[r][0].astype(F32)
         else:
             keep_ref[r] = result
             cot = mine_ref[half * y + r].astype(F32)
@@ -467,9 +470,9 @@
         finish(step, part_ref[step % 2])
 
 
-def ffn_out(place, branch, xhat, cotangent, cot_other, vectors, acts=(), w_out=None, groups=()):
+def ffn_out(place, branch, xhat, cotangent, cot_others, vectors, acts=(), w_out=None, groups=()):
     count, width = xhat.shape
-    half, block, _ = cot_other.shape
+    half, block = len(cot_others), cot_others[0].shape[1]
     hidden = 2 * acts[0].shape[1] if groups else 0
     before = [*acts, w_out] if groups else []
     out_shape = [((hidden, width), BF16)] if groups else []
@@ -489,7 +492,7 @@
         [pltpu.VMEM((2, block, width), F32)],
         places=1,
         aliases={3: 0} if groups else None,
-    )(place, *before, branch, xhat, cotangent, cot_other, vectors, *groups)
+    )(place, *before, branch, xhat, cotangent, *cot_others, vectors, *groups)
 
 
 def slot(place_ref, xx, yy, core):
@@ -516,7 +519,7 @@
             one = total[yy * rows : (yy + 1) * rows]
             two = total[(2 + yy) * rows : (3 + yy) * rows]
             send_ref[t, group(xx, yy)] = jnp.where(c == 0, two, one).astype(BF16)
-            keep_ref[t, group(xx, yy)] = jnp.where(c == 0, one, two)
+            keep_ref[t, group(xx, yy)] = jnp.where(c == 0, one, two).astype(BF16)
         return carry
 
     lax.fori_loop(0, 2 * send_ref.shape[0], step, 0)
@@ -528,7 +531,7 @@
     return vmem_call(
         functools.partial(grad_out_kernel, first=first),
         "grad_w_out",
-        [(shape, BF16), (shape, F32)],
+        [(shape, BF16), (shape, BF16)],
         6,
         cost(16 * steps * count * rows * width, 16 * steps * count * rows),
         places=1,
@@ -598,7 +601,7 @@
     ):
         line_1 += gathered(ref[row : row + 1, :], i * size, size)
     send_ref[:, :, :, :, split:] = jnp.zeros(send_ref.shape[:4] + (LANES,), BF16)
-    keep_ref[:, :, :, :, split:] = jnp.zeros(keep_ref.shape[:4] + (LANES,), F32)
+    keep_ref[:, :, :, :, split:] = jnp.zeros(keep_ref.shape[:4] + (LANES,), BF16)
     rows = send_ref.shape[3]
     columns = split // 2
     for z in range(4):
@@ -610,7 +613,7 @@
                     first, second = total[at : at + rows], total[at + 2 * rows : at + 3 * rows]
                     away, stay = slot(place_ref, xx, yy, 1 - c), slot(place_ref, xx, yy, c)
                     send_ref[away[0], z, away[1], :, cut] = jnp.where(c == 0, second, first).astype(BF16)
-                    keep_ref[stay[0], z, stay[1], :, cut] = jnp.where(c == 0, first, second)
+                    keep_ref[stay[0], z, stay[1], :, cut] = jnp.where(c == 0, first, second).astype(BF16)
         for xx in range(2):
             for yy in range(2):
                 at = 8 * z + 4 * xx + yy
@@ -620,7 +623,7 @@
                     side = jnp.where(c == 0, second, first)
                     send_ref[away[0], z, away[1], row : row + 1, split:] = side.astype(BF16)
                     side = jnp.where(c == 0, first, second)
-                    keep_ref[stay[0], z, stay[1], row : row + 1, split:] = side
+                    keep_ref[stay[0], z, stay[1], row : row + 1, split:] = side.astype(BF16)
 
 
 def ffn_back(place, d_low, d_resid, slopes, w_out, w_in, norm, low_t, sums_two, chained, tile=512, columns=768):
@@ -631,7 +634,7 @@
     scratch_shapes = []
     if chained:
         shape = (2, 4, 2, width // 32, hidden + LANES)
-        out_shape += [(shape, BF16), (shape, F32)]
+        out_shape += [(shape, BF16), (shape, BF16)]
         scratch_shapes = [pltpu.VMEM(*each) for each in backs]
     else:
         out_shape += backs
@@ -639,7 +642,7 @@
         functools.partial(ffn_back_kernel, tile=tile, columns=columns),
         "ffn_back",
         out_shape,
-        12 if chained else 10,
+        12,
         cost(6 * count * hidden * width, 6 * count * hidden + 4 * hidden * width),
         scratch_shapes,
         places=1,
@@ -684,41 +687,42 @@
     )(place, d_low, d_one, hid_table, seq_table)
 
 
-def join_kernel(place_ref, keep_ref, *refs):
-    *others, out_ref, wide_ref, sem = refs
+def join_kernel(place_ref, *refs, first, earlier):
+    *ins, out_ref, wide_ref, sem = refs
+    ins = ins[: len(ins) - earlier]
     y = place_ref[3]
-    half = keep_ref.shape[0]
-    copies = [pltpu.make_async_copy(keep_ref, out_ref.at[pl.ds(half * y, half)], sem.at[0])]
-    copies[0].start()
-    at = half * (1 - y)
-    for i, ref in enumerate(others):
+    half = out_ref.shape[0] // 2
+    copies = []
+    for i, ref in enumerate(ins):
         rows = ref.shape[0]
-        if ref.dtype == keep_ref.dtype:
-            source = ref
-        else:
-            source = wide_ref.at[pl.ds(i * rows, rows)]
-            wide_ref[i * rows : (i + 1) * rows] = ref[...].astype(wide_ref.dtype)
-        copies.append(
-            pltpu.make_async_copy(source, out_ref.at[pl.ds(at + i * rows, rows)], sem.at[i + 1])
-        )
+        source = ref
+        if ref.dtype != out_ref.dtype:
+            source = wide_ref.at[pl.ds(0, rows)]
+            wide_ref[:rows] = ref[...].astype(wide_ref.dtype)
+        at = half * y if rows == half and first == 0 and i == 0 else half * (1 - y) + first
+        copies.append(pltpu.make_async_copy(source, out_ref.at[pl.ds(at, rows)], sem.at[i]))
         copies[-1].start()
     for copy in copies:
         copy.wait()
 
 
-def join(place, keep, *others):
+def join(place, keep, other, first=0, joined=None):
     half, block, width = keep.shape
-    wide = keep.shape if others[0].dtype != keep.dtype else (1, 8, LANES)
-    return vmem_call(
-        join_kernel,
+    ins = [other] if joined is not None else [keep, other]
+    wide = other.shape if other.dtype != keep.dtype else (1, 8, LANES)
+    earlier = [] if joined is None else [joined]
+    return vmem_call(
+        functools.partial(join_kernel, first=first, earlier=len(earlier)),
         "join_rows",
         [((2 * half, block, width), keep.dtype)],
         4,
         cost(0, 16 * half * block * width),
-        [pltpu.VMEM(wide, keep.dtype), pltpu.SemaphoreType.DMA((1 + len(others),))],
+        [pltpu.VMEM(wide, keep.dtype), pltpu.SemaphoreType.DMA((2,))],
         places=1,
+        anywhere=len(earlier),
         outside=True,
-    )(place, keep, *others)[0]
+        aliases={2: 0} if earlier else None,
+    )(place, *ins, *earlier)[0]
 
 
 def finish_kernel(own_ref, *refs, spots):
@@ -744,7 +748,7 @@
 
 
 def add_up(keep, other):
-    return keep + other.astype(F32)
+    return keep.astype(F32) + other.astype(F32)
 
 
 def per_device(grid, tokens, weight_in, bias_in, weight_out, bias_out, gain_mix, shift_mix, gain_ffn, shift_ffn, cotangent):
@@ -800,26 +804,21 @@
         pair = jnp.stack([shard_out, near_out])
         column = jnp.stack([packed] + pieces)
         column, pair, tok_other = together(column, pair, tok_other)
-        near, ring_pair, far_pair, (xhat, rstd) = together(
+        near, ring_1, far_pair, twin_column, (xhat, rstd) = together(
             send(column, grid.across_0),
             send(pair, grid.ring),
             send(pair, grid.blocks),
+            core(column),
             mix(place, tokens, tok_other, *mix_tables),
         )
-        pairs = [pair, far_pair]
         both = jnp.concatenate([column, near], axis=0)
-        both, ring_pair, far_pair = together(both, ring_pair, far_pair)
-        pairs.append(ring_pair)
-        groups = [column, near, send(both, grid.across_1)]
-        twins = [core(column), core(near)]
-        groups[2], twins, ring_far, ring_pair_2 = together(
-            groups[2], twins, send(far_pair, grid.ring), send(ring_pair, grid.ring)
-        )
-        ring_far_2, ring_pair_3 = send(ring_far, grid.ring), send(ring_pair_2, grid.ring)
-        cot_other = send(after(other_rows(cotangent), groups[2]), grid.blocks)
-        w_in, bias, vectors, low, low_t = first_weight(
-            place, xhat, groups + twins + [core(groups[2])], hidden
-        )
+        both, pairs = together(both, jnp.concatenate([far_pair, ring_1], axis=0))
+        far, ring_2 = together(send(both, grid.across_1), send(pairs, grid.ring))
+        ring_3 = send(ring_2, grid.ring)
+        groups = [column, near, far, twin_column, core(after(near, far)), core(far)]
+        w_in, bias, vectors, low, low_t = first_weight(place, xhat, groups, hidden)
+        cot_part = after(other_rows(cotangent), vectors)
+        cot_0 = send(cot_part[:1], grid.blocks)
     else:
         cot_other = send(other_rows(cotangent), grid.blocks)
         xhat, rstd = mix(place, tokens, tok_other, *mix_tables)
@@ -834,27 +833,26 @@
         low, low_t = ffn_low(xhat, vectors)
     act_0, slope_0 = ffn_in(low, w_in, bias, 0, 2)
     if chained:
-        act_0, slope_0, low, ring_far_2, ring_pair_3 = together(
-            act_0, slope_0, low, ring_far_2, ring_pair_3
-        )
-        ring_far_3 = send(ring_far_2, grid.ring)
-    if chained:
-        pairs = [pair, far_pair, ring_pair, ring_far, ring_pair_2, ring_far_2]
-        pairs += [core(p) for p in pairs]
+        early = [pair, far_pair, ring_1, ring_2]
+        act_0, slope_0, low, ring_3, cot_0, twins = together(
+            act_0, slope_0, low, ring_3, cot_0, [core(p) for p in early]
+        )
+        ring_4 = send(ring_3[:2], grid.ring)
+        cot_1 = send(after(cot_part[1:], cot_0), grid.blocks)
+        pairs = early + [ring_3] + twins + [core(ring_3)]
         act_1, slope_1, w_out, branch = ffn_in_last(place, low, w_in, bias, act_0, pairs)
-        ring_far_3, cot_other, branch = together(ring_far_3, cot_other, branch)
+        ring_4, cot_1, branch = together(ring_4, cot_1, branch)
     else:
         act_1, slope_1 = ffn_in(low, w_in, bias, 1, 2)
     acts, slopes = [act_0, act_1], [slope_0, slope_1]
     if chained:
-        last = [ring_pair_3, ring_far_3]
         w_out, out_send, out_keep, d_resid, d_low, sums_two = ffn_out(
-            place, branch, xhat, cotangent, cot_other, vectors, acts, w_out, last + [core(p) for p in last]
+            place, branch, xhat, cotangent, (cot_0, cot_1), vectors, acts, w_out, [ring_4, core(ring_4)]
         )
     else:
         branch = dot(act_0, w_out[: hidden // 2]) + dot(act_1, w_out[hidden // 2 :])
         out_send, out_keep, d_resid, d_low, sums_two = ffn_out(
-            place, branch, xhat, cotangent, cot_other, vectors
+            place, branch, xhat, cotangent, (cot_other[:1], cot_other[1:]), vectors
         )
 
     norm = (xhat, rstd, vectors)
@@ -886,13 +884,12 @@
             ffn_back(place, start, d_resid, slopes, w_out, w_in, norm, low_t, sums_two, True),
         )
         quad = add_up(add_up(keep_b[0], twin_b[0]), ring)
-        twin, (gt_send, gt_keep), quad = together(
-            core(away), mix_back(place, d_mix, d_one, *back_tables), quad
-        )
-        first, ring, output = together(
+        twin, quad = together(core(away), quad)
+        first, ring, output, (gt_send, gt_keep) = together(
             low_send(add_up(keep[0], twin[0]), grid.across_1),
             low_send(quad, grid.ring),
             join(place, out_keep, out_other),
+            mix_back(place, d_mix, d_one, *back_tables),
         )
         pair = add_up(add_up(keep[1], twin[1]), first)
         quad = add_up(add_up(keep_b[1], twin_b[1]), ring)
@@ -904,14 +901,16 @@
         column = add_up(pair[:, 1], second)
         quad = add_up(add_up(keep_b[2], twin_b[2]), ring)
         gt_1 = send(after(gt_send[1:], quad), grid.blocks)
-        parts, far = together(
+        grad_tokens = join(place, gt_keep, gt_0)
+        parts, far, gt_1, grad_tokens = together(
             [low_send(pick(column, ahead[step]), grid.shifts[step]) for step in range(1, 4)],
             low_send(quad[2:], grid.across),
+            gt_1,
+            grad_tokens,
         )
         quad = add_up(quad[:2], far)
-        passed, gt_1 = together(quad[1].astype(BF16), gt_1)
-        my_w_out = add_up(quad[0], send(passed, grid.blocks))
-        grad_tokens = join(place, gt_keep, gt_0, gt_1)
+        my_w_out = add_up(quad[0], low_send(quad[1], grid.blocks))
+        grad_tokens = join(place, gt_keep, gt_1, 1, grad_tokens)
         my_w_in, *my_small = finish(pick(column, ahead[0]), parts, hidden, sizes, spots)
         my_small = [v.reshape(-1) for v in my_small]
     else:

time: 196 us -> 193 us (0.985)
  waiting for transfers between devices: 75.4 us -> 71.6 us
  starting transfers between devices: 37 us -> 40.1 us
  local copies, waits for them, and re-layouts: 7.22 us -> 4.69 us
    ppermute x42 -> x39, waiting for transfers between devices: 75.4 us -> 71.6 us  [send(): return lax.ppermute(value, AXES, perm)]
    ppermute x42 -> x39, starting transfers between devices: 37 us -> 40.1 us  [send(): return lax.ppermute(value, AXES, perm)]
    unnamed x42 -> x30, local copies, waits for them, and re-layouts: 5.4 us -> 2.8 us
    pallas_call x12 -> x13, Pallas kernels: 71.4 us -> 71.8 us  [call(): pl.pallas_call(kernel, name=name, in_specs=[pl.BlockSpec(memory_space=plt...]
  transfers between devices with their start and end apart: 42 -> 39, of which waited for: 18 -> 17; matrix products, arithmetic and copies ran while one was open for 0% -> 0% of each run, Pallas kernels for 33% -> 34%
where the time goes in v1:
time: 193 us
  Pallas kernels  71.8 us (37%)
  waiting for transfers between devices  71.6 us (37%)
  starting transfers between devices  40.1 us (21%)
  local copies, waits for them, and re-layouts  4.69 us (2%)
  other arithmetic  3.04 us (2%)
    pallas_call x13, Pallas kernels, call(): pl.pallas_call(kernel, name=name, in_specs=[pl.BlockSpec(memory_space=plt...  71.8 us
    ppermute x39, waiting for transfers between devices, send(): return lax.ppermute(value, AXES, perm)  71.6 us
    ppermute x39, starting transfers between devices, send(): return lax.ppermute(value, AXES, perm)  40.1 us
  transfers between devices with their start and end apart: 39, of which 17 were waited for; matrix products, arithmetic and copies ran while one was open for 0% of the time, Pallas kernels for 34%

profile of v1, /device:TPU:0, one launch (start us, length us, event | category | flops | bytes accessed | tf_op | source)
XLA Modules:
  0.0 192.5 jit_solution(15863377763820409972)
XLA Ops:
  2.2 3.0 %collective-permute-start.4 = (bf16[2,256,768]{2,1,0:T(8,128)(2,1)S(1)}, bf16[2,256,768]{2,1,0:T(8,128)(2,1)S(1)}, u32[]{:S(2)}, u32[]{:S(2)}) collective-permute-start(bf16[2,256,768]{2,1,0:T(8,128)(2,1)S(1)} %constant_dynamic-slice_fusion.1), channel_id=1, source_target_pairs={{0,1},{1,0},{2,3},{3,2},{4,5},{5,4},{6,7},{7,6},{8,9},{9,8},{10,11... | collective-permute-start | bytes 2359304 | tf_op jit(solution)/shard_map/ppermute | solution.py:76
  5.4 3.7 %collective-permute-start.2 = (bf16[24,3200]{1,0:T(8,128)(2,1)S(1)}, bf16[24,3200]{1,0:T(8,128)(2,1)S(1)}, u32[]{:S(2)}, u32[]{:S(2)}) collective-permute-start(bf16[24,3200]{1,0:T(8,128)(2,1)S(1)} %pad_maximum_fusion.4), channel_id=1, source_target_pairs={{0,24},{1,25},{2,26},{3,27},{4,28},{5,29},{6,30},{7,31},{8,0},{9,1... | collective-permute-start | bytes 460808 | tf_op jit(solution)/shard_map/ppermute | solution.py:76
  11.6 3.7 %collective-permute-done.3 = bf16[96,768]{1,0:T(8,128)(2,1)S(1)} collective-permute-done((bf16[96,768]{1,0:T(8,128)(2,1)S(1)}, bf16[96,768]{1,0:T(8,128)(2,1)S(1)}, u32[]{:S(2)}, u32[]{:S(2)}) %collective-permute-start.3) | collective-permute-done | bytes 147488 | tf_op jit(solution)/shard_map/ppermute | solution.py:76
  15.3 6.6 %collective-permute-done.1 = bf16[24,3200]{1,0:T(8,128)(2,1)S(1)} collective-permute-done((bf16[24,3200]{1,0:T(8,128)(2,1)S(1)}, bf16[24,3200]{1,0:T(8,128)(2,1)S(1)}, u32[]{:S(2)}, u32[]{:S(2)}) %collective-permute-start.1) | collective-permute-done | bytes 153632 | tf_op jit(solution)/shard_map/ppermute | solution.py:76
  23.0 1.8 collective-permute-start.5
  27.9 6.6 %mix_norm.1 = (f32[1024,768]{1,0:T(8,128)S(1)}, f32[1024,1]{1,0:T(8,128)S(1)}) custom-call(s32[4]{0:T(128)S(1)} %pad_add_fusion.place_ref, bf16[4,256,768]{2,1,0:T(8,128)(2,1)S(1)} %copy-done.1, bf16[2,256,768]{2,1,0:T(8,128)(2,1)S(1)} %collective-permute-done.4.other_ref, bf16[1024,512]{1,0:T(8,128)(2,1)S(1)} %copy-done.4, bf16[1536,768]{1,0:T(8,128)(2,1)} %constant.108.hid_hbm), custom_call_target="tpu_custom_call" | custom-call | flops 4026531840 | bytes 7864320 | tf_op jit(solution)/shard_map/mix_norm/pallas_call | solution.py:150
  36.2 1.6 collective-permute-start.9
  38.2 14.2 %collective-permute-done.10.refs_3_ = bf16[4,96,768]{2,1,0:T(8,128)(2,1)S(1)} collective-permute-done((bf16[4,96,768]{2,1,0:T(8,128)(2,1)S(1)}, bf16[4,96,768]{2,1,0:T(8,128)(2,1)S(1)}, u32[]{:S(2)}, u32[]{:S(2)}) %collective-permute-start.10) | collective-permute-done | bytes 589856 | tf_op jit(solution)/shard_map/ppermute | solution.py:76
  53.0 2.6 %collective-permute-start.12 = (bf16[8,24,3200]{2,1,0:T(8,128)(2,1)S(1)}, bf16[8,24,3200]{2,1,0:T(8,128)(2,1)S(1)}, u32[]{:S(2)}, u32[]{:S(2)}) collective-permute-start(bf16[8,24,3200]{2,1,0:T(8,128)(2,1)S(1)} %collective-permute-done.9.refs_2_), channel_id=1, source_target_pairs={{0,2},{1,3},{2,0},{3,1},{4,6},{5,7},{6,4},{7,5},{8,10},{9,11},{10,... | collective-permute-start | bytes 3686408 | tf_op jit(solution)/shard_map/ppermute | solution.py:76
  56.3 2.2 %collective-permute-start.13 = (bf16[4,96,768]{2,1,0:T(8,128)(2,1)S(1)}, bf16[4,96,768]{2,1,0:T(8,128)(2,1)S(1)}, u32[]{:S(2)}, u32[]{:S(2)}) collective-permute-start(bf16[4,96,768]{2,1,0:T(8,128)(2,1)S(1)} %collective-permute-done.10.refs_3_), channel_id=1, source_target_pairs={{0,8},{1,9},{2,10},{3,11},{4,12},{5,13},{6,14},{7,15},{8,16},{9,17... | collective-permute-start | bytes 1769480 | tf_op jit(solution)/shard_map/ppermute | solution.py:76
  59.0 2.4 %first_weight.1 = (bf16[768,3072]{1,0:T(8,128)(2,1)S(1)}, f32[1,3072]{1,0:T(1,128)S(1)}, f32[8,768]{1,0:T(8,128)S(1)}, bf16[1024,768]{1,0:T(8,128)(2,1)S(1)}, bf16[768,1024]{1,0:T(8,128)(2,1)S(1)}) custom-call(s32[4]{0:T(128)S(1)} %pad_add_fusion.place_ref, f32[1024,768]{1,0:T(8,128)S(1)} %get-tuple-element.137.xhat_ref.refs_4_, ...), custom_call_target="tpu_custom_call" | custom-call | flops 1572864 | bytes 9830400 | tf_op jit(solution)/shard_map/first_weight/pallas_call | solution.py:150
  63.1 7.5 %ffn_in_gelu.1 = (bf16[1024,1536]{1,0:T(8,128)(2,1)S(1)}, bf16[1024,1536]{1,0:T(8,128)(2,1)S(1)}) custom-call(bf16[1024,768]{1,0:T(8,128)(2,1)S(1)} %get-tuple-element.155.low_ref, bf16[768,3072]{1,0:T(8,128)(2,1)S(1)} %get-tuple-element.147.w_ref.w_in_ref, f32[1,3072]{1,0:T(1,128)S(1)} %get-tuple-element.148.bias_ref), custom_call_target="tpu_custom_call" | custom-call | flops 2415919104 | bytes 6291456 | tf_op jit(solution)/shard_map/ffn_in_gelu/pallas_call | solution.py:150
  70.6 3.9 %collective-permute-done.13.refs_4_ = bf16[4,96,768]{2,1,0:T(8,128)(2,1)S(1)} collective-permute-done((bf16[4,96,768]{2,1,0:T(8,128)(2,1)S(1)}, bf16[4,96,768]{2,1,0:T(8,128)(2,1)S(1)}, u32[]{:S(2)}, u32[]{:S(2)}) %collective-permute-start.13) | collective-permute-done | bytes 589856 | tf_op jit(solution)/shard_map/ppermute | solution.py:76
  76.9 12.4 %ffn_in_out.1 = (bf16[1024,1536]{1,0:T(8,128)(2,1)S(1)}, bf16[1024,1536]{1,0:T(8,128)(2,1)S(1)}, bf16[3072,768]{1,0:T(8,128)(2,1)S(1)}, f32[1024,768]{1,0:T(8,128)S(1)}) custom-call(s32[4]{0:T(128)S(1)} %pad_add_fusion.place_ref, bf16[1024,768]{1,0:T(8,128)(2,1)S(1)} %get-tuple-element.155.low_ref, bf16[768,3072]{1,0:T(8,128)(2,1)S(1)} %get-tuple-element.147.w_ref.w_in_ref, ...), custom_call_target="tpu_custom_call" | custom-call | flops 6039797760 | bytes 12582912 | tf_op jit(solution)/shard_map/ffn_in_out/pallas_call | solution.py:150
  91.0 4.7 %ffn_out_norm.1 = (bf16[3072,768]{1,0:T(8,128)(2,1)S(1)}, bf16[2,256,768]{2,1,0:T(8,128)(2,1)S(1)}, bf16[2,256,768]{2,1,0:T(8,128)(2,1)S(1)}, f32[1024,768]{1,0:...) custom-call(s32[4]{0:T(128)S(1)} %pad_add_fusion.place_ref, ...), custom_call_target="tpu_custom_call", output_to_operand_aliasing={{0}: (3, {})} | custom-call | flops 1207959552 | bytes 23592960 | tf_op jit(solution)/shard_map/ffn_out_norm/pallas_call | solution.py:150
  95.7 2.3 %grad_w_out.2 = (bf16[1,4,96,768]{3,2,1,0:T(8,128)(2,1)S(1)}, bf16[1,4,96,768]{3,2,1,0:T(8,128)(2,1)S(1)}) custom-call(s32[4]{0:T(128)S(1)} %pad_add_fusion.place_ref, bf16[1024,1536]{1,0:T(8,128)(2,1)S(1)} %get-tuple-element.154.act_0_ref.refs_0_, bf16[1024,1536]{1,0:T(8,128)(2,1)S(1)} %get-tuple-element.161.refs_1_.act_1_ref, ...), custom_call_target="tpu_custom_call" | custom-call | flops 1207959552 | bytes 1572864 | tf_op jit(solution)/shard_map/grad_w_out/pallas_call | solution.py:150
  98.2 5.9 %grad_w_out.3 = (bf16[3,4,96,768]{3,2,1,0:T(8,128)(2,1)S(1)}, bf16[3,4,96,768]{3,2,1,0:T(8,128)(2,1)S(1)}) custom-call(s32[4]{0:T(128)S(1)} %pad_add_fusion.place_ref, bf16[1024,1536]{1,0:T(8,128)(2,1)S(1)} %get-tuple-element.154.act_0_ref.refs_0_, bf16[1024,1536]{1,0:T(8,128)(2,1)S(1)} %get-tuple-element.161.refs_1_.act_1_ref, ...), custom_call_target="tpu_custom_call" | custom-call | flops 3623878656 | bytes 4718592 | tf_op jit(solution)/shard_map/grad_w_out/pallas_call | solution.py:150
  104.8 1.6 collective-permute-start.25
  106.9 19.0 %ffn_back.1 = (bf16[1024,768]{1,0:T(8,128)(2,1)S(1)}, f32[1024,768]{1,0:T(8,128)S(1)}, bf16[2,4,2,24,3200]{4,3,2,1,0:T(8,128)(2,1)S(1)}, bf16[2,4,2,24,3200]{4,3,2,1,0:T(8,128)(2,1)S(1)}) custom-call(s32[4]{0:T(128)S(1)} %pad_add_fusion.place_ref, bf16[1024,768]{1,0:T(8,128)(2,1)S(1)} %get-tuple-element.184.low_ref, ...), custom_call_target="tpu_custom_call" | custom-call | flops 14495514624 | bytes 28311552 | tf_op jit(solution)/shard_map/ffn_back/pallas_call | solution.py:150
  128.9 3.2 %collective-permute-done.27 = bf16[2,4,2,24,3200]{4,3,1,2,0:T(8,128)(2,1)S(1)} collective-permute-done((bf16[2,4,2,24,3200]{4,3,1,2,0:T(8,128)(2,1)S(1)}, bf16[2,4,2,24,3200]{4,3,1,2,0:T(8,128)(2,1)S(1)}, u32[]{:S(2)}, u32[]{:S(2)}) %collective-permute-start.27) | collective-permute-done | bytes 2457632 | tf_op jit(solution)/shard_map/ppermute | solution.py:76
  132.4 1.6 collective-permute-start.28
  135.5 1.7 join_rows.3
  137.6 5.0 %mix_back.1 = (bf16[2,256,768]{2,1,0:T(8,128)(2,1)S(1)}, f32[2,256,768]{2,1,0:T(8,128)S(1)}) custom-call(s32[4]{0:T(128)S(1)} %pad_add_fusion.place_ref, bf16[1024,768]{1,0:T(8,128)(2,1)S(1)} %get-tuple-element.204.low_ref, f32[1024,768]{1,0:T(8,128)S(1)} %get-tuple-element.205.one_ref, bf16[768,1536]{1,0:T(8,128)(2,1)S(1)} %copy-done.2, ...), custom_call_target="tpu_custom_call" | custom-call | flops 4026531840 | bytes 7864320 | tf_op jit(solution)/shard_map/mix_back/pallas_call | solution.py:150
  142.6 8.5 %collective-permute-done.29 = bf16[4,96,768]{2,1,0:T(8,128)(2,1)S(1)} collective-permute-done((bf16[4,96,768]{2,1,0:T(8,128)(2,1)S(1)}, bf16[4,96,768]{2,1,0:T(8,128)(2,1)S(1)}, u32[]{:S(2)}, u32[]{:S(2)}) %collective-permute-start.29) | collective-permute-done | bytes 589856 | tf_op jit(solution)/shard_map/ppermute | solution.py:76
  153.5 1.6 collective-permute-start.32
  155.1 10.5 %collective-permute-done.32.refs_1_ = bf16[1,256,768]{2,1,0:T(8,128)(2,1)S(1)} collective-permute-done((bf16[1,256,768]{2,1,0:T(8,128)(2,1)S(1)}, bf16[1,256,768]{2,1,0:T(8,128)(2,1)S(1)}, u32[]{:S(2)}, u32[]{:S(2)}) %collective-permute-start.32) | collective-permute-done | bytes 393248 | tf_op jit(solution)/shard_map/ppermute | solution.py:76
  165.6 2.6 %collective-permute-done.31 = bf16[4,96,768]{2,1,0:T(8,128)(2,1)S(1)} collective-permute-done((bf16[4,96,768]{2,1,0:T(8,128)(2,1)S(1)}, bf16[4,96,768]{2,1,0:T(8,128)(2,1)S(1)}, u32[]{:S(2)}, u32[]{:S(2)}) %collective-permute-start.31) | collective-permute-done | bytes 589856 | tf_op jit(solution)/shard_map/ppermute | solution.py:76
  168.6 2.2 %collective-permute-start.37 = (bf16[1,256,768]{2,1,0:T(8,128)(2,1)S(1)}, bf16[1,256,768]{2,1,0:T(8,128)(2,1)S(1)}, u32[]{:S(2)}, u32[]{:S(2)}) collective-permute-start(bf16[1,256,768]{2,1,0:T(8,128)(2,1)S(1)} %get-tuple-element.217), channel_id=1, source_target_pairs={{0,1},{1,0},{2,3},{3,2},{4,5},{5,4},{6,7},{7,6},{8,9},{9,8},{10,11... | collective-permute-start | bytes 1179656 | tf_op jit(solution)/shard_map/ppermute | solution.py:76
  173.0 2.0 %join_rows.4.refs_1_ = f32[4,256,768]{2,1,0:T(8,128)} custom-call(s32[4]{0:T(128)S(1)} %pad_add_fusion.place_ref, f32[2,256,768]{2,1,0:T(8,128)S(1)} %get-tuple-element.218.refs_0_, bf16[1,256,768]{2,1,0:T(8,128)(2,1)S(1)} %collective-permute-done.32.refs_1_), custom_call_target="tpu_custom_call" | custom-call | bytes 6291456 | tf_op jit(solution)/shard_map/join_rows/pallas_call | solution.py:150
  175.0 3.5 %collective-permute-done.35.refs_2_ = bf16[24,3200]{1,0:T(8,128)(2,1)S(1)} collective-permute-done((bf16[24,3200]{1,0:T(8,128)(2,1)S(1)}, bf16[24,3200]{1,0:T(8,128)(2,1)S(1)}, u32[]{:S(2)}, u32[]{:S(2)}) %collective-permute-start.35) | collective-permute-done | bytes 153632 | tf_op jit(solution)/shard_map/ppermute | solution.py:76
  178.5 6.5 %collective-permute-done.34.refs_1_ = bf16[24,3200]{1,0:T(8,128)(2,1)S(1)} collective-permute-done((bf16[24,3200]{1,0:T(8,128)(2,1)S(1)}, bf16[24,3200]{1,0:T(8,128)(2,1)S(1)}, u32[]{:S(2)}, u32[]{:S(2)}) %collective-permute-start.34) | collective-permute-done | bytes 153632 | tf_op jit(solution)/shard_map/ppermute | solution.py:76
  188.6 3.2 %collective-permute-done.38 = bf16[96,768]{1,0:T(8,128)(2,1)S(1)} collective-permute-done((bf16[96,768]{1,0:T(8,128)(2,1)S(1)}, bf16[96,768]{1,0:T(8,128)(2,1)S(1)}, u32[]{:S(2)}, u32[]{:S(2)}) %collective-permute-start.38) | collective-permute-done | bytes 147488 | tf_op jit(solution)/shard_map/ppermute | solution.py:76
  (117 shorter events, 33.7 us)
Async XLA Ops:
  2.2 20.6 %collective-permute-start.4 = (bf16[2,256,768]{2,1,0:T(8,128)(2,1)S(1)}, bf16[2,256,768]{2,1,0:T(8,128)(2,1)S(1)}, u32[]{:S(2)}, u32[]{:S(2)}) collective-permute-start(bf16[2,256,768]{2,1,0:T(8,128)(2,1)S(1)} %constant_dynamic-slice_fusion.1), channel_id=1, source_target_pairs={{0,1},{1,0},{2,3},{3,2},{4,5},{5,4},{6,7},{7,6},{8,9},{9,8},{10,11... | collective-permute-start | bytes 2359304 | tf_op jit(solution)/shard_map/ppermute | solution.py:76
  5.4 9.8 %collective-permute-start.2 = (bf16[24,3200]{1,0:T(8,128)(2,1)S(1)}, bf16[24,3200]{1,0:T(8,128)(2,1)S(1)}, u32[]{:S(2)}, u32[]{:S(2)}) collective-permute-start(bf16[24,3200]{1,0:T(8,128)(2,1)S(1)} %pad_maximum_fusion.4), channel_id=1, source_target_pairs={{0,24},{1,25},{2,26},{3,27},{4,28},{5,29},{6,30},{7,31},{8,0},{9,1... | collective-permute-start | bytes 460808 | tf_op jit(solution)/shard_map/ppermute | solution.py:76
  9.1 12.7 %collective-permute-start.1 = (bf16[24,3200]{1,0:T(8,128)(2,1)S(1)}, bf16[24,3200]{1,0:T(8,128)(2,1)S(1)}, u32[]{:S(2)}, u32[]{:S(2)}) collective-permute-start(bf16[24,3200]{1,0:T(8,128)(2,1)S(1)} %pad_maximum_fusion.4), channel_id=1, source_target_pairs={{0,16},{1,17},{2,18},{3,19},{4,20},{5,21},{6,22},{7,23},{8,24},{9,... | collective-permute-start | bytes 460808 | tf_op jit(solution)/shard_map/ppermute | solution.py:76
  9.1 12.7 %collective-permute-start = (bf16[24,3200]{1,0:T(8,128)(2,1)S(1)}, bf16[24,3200]{1,0:T(8,128)(2,1)S(1)}, u32[]{:S(2)}, u32[]{:S(2)}) collective-permute-start(bf16[24,3200]{1,0:T(8,128)(2,1)S(1)} %pad_maximum_fusion.4), channel_id=1, source_target_pairs={{0,8},{1,9},{2,10},{3,11},{4,12},{5,13},{6,14},{7,15},{8,16},{9,17... | collective-permute-start | bytes 460808 | tf_op jit(solution)/shard_map/ppermute | solution.py:76
  23.0 13.0 %collective-permute-start.8 = (bf16[4,24,3200]{2,1,0:T(8,128)(2,1)S(1)}, bf16[4,24,3200]{2,1,0:T(8,128)(2,1)S(1)}, u32[]{:S(2)}, u32[]{:S(2)}) collective-permute-start(bf16[4,24,3200]{2,1,0:T(8,128)(2,1)S(1)} %pad_maximum_fusion.1.refs_0_), channel_id=1, source_target_pairs={{0,2},{1,3},{2,0},{3,1},{4,6},{5,7},{6,4},{7,5},{8,10},{9,11},{10,... | collective-permute-start | bytes 1843208 | tf_op jit(solution)/shard_map/ppermute | solution.py:76
  23.0 13.0 %collective-permute-start.5 = (bf16[4,24,3200]{2,1,0:T(8,128)(2,1)S(1)}, bf16[4,24,3200]{2,1,0:T(8,128)(2,1)S(1)}, u32[]{:S(2)}, u32[]{:S(2)}) collective-permute-start(bf16[4,24,3200]{2,1,0:T(8,128)(2,1)S(1)} %pad_maximum_fusion.1.refs_0_), channel_id=1, source_target_pairs={{0,4},{1,5},{2,3},{3,2},{4,0},{5,1},{6,7},{7,6},{8,12},{9,13},{10,... | collective-permute-start | bytes 1843208 | tf_op jit(solution)/shard_map/ppermute | solution.py:76
  24.8 9.9 %collective-permute-start.7 = (bf16[2,96,768]{2,1,0:T(8,128)(2,1)S(1)}, bf16[2,96,768]{2,1,0:T(8,128)(2,1)S(1)}, u32[]{:S(2)}, u32[]{:S(2)}) collective-permute-start(bf16[2,96,768]{2,1,0:T(8,128)(2,1)S(1)} %pad_maximum_fusion.3.refs_0_), channel_id=1, source_target_pairs={{0,1},{1,0},{2,3},{3,2},{4,5},{5,4},{6,7},{7,6},{8,9},{9,8},{10,11... | collective-permute-start | bytes 884744 | tf_op jit(solution)/shard_map/ppermute | solution.py:76
  26.3 9.7 %collective-permute-start.6 = (bf16[2,96,768]{2,1,0:T(8,128)(2,1)S(1)}, bf16[2,96,768]{2,1,0:T(8,128)(2,1)S(1)}, u32[]{:S(2)}, u32[]{:S(2)}) collective-permute-start(bf16[2,96,768]{2,1,0:T(8,128)(2,1)S(1)} %pad_maximum_fusion.3.refs_0_), channel_id=1, source_target_pairs={{0,8},{1,9},{2,10},{3,11},{4,12},{5,13},{6,14},{7,15},{8,16},{9,17... | collective-permute-start | bytes 884744 | tf_op jit(solution)/shard_map/ppermute | solution.py:76
  36.2 16.8 %collective-permute-start.9 = (bf16[8,24,3200]{2,1,0:T(8,128)(2,1)S(1)}, bf16[8,24,3200]{2,1,0:T(8,128)(2,1)S(1)}, u32[]{:S(2)}, u32[]{:S(2)}) collective-permute-start(bf16[8,24,3200]{2,1,0:T(8,128)(2,1)S(1)} %pad_maximum_fusion), channel_id=1, source_target_pairs={{0,1},{1,0},{2,6},{3,7},{4,5},{5,4},{6,2},{7,3},{8,9},{9,8},{10,14... | collective-permute-start | bytes 3686408 | tf_op jit(solution)/shard_map/ppermute | solution.py:76
  37.8 14.6 %collective-permute-start.10 = (bf16[4,96,768]{2,1,0:T(8,128)(2,1)S(1)}, bf16[4,96,768]{2,1,0:T(8,128)(2,1)S(1)}, u32[]{:S(2)}, u32[]{:S(2)}) collective-permute-start(bf16[4,96,768]{2,1,0:T(8,128)(2,1)S(1)} %pad_maximum_fusion.2), channel_id=1, source_target_pairs={{0,8},{1,9},{2,10},{3,11},{4,12},{5,13},{6,14},{7,15},{8,16},{9,17... | collective-permute-start | bytes 1769480 | tf_op jit(solution)/shard_map/ppermute | solution.py:76
  55.7 6.9 %collective-permute-start.15 = (bf16[2,96,768]{2,1,0:T(8,128)(2,1)S(1)}, bf16[2,96,768]{2,1,0:T(8,128)(2,1)S(1)}, u32[]{:S(2)}, u32[]{:S(2)}) collective-permute-start(bf16[2,96,768]{2,1,0:T(8,128)(2,1)S(1)} %pad_maximum_fusion.3.refs_0_), channel_id=1, source_target_pairs={{0,2},{1,3},{2,0},{3,1},{4,6},{5,7},{6,4},{7,5},{8,10},{9,11},{10,... | collective-permute-start | bytes 884744 | tf_op jit(solution)/shard_map/ppermute | solution.py:76
  56.3 14.3 %collective-permute-start.18 = (bf16[4,96,768]{2,1,0:T(8,128)(2,1)S(1)}, bf16[4,96,768]{2,1,0:T(8,128)(2,1)S(1)}, u32[]{:S(2)}, u32[]{:S(2)}) collective-permute-start(bf16[4,96,768]{2,1,0:T(8,128)(2,1)S(1)} %collective-permute-done.10.refs_3_), channel_id=1, source_target_pairs={{0,2},{1,3},{2,0},{3,1},{4,6},{5,7},{6,4},{7,5},{8,10},{9,11},{10,... | collective-permute-start | bytes 1769480 | tf_op jit(solution)/shard_map/ppermute | solution.py:76
  56.3 18.1 %collective-permute-start.13 = (bf16[4,96,768]{2,1,0:T(8,128)(2,1)S(1)}, bf16[4,96,768]{2,1,0:T(8,128)(2,1)S(1)}, u32[]{:S(2)}, u32[]{:S(2)}) collective-permute-start(bf16[4,96,768]{2,1,0:T(8,128)(2,1)S(1)} %collective-permute-done.10.refs_3_), channel_id=1, source_target_pairs={{0,8},{1,9},{2,10},{3,11},{4,12},{5,13},{6,14},{7,15},{8,16},{9,17... | collective-permute-start | bytes 1769480 | tf_op jit(solution)/shard_map/ppermute | solution.py:76
  61.5 12.9 %collective-permute-start.14 = (bf16[1,256,768]{2,1,0:T(8,128)(2,1)S(1)}, bf16[1,256,768]{2,1,0:T(8,128)(2,1)S(1)}, u32[]{:S(2)}, u32[]{:S(2)}) collective-permute-start(bf16[1,256,768]{2,1,0:T(8,128)(2,1)S(1)} %get-tuple-element.240), channel_id=1, source_target_pairs={{0,1},{1,0},{2,3},{3,2},{4,5},{5,4},{6,7},{7,6},{8,9},{9,8},{10,11... | collective-permute-start | bytes 1179656 | tf_op jit(solution)/shard_map/ppermute | solution.py:76
  62.5 8.0 %collective-permute-start.16 = (bf16[2,96,768]{2,1,0:T(8,128)(2,1)S(1)}, bf16[2,96,768]{2,1,0:T(8,128)(2,1)S(1)}, u32[]{:S(2)}, u32[]{:S(2)}) collective-permute-start(bf16[2,96,768]{2,1,0:T(8,128)(2,1)S(1)} %collective-permute-done.7.refs_1_), channel_id=1, source_target_pairs={{0,2},{1,3},{2,0},{3,1},{4,6},{5,7},{6,4},{7,5},{8,10},{9,11},{10,... | collective-permute-start | bytes 884744 | tf_op jit(solution)/shard_map/ppermute | solution.py:76
  62.6 8.0 %collective-permute-start.17 = (bf16[2,96,768]{2,1,0:T(8,128)(2,1)S(1)}, bf16[2,96,768]{2,1,0:T(8,128)(2,1)S(1)}, u32[]{:S(2)}, u32[]{:S(2)}) collective-permute-start(bf16[2,96,768]{2,1,0:T(8,128)(2,1)S(1)} %collective-permute-done.6.refs_2_), channel_id=1, source_target_pairs={{0,2},{1,3},{2,0},{3,1},{4,6},{5,7},{6,4},{7,5},{8,10},{9,11},{10,... | collective-permute-start | bytes 884744 | tf_op jit(solution)/shard_map/ppermute | solution.py:76
  74.5 14.9 %collective-permute-start.20 = (bf16[2,96,768]{2,1,0:T(8,128)(2,1)S(1)}, bf16[2,96,768]{2,1,0:T(8,128)(2,1)S(1)}, u32[]{:S(2)}, u32[]{:S(2)}) collective-permute-start(bf16[2,96,768]{2,1,0:T(8,128)(2,1)S(1)} %slice.67), channel_id=1, source_target_pairs={{0,8},{1,9},{2,10},{3,11},{4,12},{5,13},{6,14},{7,15},{8,16},{9,17... | collective-permute-start | bytes 884744 | tf_op jit(solution)/shard_map/ppermute | solution.py:76
  75.4 14.0 %collective-permute-start.21 = (bf16[1,256,768]{2,1,0:T(8,128)(2,1)S(1)}, bf16[1,256,768]{2,1,0:T(8,128)(2,1)S(1)}, u32[]{:S(2)}, u32[]{:S(2)}) collective-permute-start(bf16[1,256,768]{2,1,0:T(8,128)(2,1)S(1)} %get-tuple-element.164), channel_id=1, source_target_pairs={{0,1},{1,0},{2,3},{3,2},{4,5},{5,4},{6,7},{7,6},{8,9},{9,8},{10,11... | collective-permute-start | bytes 1179656 | tf_op jit(solution)/shard_map/ppermute | solution.py:76
  104.3 21.6 %collective-permute-start.24 = (bf16[3,4,96,768]{3,2,1,0:T(8,128)(2,1)S(1)}, bf16[3,4,96,768]{3,2,1,0:T(8,128)(2,1)S(1)}, u32[]{:S(2)}, u32[]{:S(2)}) collective-permute-start(bf16[3,4,96,768]{3,2,1,0:T(8,128)(2,1)S(1)} %get-tuple-element.181), channel_id=1, source_target_pairs={{0,2},{1,3},{2,0},{3,1},{4,6},{5,7},{6,4},{7,5},{8,10},{9,11},{10,... | collective-permute-start | bytes 5308424 | tf_op jit(solution)/shard_map/ppermute | solution.py:76
  104.8 21.2 %collective-permute-start.25 = (bf16[4,96,768]{2,1,0:T(8,128)(2,1)S(1)}, bf16[4,96,768]{2,1,0:T(8,128)(2,1)S(1)}, u32[]{:S(2)}, u32[]{:S(2)}) collective-permute-start(bf16[4,96,768]{2,1,0:T(8,128)(2,1)S(1)} %add_bitcast_fusion), channel_id=1, source_target_pairs={{0,8},{1,9},{2,10},{3,11},{4,12},{5,13},{6,14},{7,15},{8,16},{9,17... | collective-permute-start | bytes 1769480 | tf_op jit(solution)/shard_map/ppermute | solution.py:76
  106.4 19.6 %collective-permute-start.26 = (bf16[2,256,768]{2,1,0:T(8,128)(2,1)S(1)}, bf16[2,256,768]{2,1,0:T(8,128)(2,1)S(1)}, u32[]{:S(2)}, u32[]{:S(2)}) collective-permute-start(bf16[2,256,768]{2,1,0:T(8,128)(2,1)S(1)} %get-tuple-element.183), channel_id=1, source_target_pairs={{0,1},{1,0},{2,3},{3,2},{4,5},{5,4},{6,7},{7,6},{8,9},{9,8},{10,11... | collective-permute-start | bytes 2359304 | tf_op jit(solution)/shard_map/ppermute | solution.py:76
  132.4 18.7 %collective-permute-start.28 = (bf16[4,2,24,3200]{3,2,0,1:T(8,128)(2,1)S(1)}, bf16[4,2,24,3200]{3,2,0,1:T(8,128)(2,1)S(1)}, u32[]{:S(2)}, u32[]{:S(2)}) collective-permute-start(bf16[4,2,24,3200]{3,2,0,1:T(8,128)(2,1)S(1)} %fusion), channel_id=1, source_target_pairs={{0,1},{1,0},{2,6},{3,7},{4,5},{5,4},{6,2},{7,3},{8,9},{9,8},{10,14... | collective-permute-start | bytes 3686408 | tf_op jit(solution)/shard_map/ppermute | solution.py:76
  134.0 17.1 %collective-permute-start.29 = (bf16[4,96,768]{2,1,0:T(8,128)(2,1)S(1)}, bf16[4,96,768]{2,1,0:T(8,128)(2,1)S(1)}, u32[]{:S(2)}, u32[]{:S(2)}) collective-permute-start(bf16[4,96,768]{2,1,0:T(8,128)(2,1)S(1)} %bitcast_add_fusion.3), channel_id=1, source_target_pairs={{0,8},{1,9},{2,10},{3,11},{4,12},{5,13},{6,14},{7,15},{8,16},{9,17... | collective-permute-start | bytes 1769480 | tf_op jit(solution)/shard_map/ppermute | solution.py:76
  151.8 16.3 %collective-permute-start.31 = (bf16[4,96,768]{2,1,0:T(8,128)(2,1)S(1)}, bf16[4,96,768]{2,1,0:T(8,128)(2,1)S(1)}, u32[]{:S(2)}, u32[]{:S(2)}) collective-permute-start(bf16[4,96,768]{2,1,0:T(8,128)(2,1)S(1)} %fusion.2), channel_id=1, source_target_pairs={{0,8},{1,9},{2,10},{3,11},{4,12},{5,13},{6,14},{7,15},{8,16},{9,17... | collective-permute-start | bytes 1769480 | tf_op jit(solution)/shard_map/ppermute | solution.py:76
  152.0 16.2 %collective-permute-start.30 = (bf16[4,24,3200]{2,1,0:T(8,128)(2,1)S(1)}, bf16[4,24,3200]{2,1,0:T(8,128)(2,1)S(1)}, u32[]{:S(2)}, u32[]{:S(2)}) collective-permute-start(bf16[4,24,3200]{2,1,0:T(8,128)(2,1)S(1)} %fusion.3), channel_id=1, source_target_pairs={{0,4},{1,5},{2,3},{3,2},{4,0},{5,1},{6,7},{7,6},{8,12},{9,13},{10,... | collective-permute-start | bytes 1843208 | tf_op jit(solution)/shard_map/ppermute | solution.py:76
  153.5 12.1 %collective-permute-start.32 = (bf16[1,256,768]{2,1,0:T(8,128)(2,1)S(1)}, bf16[1,256,768]{2,1,0:T(8,128)(2,1)S(1)}, u32[]{:S(2)}, u32[]{:S(2)}) collective-permute-start(bf16[1,256,768]{2,1,0:T(8,128)(2,1)S(1)} %get-tuple-element.238), channel_id=1, source_target_pairs={{0,1},{1,0},{2,3},{3,2},{4,5},{5,4},{6,7},{7,6},{8,9},{9,8},{10,11... | collective-permute-start | bytes 1179656 | tf_op jit(solution)/shard_map/ppermute | solution.py:76
  168.6 16.4 %collective-permute-start.36 = (bf16[2,96,768]{2,1,0:T(8,128)(2,1)S(1)}, bf16[2,96,768]{2,1,0:T(8,128)(2,1)S(1)}, u32[]{:S(2)}, u32[]{:S(2)}) collective-permute-start(bf16[2,96,768]{2,1,0:T(8,128)(2,1)S(1)} %slice.119), channel_id=1, source_target_pairs={{0,4},{1,5},{2,6},{3,7},{4,0},{5,1},{6,2},{7,3},{8,12},{9,13},{10,... | collective-permute-start | bytes 884744 | tf_op jit(solution)/shard_map/ppermute | solution.py:76
  168.6 16.4 %collective-permute-start.37 = (bf16[1,256,768]{2,1,0:T(8,128)(2,1)S(1)}, bf16[1,256,768]{2,1,0:T(8,128)(2,1)S(1)}, u32[]{:S(2)}, u32[]{:S(2)}) collective-permute-start(bf16[1,256,768]{2,1,0:T(8,128)(2,1)S(1)} %get-tuple-element.217), channel_id=1, source_target_pairs={{0,1},{1,0},{2,3},{3,2},{4,5},{5,4},{6,7},{7,6},{8,9},{9,8},{10,11... | collective-permute-start | bytes 1179656 | tf_op jit(solution)/shard_map/ppermute | solution.py:76
  170.9 7.6 %collective-permute-start.35 = (bf16[24,3200]{1,0:T(8,128)(2,1)S(1)}, bf16[24,3200]{1,0:T(8,128)(2,1)S(1)}, u32[]{:S(2)}, u32[]{:S(2)}) collective-permute-start(bf16[24,3200]{1,0:T(8,128)(2,1)S(1)} %get-tuple-element.234), channel_id=1, source_target_pairs={{0,24},{1,25},{2,26},{3,27},{4,28},{5,29},{6,30},{7,31},{8,0},{9,1... | collective-permute-start | bytes 460808 | tf_op jit(solution)/shard_map/ppermute | solution.py:76
  171.9 13.1 %collective-permute-start.34 = (bf16[24,3200]{1,0:T(8,128)(2,1)S(1)}, bf16[24,3200]{1,0:T(8,128)(2,1)S(1)}, u32[]{:S(2)}, u32[]{:S(2)}) collective-permute-start(bf16[24,3200]{1,0:T(8,128)(2,1)S(1)} %get-tuple-element.235), channel_id=1, source_target_pairs={{0,16},{1,17},{2,18},{3,19},{4,20},{5,21},{6,22},{7,23},{8,24},{9,... | collective-permute-start | bytes 460808 | tf_op jit(solution)/shard_map/ppermute | solution.py:76
  171.9 13.1 %collective-permute-start.33 = (bf16[24,3200]{1,0:T(8,128)(2,1)S(1)}, bf16[24,3200]{1,0:T(8,128)(2,1)S(1)}, u32[]{:S(2)}, u32[]{:S(2)}) collective-permute-start(bf16[24,3200]{1,0:T(8,128)(2,1)S(1)} %get-tuple-element.236), channel_id=1, source_target_pairs={{0,8},{1,9},{2,10},{3,11},{4,12},{5,13},{6,14},{7,15},{8,16},{9,17... | collective-permute-start | bytes 460808 | tf_op jit(solution)/shard_map/ppermute | solution.py:76
  185.1 6.7 %collective-permute-start.38 = (bf16[96,768]{1,0:T(8,128)(2,1)S(1)}, bf16[96,768]{1,0:T(8,128)(2,1)S(1)}, u32[]{:S(2)}, u32[]{:S(2)}) collective-permute-start(bf16[96,768]{1,0:T(8,128)(2,1)S(1)} %fusion.8), channel_id=1, source_target_pairs={{0,1},{1,0},{2,3},{3,2},{4,5},{5,4},{6,7},{7,6},{8,9},{9,8},{10,11... | collective-permute-start | bytes 442376 | tf_op jit(solution)/shard_map/ppermute | solution.py:76
  (22 other events, 155.0 us)

commit v2 on v1

--- a/solution.py
+++ b/solution.py
@@ -726,8 +726,9 @@
 
 
 def finish_kernel(own_ref, *refs, spots):
-    parts, (w_ref, *smalls) = refs[:3], refs[3:]
+    parts, (first_ref, near_ref, out_ref, w_ref, *smalls) = refs[:3], refs[3:]
     split = w_ref.shape[1]
+    out_ref[...] = first_ref[...] + near_ref[...].astype(F32)
     total = own_ref[...]
     for ref in parts:
         total += ref[...].astype(F32)
@@ -736,15 +737,15 @@
         ref[...] = total[line : line + 1, split + at : split + at + ref.shape[1]]
 
 
-def finish(own, parts, split, sizes, spots):
+def finish(own, parts, first, near, split, sizes, spots):
     rows, _ = own.shape
     return vmem_call(
         functools.partial(finish_kernel, spots=spots),
-        "finish_w_in",
-        [((rows, split), F32)] + [((1, size), F32) for size in sizes],
+        "finish_sums",
+        [(first.shape, F32), ((rows, split), F32)] + [((1, size), F32) for size in sizes],
         4,
         cost(3 * rows * split, 14 * rows * split),
-    )(own, *parts)
+    )(own, *parts, first, near)
 
 
 def add_up(keep, other):
@@ -884,14 +885,15 @@
             ffn_back(place, start, d_resid, slopes, w_out, w_in, norm, low_t, sums_two, True),
         )
         quad = add_up(add_up(keep_b[0], twin_b[0]), ring)
-        twin, quad = together(core(away), quad)
-        first, ring, output, (gt_send, gt_keep) = together(
-            low_send(add_up(keep[0], twin[0]), grid.across_1),
+        twin, quad = together(core(away[0]), quad)
+        first, ring, output, twin_1, (gt_send, gt_keep) = together(
+            low_send(add_up(keep[0], twin), grid.across_1),
             low_send(quad, grid.ring),
             join(place, out_keep, out_other),
+            core(away[1]),
             mix_back(place, d_mix, d_one, *back_tables),
         )
-        pair = add_up(add_up(keep[1], twin[1]), first)
+        pair = add_up(add_up(keep[1], twin_1), first)
         quad = add_up(add_up(keep_b[1], twin_b[1]), ring)
         second, ring, gt_0 = together(
             low_send(pair[:, 0], grid.across_0),
@@ -902,16 +904,22 @@
         quad = add_up(add_up(keep_b[2], twin_b[2]), ring)
         gt_1 = send(after(gt_send[1:], quad), grid.blocks)
         grad_tokens = join(place, gt_keep, gt_0)
-        parts, far, gt_1, grad_tokens = together(
-            [low_send(pick(column, ahead[step]), grid.shifts[step]) for step in range(1, 4)],
+        parts, far, gt_1, grad_tokens, column = together(
+            [low_send(pick(column, ahead[step]), grid.shifts[step]) for step in (2, 3)],
             low_send(quad[2:], grid.across),
             gt_1,
             grad_tokens,
+            column,
         )
         quad = add_up(quad[:2], far)
-        my_w_out = add_up(quad[0], low_send(quad[1], grid.blocks))
-        grad_tokens = join(place, gt_keep, gt_1, 1, grad_tokens)
-        my_w_in, *my_small = finish(pick(column, ahead[0]), parts, hidden, sizes, spots)
+        near, last, grad_tokens = together(
+            low_send(quad[1], grid.blocks),
+            low_send(pick(column, ahead[1]), grid.shifts[1]),
+            join(place, gt_keep, gt_1, 1, grad_tokens),
+        )
+        my_w_out, my_w_in, *my_small = finish(
+            pick(column, ahead[0]), parts + [last], quad[0], near, hidden, sizes, spots
+        )
         my_small = [v.reshape(-1) for v in my_small]
     else:
         output = join_rows(out_keep, send(out_send, grid.blocks))

time: 193 us -> 189 us (0.979)
  local copies, waits for them, and re-layouts: 4.69 us -> 2.31 us
    unnamed x30 -> x26, local copies, waits for them, and re-layouts: 2.8 us -> 0.38 us
    ppermute x39 -> x40, waiting for transfers between devices: 71.6 us -> 71 us  [send(): return lax.ppermute(value, AXES, perm)]
    ppermute x39 -> x40, starting transfers between devices: 40.1 us -> 40.2 us  [send(): return lax.ppermute(value, AXES, perm)]
  transfers between devices with their start and end apart: 39 -> 40, of which waited for: 17 -> 18; matrix products, arithmetic and copies ran while one was open for 0% -> 1% of each run, Pallas kernels for 34% -> 34%
where the time goes in v2:
time: 189 us
  Pallas kernels  71.9 us (38%)
  waiting for transfers between devices  71 us (38%)
  starting transfers between devices  40.2 us (21%)
  local copies, waits for them, and re-layouts  2.31 us (1%)
  other arithmetic  2.14 us (1%)
    pallas_call x13, Pallas kernels, call(): pl.pallas_call(kernel, name=name, in_specs=[pl.BlockSpec(memory_space=plt...  71.9 us
    ppermute x40, waiting for transfers between devices, send(): return lax.ppermute(value, AXES, perm)  71 us
    ppermute x40, starting transfers between devices, send(): return lax.ppermute(value, AXES, perm)  40.2 us
  transfers between devices with their start and end apart: 40, of which 18 were waited for; matrix products, arithmetic and copies ran while one was open for 1% of the time, Pallas kernels for 34%

profile of v2, /device:TPU:0, one launch (start us, length us, event | category | flops | bytes accessed | tf_op | source)
XLA Modules:
  0.0 188.8 jit_solution(13043228746829476593)
XLA Ops:
  2.2 3.0 %collective-permute-start.4 = (bf16[2,256,768]{2,1,0:T(8,128)(2,1)S(1)}, bf16[2,256,768]{2,1,0:T(8,128)(2,1)S(1)}, u32[]{:S(2)}, u32[]{:S(2)}) collective-permute-start(bf16[2,256,768]{2,1,0:T(8,128)(2,1)S(1)} %constant_dynamic-slice_fusion.1), channel_id=1, source_target_pairs={{0,1},{1,0},{2,3},{3,2},{4,5},{5,4},{6,7},{7,6},{8,9},{9,8},{10,11... | collective-permute-start | bytes 2359304 | tf_op jit(solution)/shard_map/ppermute | solution.py:76
  5.4 3.7 %collective-permute-start.2 = (bf16[24,3200]{1,0:T(8,128)(2,1)S(1)}, bf16[24,3200]{1,0:T(8,128)(2,1)S(1)}, u32[]{:S(2)}, u32[]{:S(2)}) collective-permute-start(bf16[24,3200]{1,0:T(8,128)(2,1)S(1)} %pad_maximum_fusion.4), channel_id=1, source_target_pairs={{0,24},{1,25},{2,26},{3,27},{4,28},{5,29},{6,30},{7,31},{8,0},{9,1... | collective-permute-start | bytes 460808 | tf_op jit(solution)/shard_map/ppermute | solution.py:76
  11.6 3.7 %collective-permute-done.3 = bf16[96,768]{1,0:T(8,128)(2,1)S(1)} collective-permute-done((bf16[96,768]{1,0:T(8,128)(2,1)S(1)}, bf16[96,768]{1,0:T(8,128)(2,1)S(1)}, u32[]{:S(2)}, u32[]{:S(2)}) %collective-permute-start.3) | collective-permute-done | bytes 147488 | tf_op jit(solution)/shard_map/ppermute | solution.py:76
  15.3 6.6 %collective-permute-done.1 = bf16[24,3200]{1,0:T(8,128)(2,1)S(1)} collective-permute-done((bf16[24,3200]{1,0:T(8,128)(2,1)S(1)}, bf16[24,3200]{1,0:T(8,128)(2,1)S(1)}, u32[]{:S(2)}, u32[]{:S(2)}) %collective-permute-start.1) | collective-permute-done | bytes 153632 | tf_op jit(solution)/shard_map/ppermute | solution.py:76
  23.0 1.8 collective-permute-start.5
  27.9 6.6 %mix_norm.1 = (f32[1024,768]{1,0:T(8,128)S(1)}, f32[1024,1]{1,0:T(8,128)S(1)}) custom-call(s32[4]{0:T(128)S(1)} %pad_add_fusion.place_ref, bf16[4,256,768]{2,1,0:T(8,128)(2,1)S(1)} %copy-done.1, bf16[2,256,768]{2,1,0:T(8,128)(2,1)S(1)} %collective-permute-done.4.other_ref, bf16[1024,512]{1,0:T(8,128)(2,1)S(1)} %copy-done.4, bf16[1536,768]{1,0:T(8,128)(2,1)} %constant.108.hid_hbm), custom_call_target="tpu_custom_call" | custom-call | flops 4026531840 | bytes 7864320 | tf_op jit(solution)/shard_map/mix_norm/pallas_call | solution.py:150
  36.2 1.6 collective-permute-start.9
  38.2 14.2 %collective-permute-done.10.refs_3_ = bf16[4,96,768]{2,1,0:T(8,128)(2,1)S(1)} collective-permute-done((bf16[4,96,768]{2,1,0:T(8,128)(2,1)S(1)}, bf16[4,96,768]{2,1,0:T(8,128)(2,1)S(1)}, u32[]{:S(2)}, u32[]{:S(2)}) %collective-permute-start.10) | collective-permute-done | bytes 589856 | tf_op jit(solution)/shard_map/ppermute | solution.py:76
  53.0 2.6 %collective-permute-start.12 = (bf16[8,24,3200]{2,1,0:T(8,128)(2,1)S(1)}, bf16[8,24,3200]{2,1,0:T(8,128)(2,1)S(1)}, u32[]{:S(2)}, u32[]{:S(2)}) collective-permute-start(bf16[8,24,3200]{2,1,0:T(8,128)(2,1)S(1)} %collective-permute-done.9.refs_2_), channel_id=1, source_target_pairs={{0,2},{1,3},{2,0},{3,1},{4,6},{5,7},{6,4},{7,5},{8,10},{9,11},{10,... | collective-permute-start | bytes 3686408 | tf_op jit(solution)/shard_map/ppermute | solution.py:76
  56.3 2.2 %collective-permute-start.13 = (bf16[4,96,768]{2,1,0:T(8,128)(2,1)S(1)}, bf16[4,96,768]{2,1,0:T(8,128)(2,1)S(1)}, u32[]{:S(2)}, u32[]{:S(2)}) collective-permute-start(bf16[4,96,768]{2,1,0:T(8,128)(2,1)S(1)} %collective-permute-done.10.refs_3_), channel_id=1, source_target_pairs={{0,8},{1,9},{2,10},{3,11},{4,12},{5,13},{6,14},{7,15},{8,16},{9,17... | collective-permute-start | bytes 1769480 | tf_op jit(solution)/shard_map/ppermute | solution.py:76
  59.0 2.4 %first_weight.1 = (bf16[768,3072]{1,0:T(8,128)(2,1)S(1)}, f32[1,3072]{1,0:T(1,128)S(1)}, f32[8,768]{1,0:T(8,128)S(1)}, bf16[1024,768]{1,0:T(8,128)(2,1)S(1)}, bf16[768,1024]{1,0:T(8,128)(2,1)S(1)}) custom-call(s32[4]{0:T(128)S(1)} %pad_add_fusion.place_ref, f32[1024,768]{1,0:T(8,128)S(1)} %get-tuple-element.142.xhat_ref.refs_4_, ...), custom_call_target="tpu_custom_call" | custom-call | flops 1572864 | bytes 9830400 | tf_op jit(solution)/shard_map/first_weight/pallas_call | solution.py:150
  63.1 7.5 %ffn_in_gelu.1 = (bf16[1024,1536]{1,0:T(8,128)(2,1)S(1)}, bf16[1024,1536]{1,0:T(8,128)(2,1)S(1)}) custom-call(bf16[1024,768]{1,0:T(8,128)(2,1)S(1)} %get-tuple-element.160.low_ref, bf16[768,3072]{1,0:T(8,128)(2,1)S(1)} %get-tuple-element.152.w_ref.w_in_ref, f32[1,3072]{1,0:T(1,128)S(1)} %get-tuple-element.153.bias_ref), custom_call_target="tpu_custom_call" | custom-call | flops 2415919104 | bytes 6291456 | tf_op jit(solution)/shard_map/ffn_in_gelu/pallas_call | solution.py:150
  70.6 3.9 %collective-permute-done.13.refs_4_ = bf16[4,96,768]{2,1,0:T(8,128)(2,1)S(1)} collective-permute-done((bf16[4,96,768]{2,1,0:T(8,128)(2,1)S(1)}, bf16[4,96,768]{2,1,0:T(8,128)(2,1)S(1)}, u32[]{:S(2)}, u32[]{:S(2)}) %collective-permute-start.13) | collective-permute-done | bytes 589856 | tf_op jit(solution)/shard_map/ppermute | solution.py:76
  76.9 12.4 %ffn_in_out.1 = (bf16[1024,1536]{1,0:T(8,128)(2,1)S(1)}, bf16[1024,1536]{1,0:T(8,128)(2,1)S(1)}, bf16[3072,768]{1,0:T(8,128)(2,1)S(1)}, f32[1024,768]{1,0:T(8,128)S(1)}) custom-call(s32[4]{0:T(128)S(1)} %pad_add_fusion.place_ref, bf16[1024,768]{1,0:T(8,128)(2,1)S(1)} %get-tuple-element.160.low_ref, bf16[768,3072]{1,0:T(8,128)(2,1)S(1)} %get-tuple-element.152.w_ref.w_in_ref, ...), custom_call_target="tpu_custom_call" | custom-call | flops 6039797760 | bytes 12582912 | tf_op jit(solution)/shard_map/ffn_in_out/pallas_call | solution.py:150
  91.0 4.7 %ffn_out_norm.1 = (bf16[3072,768]{1,0:T(8,128)(2,1)S(1)}, bf16[2,256,768]{2,1,0:T(8,128)(2,1)S(1)}, bf16[2,256,768]{2,1,0:T(8,128)(2,1)S(1)}, f32[1024,768]{1,0:...) custom-call(s32[4]{0:T(128)S(1)} %pad_add_fusion.place_ref, ...), custom_call_target="tpu_custom_call", output_to_operand_aliasing={{0}: (3, {})} | custom-call | flops 1207959552 | bytes 23592960 | tf_op jit(solution)/shard_map/ffn_out_norm/pallas_call | solution.py:150
  95.7 2.3 %grad_w_out.2 = (bf16[1,4,96,768]{3,2,1,0:T(8,128)(2,1)S(1)}, bf16[1,4,96,768]{3,2,1,0:T(8,128)(2,1)S(1)}) custom-call(s32[4]{0:T(128)S(1)} %pad_add_fusion.place_ref, bf16[1024,1536]{1,0:T(8,128)(2,1)S(1)} %get-tuple-element.159.act_0_ref.refs_0_, bf16[1024,1536]{1,0:T(8,128)(2,1)S(1)} %get-tuple-element.166.refs_1_.act_1_ref, ...), custom_call_target="tpu_custom_call" | custom-call | flops 1207959552 | bytes 1572864 | tf_op jit(solution)/shard_map/grad_w_out/pallas_call | solution.py:150
  98.2 5.9 %grad_w_out.3 = (bf16[3,4,96,768]{3,2,1,0:T(8,128)(2,1)S(1)}, bf16[3,4,96,768]{3,2,1,0:T(8,128)(2,1)S(1)}) custom-call(s32[4]{0:T(128)S(1)} %pad_add_fusion.place_ref, bf16[1024,1536]{1,0:T(8,128)(2,1)S(1)} %get-tuple-element.159.act_0_ref.refs_0_, bf16[1024,1536]{1,0:T(8,128)(2,1)S(1)} %get-tuple-element.166.refs_1_.act_1_ref, ...), custom_call_target="tpu_custom_call" | custom-call | flops 3623878656 | bytes 4718592 | tf_op jit(solution)/shard_map/grad_w_out/pallas_call | solution.py:150
  104.8 1.6 collective-permute-start.25
  106.9 19.0 %ffn_back.1 = (bf16[1024,768]{1,0:T(8,128)(2,1)S(1)}, f32[1024,768]{1,0:T(8,128)S(1)}, bf16[2,4,2,24,3200]{4,3,2,1,0:T(8,128)(2,1)S(1)}, bf16[2,4,2,24,3200]{4,3,2,1,0:T(8,128)(2,1)S(1)}) custom-call(s32[4]{0:T(128)S(1)} %pad_add_fusion.place_ref, bf16[1024,768]{1,0:T(8,128)(2,1)S(1)} %get-tuple-element.189.low_ref, ...), custom_call_target="tpu_custom_call" | custom-call | flops 14495514624 | bytes 28311552 | tf_op jit(solution)/shard_map/ffn_back/pallas_call | solution.py:150
  126.9 2.2 %collective-permute-done.27 = bf16[4,2,24,3200]{3,2,0,1:T(8,128)(2,1)S(1)} collective-permute-done((bf16[4,2,24,3200]{3,2,0,1:T(8,128)(2,1)S(1)}, bf16[4,2,24,3200]{3,2,0,1:T(8,128)(2,1)S(1)}, u32[]{:S(2)}, u32[]{:S(2)}) %collective-permute-start.27) | collective-permute-done | bytes 1228832 | tf_op jit(solution)/shard_map/ppermute | solution.py:76
  132.6 1.7 join_rows.3
  134.6 5.0 %mix_back.1 = (bf16[2,256,768]{2,1,0:T(8,128)(2,1)S(1)}, f32[2,256,768]{2,1,0:T(8,128)S(1)}) custom-call(s32[4]{0:T(128)S(1)} %pad_add_fusion.place_ref, bf16[1024,768]{1,0:T(8,128)(2,1)S(1)} %get-tuple-element.209.low_ref, f32[1024,768]{1,0:T(8,128)S(1)} %get-tuple-element.210.one_ref, bf16[768,1536]{1,0:T(8,128)(2,1)S(1)} %copy-done.2, ...), custom_call_target="tpu_custom_call" | custom-call | flops 4026531840 | bytes 7864320 | tf_op jit(solution)/shard_map/mix_back/pallas_call | solution.py:150
  139.6 8.5 %collective-permute-done.29 = bf16[4,96,768]{2,1,0:T(8,128)(2,1)S(1)} collective-permute-done((bf16[4,96,768]{2,1,0:T(8,128)(2,1)S(1)}, bf16[4,96,768]{2,1,0:T(8,128)(2,1)S(1)}, u32[]{:S(2)}, u32[]{:S(2)}) %collective-permute-start.29) | collective-permute-done | bytes 589856 | tf_op jit(solution)/shard_map/ppermute | solution.py:76
  150.4 1.6 collective-permute-start.33
  152.0 10.5 %collective-permute-done.33.refs_1_ = bf16[1,256,768]{2,1,0:T(8,128)(2,1)S(1)} collective-permute-done((bf16[1,256,768]{2,1,0:T(8,128)(2,1)S(1)}, bf16[1,256,768]{2,1,0:T(8,128)(2,1)S(1)}, u32[]{:S(2)}, u32[]{:S(2)}) %collective-permute-start.33) | collective-permute-done | bytes 393248 | tf_op jit(solution)/shard_map/ppermute | solution.py:76
  162.5 2.2 %collective-permute-done.32 = bf16[4,96,768]{2,1,0:T(8,128)(2,1)S(1)} collective-permute-done((bf16[4,96,768]{2,1,0:T(8,128)(2,1)S(1)}, bf16[4,96,768]{2,1,0:T(8,128)(2,1)S(1)}, u32[]{:S(2)}, u32[]{:S(2)}) %collective-permute-start.32) | collective-permute-done | bytes 589856 | tf_op jit(solution)/shard_map/ppermute | solution.py:76
  165.1 2.2 %collective-permute-start.37 = (bf16[1,256,768]{2,1,0:T(8,128)(2,1)S(1)}, bf16[1,256,768]{2,1,0:T(8,128)(2,1)S(1)}, u32[]{:S(2)}, u32[]{:S(2)}) collective-permute-start(bf16[1,256,768]{2,1,0:T(8,128)(2,1)S(1)} %get-tuple-element.222), channel_id=1, source_target_pairs={{0,1},{1,0},{2,3},{3,2},{4,5},{5,4},{6,7},{7,6},{8,9},{9,8},{10,11... | collective-permute-start | bytes 1179656 | tf_op jit(solution)/shard_map/ppermute | solution.py:76
  168.8 2.0 %join_rows.4.refs_1_ = f32[4,256,768]{2,1,0:T(8,128)} custom-call(s32[4]{0:T(128)S(1)} %pad_add_fusion.place_ref, f32[2,256,768]{2,1,0:T(8,128)S(1)} %get-tuple-element.223.refs_0_, bf16[1,256,768]{2,1,0:T(8,128)(2,1)S(1)} %collective-permute-done.33.refs_1_), custom_call_target="tpu_custom_call" | custom-call | bytes 6291456 | tf_op jit(solution)/shard_map/join_rows/pallas_call | solution.py:150
  170.8 4.4 %collective-permute-done.35.refs_1_ = bf16[24,3200]{1,0:T(8,128)(2,1)S(1)} collective-permute-done((bf16[24,3200]{1,0:T(8,128)(2,1)S(1)}, bf16[24,3200]{1,0:T(8,128)(2,1)S(1)}, u32[]{:S(2)}, u32[]{:S(2)}) %collective-permute-start.35) | collective-permute-done | bytes 153632 | tf_op jit(solution)/shard_map/ppermute | solution.py:76
  175.1 3.7 %collective-permute-done.34.refs_0_ = bf16[24,3200]{1,0:T(8,128)(2,1)S(1)} collective-permute-done((bf16[24,3200]{1,0:T(8,128)(2,1)S(1)}, bf16[24,3200]{1,0:T(8,128)(2,1)S(1)}, u32[]{:S(2)}, u32[]{:S(2)}) %collective-permute-start.34) | collective-permute-done | bytes 153632 | tf_op jit(solution)/shard_map/ppermute | solution.py:76
  181.9 3.7 %collective-permute-done.38.refs_4_ = bf16[96,768]{1,0:T(8,128)(2,1)S(1)} collective-permute-done((bf16[96,768]{1,0:T(8,128)(2,1)S(1)}, bf16[96,768]{1,0:T(8,128)(2,1)S(1)}, u32[]{:S(2)}, u32[]{:S(2)}) %collective-permute-start.38) | collective-permute-done | bytes 147488 | tf_op jit(solution)/shard_map/ppermute | solution.py:76
  185.6 2.2 %collective-permute-done.39.refs_2_ = bf16[24,3200]{1,0:T(8,128)(2,1)S(1)} collective-permute-done((bf16[24,3200]{1,0:T(8,128)(2,1)S(1)}, bf16[24,3200]{1,0:T(8,128)(2,1)S(1)}, u32[]{:S(2)}, u32[]{:S(2)}) %collective-permute-start.39) | collective-permute-done | bytes 153632 | tf_op jit(solution)/shard_map/ppermute | solution.py:76
  (116 shorter events, 32.2 us)
Async XLA Ops:
  2.2 20.6 %collective-permute-start.4 = (bf16[2,256,768]{2,1,0:T(8,128)(2,1)S(1)}, bf16[2,256,768]{2,1,0:T(8,128)(2,1)S(1)}, u32[]{:S(2)}, u32[]{:S(2)}) collective-permute-start(bf16[2,256,768]{2,1,0:T(8,128)(2,1)S(1)} %constant_dynamic-slice_fusion.1), channel_id=1, source_target_pairs={{0,1},{1,0},{2,3},{3,2},{4,5},{5,4},{6,7},{7,6},{8,9},{9,8},{10,11... | collective-permute-start | bytes 2359304 | tf_op jit(solution)/shard_map/ppermute | solution.py:76
  5.4 9.8 %collective-permute-start.2 = (bf16[24,3200]{1,0:T(8,128)(2,1)S(1)}, bf16[24,3200]{1,0:T(8,128)(2,1)S(1)}, u32[]{:S(2)}, u32[]{:S(2)}) collective-permute-start(bf16[24,3200]{1,0:T(8,128)(2,1)S(1)} %pad_maximum_fusion.4), channel_id=1, source_target_pairs={{0,24},{1,25},{2,26},{3,27},{4,28},{5,29},{6,30},{7,31},{8,0},{9,1... | collective-permute-start | bytes 460808 | tf_op jit(solution)/shard_map/ppermute | solution.py:76
  9.1 12.7 %collective-permute-start.1 = (bf16[24,3200]{1,0:T(8,128)(2,1)S(1)}, bf16[24,3200]{1,0:T(8,128)(2,1)S(1)}, u32[]{:S(2)}, u32[]{:S(2)}) collective-permute-start(bf16[24,3200]{1,0:T(8,128)(2,1)S(1)} %pad_maximum_fusion.4), channel_id=1, source_target_pairs={{0,16},{1,17},{2,18},{3,19},{4,20},{5,21},{6,22},{7,23},{8,24},{9,... | collective-permute-start | bytes 460808 | tf_op jit(solution)/shard_map/ppermute | solution.py:76
  9.1 12.7 %collective-permute-start = (bf16[24,3200]{1,0:T(8,128)(2,1)S(1)}, bf16[24,3200]{1,0:T(8,128)(2,1)S(1)}, u32[]{:S(2)}, u32[]{:S(2)}) collective-permute-start(bf16[24,3200]{1,0:T(8,128)(2,1)S(1)} %pad_maximum_fusion.4), channel_id=1, source_target_pairs={{0,8},{1,9},{2,10},{3,11},{4,12},{5,13},{6,14},{7,15},{8,16},{9,17... | collective-permute-start | bytes 460808 | tf_op jit(solution)/shard_map/ppermute | solution.py:76
  23.0 13.0 %collective-permute-start.8 = (bf16[4,24,3200]{2,1,0:T(8,128)(2,1)S(1)}, bf16[4,24,3200]{2,1,0:T(8,128)(2,1)S(1)}, u32[]{:S(2)}, u32[]{:S(2)}) collective-permute-start(bf16[4,24,3200]{2,1,0:T(8,128)(2,1)S(1)} %pad_maximum_fusion.1.refs_0_), channel_id=1, source_target_pairs={{0,2},{1,3},{2,0},{3,1},{4,6},{5,7},{6,4},{7,5},{8,10},{9,11},{10,... | collective-permute-start | bytes 1843208 | tf_op jit(solution)/shard_map/ppermute | solution.py:76
  23.0 13.0 %collective-permute-start.5 = (bf16[4,24,3200]{2,1,0:T(8,128)(2,1)S(1)}, bf16[4,24,3200]{2,1,0:T(8,128)(2,1)S(1)}, u32[]{:S(2)}, u32[]{:S(2)}) collective-permute-start(bf16[4,24,3200]{2,1,0:T(8,128)(2,1)S(1)} %pad_maximum_fusion.1.refs_0_), channel_id=1, source_target_pairs={{0,4},{1,5},{2,3},{3,2},{4,0},{5,1},{6,7},{7,6},{8,12},{9,13},{10,... | collective-permute-start | bytes 1843208 | tf_op jit(solution)/shard_map/ppermute | solution.py:76
  24.8 9.9 %collective-permute-start.7 = (bf16[2,96,768]{2,1,0:T(8,128)(2,1)S(1)}, bf16[2,96,768]{2,1,0:T(8,128)(2,1)S(1)}, u32[]{:S(2)}, u32[]{:S(2)}) collective-permute-start(bf16[2,96,768]{2,1,0:T(8,128)(2,1)S(1)} %pad_maximum_fusion.3.refs_0_), channel_id=1, source_target_pairs={{0,1},{1,0},{2,3},{3,2},{4,5},{5,4},{6,7},{7,6},{8,9},{9,8},{10,11... | collective-permute-start | bytes 884744 | tf_op jit(solution)/shard_map/ppermute | solution.py:76
  26.3 9.7 %collective-permute-start.6 = (bf16[2,96,768]{2,1,0:T(8,128)(2,1)S(1)}, bf16[2,96,768]{2,1,0:T(8,128)(2,1)S(1)}, u32[]{:S(2)}, u32[]{:S(2)}) collective-permute-start(bf16[2,96,768]{2,1,0:T(8,128)(2,1)S(1)} %pad_maximum_fusion.3.refs_0_), channel_id=1, source_target_pairs={{0,8},{1,9},{2,10},{3,11},{4,12},{5,13},{6,14},{7,15},{8,16},{9,17... | collective-permute-start | bytes 884744 | tf_op jit(solution)/shard_map/ppermute | solution.py:76
  36.2 16.8 %collective-permute-start.9 = (bf16[8,24,3200]{2,1,0:T(8,128)(2,1)S(1)}, bf16[8,24,3200]{2,1,0:T(8,128)(2,1)S(1)}, u32[]{:S(2)}, u32[]{:S(2)}) collective-permute-start(bf16[8,24,3200]{2,1,0:T(8,128)(2,1)S(1)} %pad_maximum_fusion), channel_id=1, source_target_pairs={{0,1},{1,0},{2,6},{3,7},{4,5},{5,4},{6,2},{7,3},{8,9},{9,8},{10,14... | collective-permute-start | bytes 3686408 | tf_op jit(solution)/shard_map/ppermute | solution.py:76
  37.8 14.6 %collective-permute-start.10 = (bf16[4,96,768]{2,1,0:T(8,128)(2,1)S(1)}, bf16[4,96,768]{2,1,0:T(8,128)(2,1)S(1)}, u32[]{:S(2)}, u32[]{:S(2)}) collective-permute-start(bf16[4,96,768]{2,1,0:T(8,128)(2,1)S(1)} %pad_maximum_fusion.2), channel_id=1, source_target_pairs={{0,8},{1,9},{2,10},{3,11},{4,12},{5,13},{6,14},{7,15},{8,16},{9,17... | collective-permute-start | bytes 1769480 | tf_op jit(solution)/shard_map/ppermute | solution.py:76
  55.7 6.9 %collective-permute-start.15 = (bf16[2,96,768]{2,1,0:T(8,128)(2,1)S(1)}, bf16[2,96,768]{2,1,0:T(8,128)(2,1)S(1)}, u32[]{:S(2)}, u32[]{:S(2)}) collective-permute-start(bf16[2,96,768]{2,1,0:T(8,128)(2,1)S(1)} %pad_maximum_fusion.3.refs_0_), channel_id=1, source_target_pairs={{0,2},{1,3},{2,0},{3,1},{4,6},{5,7},{6,4},{7,5},{8,10},{9,11},{10,... | collective-permute-start | bytes 884744 | tf_op jit(solution)/shard_map/ppermute | solution.py:76
  56.3 14.3 %collective-permute-start.18 = (bf16[4,96,768]{2,1,0:T(8,128)(2,1)S(1)}, bf16[4,96,768]{2,1,0:T(8,128)(2,1)S(1)}, u32[]{:S(2)}, u32[]{:S(2)}) collective-permute-start(bf16[4,96,768]{2,1,0:T(8,128)(2,1)S(1)} %collective-permute-done.10.refs_3_), channel_id=1, source_target_pairs={{0,2},{1,3},{2,0},{3,1},{4,6},{5,7},{6,4},{7,5},{8,10},{9,11},{10,... | collective-permute-start | bytes 1769480 | tf_op jit(solution)/shard_map/ppermute | solution.py:76
  56.3 18.1 %collective-permute-start.13 = (bf16[4,96,768]{2,1,0:T(8,128)(2,1)S(1)}, bf16[4,96,768]{2,1,0:T(8,128)(2,1)S(1)}, u32[]{:S(2)}, u32[]{:S(2)}) collective-permute-start(bf16[4,96,768]{2,1,0:T(8,128)(2,1)S(1)} %collective-permute-done.10.refs_3_), channel_id=1, source_target_pairs={{0,8},{1,9},{2,10},{3,11},{4,12},{5,13},{6,14},{7,15},{8,16},{9,17... | collective-permute-start | bytes 1769480 | tf_op jit(solution)/shard_map/ppermute | solution.py:76
  61.5 12.9 %collective-permute-start.14 = (bf16[1,256,768]{2,1,0:T(8,128)(2,1)S(1)}, bf16[1,256,768]{2,1,0:T(8,128)(2,1)S(1)}, u32[]{:S(2)}, u32[]{:S(2)}) collective-permute-start(bf16[1,256,768]{2,1,0:T(8,128)(2,1)S(1)} %get-tuple-element.251), channel_id=1, source_target_pairs={{0,1},{1,0},{2,3},{3,2},{4,5},{5,4},{6,7},{7,6},{8,9},{9,8},{10,11... | collective-permute-start | bytes 1179656 | tf_op jit(solution)/shard_map/ppermute | solution.py:76
  62.5 8.0 %collective-permute-start.16 = (bf16[2,96,768]{2,1,0:T(8,128)(2,1)S(1)}, bf16[2,96,768]{2,1,0:T(8,128)(2,1)S(1)}, u32[]{:S(2)}, u32[]{:S(2)}) collective-permute-start(bf16[2,96,768]{2,1,0:T(8,128)(2,1)S(1)} %collective-permute-done.7.refs_1_), channel_id=1, source_target_pairs={{0,2},{1,3},{2,0},{3,1},{4,6},{5,7},{6,4},{7,5},{8,10},{9,11},{10,... | collective-permute-start | bytes 884744 | tf_op jit(solution)/shard_map/ppermute | solution.py:76
  62.6 8.0 %collective-permute-start.17 = (bf16[2,96,768]{2,1,0:T(8,128)(2,1)S(1)}, bf16[2,96,768]{2,1,0:T(8,128)(2,1)S(1)}, u32[]{:S(2)}, u32[]{:S(2)}) collective-permute-start(bf16[2,96,768]{2,1,0:T(8,128)(2,1)S(1)} %collective-permute-done.6.refs_2_), channel_id=1, source_target_pairs={{0,2},{1,3},{2,0},{3,1},{4,6},{5,7},{6,4},{7,5},{8,10},{9,11},{10,... | collective-permute-start | bytes 884744 | tf_op jit(solution)/shard_map/ppermute | solution.py:76
  74.5 14.9 %collective-permute-start.20 = (bf16[2,96,768]{2,1,0:T(8,128)(2,1)S(1)}, bf16[2,96,768]{2,1,0:T(8,128)(2,1)S(1)}, u32[]{:S(2)}, u32[]{:S(2)}) collective-permute-start(bf16[2,96,768]{2,1,0:T(8,128)(2,1)S(1)} %slice.67), channel_id=1, source_target_pairs={{0,8},{1,9},{2,10},{3,11},{4,12},{5,13},{6,14},{7,15},{8,16},{9,17... | collective-permute-start | bytes 884744 | tf_op jit(solution)/shard_map/ppermute | solution.py:76
  75.4 14.0 %collective-permute-start.21 = (bf16[1,256,768]{2,1,0:T(8,128)(2,1)S(1)}, bf16[1,256,768]{2,1,0:T(8,128)(2,1)S(1)}, u32[]{:S(2)}, u32[]{:S(2)}) collective-permute-start(bf16[1,256,768]{2,1,0:T(8,128)(2,1)S(1)} %get-tuple-element.169), channel_id=1, source_target_pairs={{0,1},{1,0},{2,3},{3,2},{4,5},{5,4},{6,7},{7,6},{8,9},{9,8},{10,11... | collective-permute-start | bytes 1179656 | tf_op jit(solution)/shard_map/ppermute | solution.py:76
  104.3 21.6 %collective-permute-start.24 = (bf16[3,4,96,768]{3,2,1,0:T(8,128)(2,1)S(1)}, bf16[3,4,96,768]{3,2,1,0:T(8,128)(2,1)S(1)}, u32[]{:S(2)}, u32[]{:S(2)}) collective-permute-start(bf16[3,4,96,768]{3,2,1,0:T(8,128)(2,1)S(1)} %get-tuple-element.186), channel_id=1, source_target_pairs={{0,2},{1,3},{2,0},{3,1},{4,6},{5,7},{6,4},{7,5},{8,10},{9,11},{10,... | collective-permute-start | bytes 5308424 | tf_op jit(solution)/shard_map/ppermute | solution.py:76
  104.8 21.2 %collective-permute-start.25 = (bf16[4,96,768]{2,1,0:T(8,128)(2,1)S(1)}, bf16[4,96,768]{2,1,0:T(8,128)(2,1)S(1)}, u32[]{:S(2)}, u32[]{:S(2)}) collective-permute-start(bf16[4,96,768]{2,1,0:T(8,128)(2,1)S(1)} %add_bitcast_fusion), channel_id=1, source_target_pairs={{0,8},{1,9},{2,10},{3,11},{4,12},{5,13},{6,14},{7,15},{8,16},{9,17... | collective-permute-start | bytes 1769480 | tf_op jit(solution)/shard_map/ppermute | solution.py:76
  106.4 19.6 %collective-permute-start.26 = (bf16[2,256,768]{2,1,0:T(8,128)(2,1)S(1)}, bf16[2,256,768]{2,1,0:T(8,128)(2,1)S(1)}, u32[]{:S(2)}, u32[]{:S(2)}) collective-permute-start(bf16[2,256,768]{2,1,0:T(8,128)(2,1)S(1)} %get-tuple-element.188), channel_id=1, source_target_pairs={{0,1},{1,0},{2,3},{3,2},{4,5},{5,4},{6,7},{7,6},{8,9},{9,8},{10,11... | collective-permute-start | bytes 2359304 | tf_op jit(solution)/shard_map/ppermute | solution.py:76
  126.2 13.4 %collective-permute-start.30 = (bf16[4,2,24,3200]{3,2,0,1:T(8,128)(2,1)S(1)}, bf16[4,2,24,3200]{3,2,0,1:T(8,128)(2,1)S(1)}, u32[]{:S(2)}, u32[]{:S(2)}) collective-permute-start(bf16[4,2,24,3200]{3,2,0,1:T(8,128)(2,1)S(1)} %get-tuple-element.244), channel_id=1, source_target_pairs={{0,2},{1,3},{2,0},{3,1},{4,6},{5,7},{6,4},{7,5},{8,10},{9,11},{10,... | collective-permute-start | bytes 3686408 | tf_op jit(solution)/shard_map/ppermute | solution.py:76
  129.4 18.7 %collective-permute-start.28 = (bf16[4,2,24,3200]{3,2,0,1:T(8,128)(2,1)S(1)}, bf16[4,2,24,3200]{3,2,0,1:T(8,128)(2,1)S(1)}, u32[]{:S(2)}, u32[]{:S(2)}) collective-permute-start(bf16[4,2,24,3200]{3,2,0,1:T(8,128)(2,1)S(1)} %fusion.1), channel_id=1, source_target_pairs={{0,1},{1,0},{2,6},{3,7},{4,5},{5,4},{6,2},{7,3},{8,9},{9,8},{10,14... | collective-permute-start | bytes 3686408 | tf_op jit(solution)/shard_map/ppermute | solution.py:76
  131.0 17.1 %collective-permute-start.29 = (bf16[4,96,768]{2,1,0:T(8,128)(2,1)S(1)}, bf16[4,96,768]{2,1,0:T(8,128)(2,1)S(1)}, u32[]{:S(2)}, u32[]{:S(2)}) collective-permute-start(bf16[4,96,768]{2,1,0:T(8,128)(2,1)S(1)} %bitcast_add_fusion.2), channel_id=1, source_target_pairs={{0,8},{1,9},{2,10},{3,11},{4,12},{5,13},{6,14},{7,15},{8,16},{9,17... | collective-permute-start | bytes 1769480 | tf_op jit(solution)/shard_map/ppermute | solution.py:76
  148.4 16.3 %collective-permute-start.32 = (bf16[4,96,768]{2,1,0:T(8,128)(2,1)S(1)}, bf16[4,96,768]{2,1,0:T(8,128)(2,1)S(1)}, u32[]{:S(2)}, u32[]{:S(2)}) collective-permute-start(bf16[4,96,768]{2,1,0:T(8,128)(2,1)S(1)} %fusion.3), channel_id=1, source_target_pairs={{0,8},{1,9},{2,10},{3,11},{4,12},{5,13},{6,14},{7,15},{8,16},{9,17... | collective-permute-start | bytes 1769480 | tf_op jit(solution)/shard_map/ppermute | solution.py:76
  148.9 15.8 %collective-permute-start.31 = (bf16[4,24,3200]{2,1,0:T(8,128)(2,1)S(1)}, bf16[4,24,3200]{2,1,0:T(8,128)(2,1)S(1)}, u32[]{:S(2)}, u32[]{:S(2)}) collective-permute-start(bf16[4,24,3200]{2,1,0:T(8,128)(2,1)S(1)} %fusion.4), channel_id=1, source_target_pairs={{0,4},{1,5},{2,3},{3,2},{4,0},{5,1},{6,7},{7,6},{8,12},{9,13},{10,... | collective-permute-start | bytes 1843208 | tf_op jit(solution)/shard_map/ppermute | solution.py:76
  150.4 12.1 %collective-permute-start.33 = (bf16[1,256,768]{2,1,0:T(8,128)(2,1)S(1)}, bf16[1,256,768]{2,1,0:T(8,128)(2,1)S(1)}, u32[]{:S(2)}, u32[]{:S(2)}) collective-permute-start(bf16[1,256,768]{2,1,0:T(8,128)(2,1)S(1)} %get-tuple-element.249), channel_id=1, source_target_pairs={{0,1},{1,0},{2,3},{3,2},{4,5},{5,4},{6,7},{7,6},{8,9},{9,8},{10,11... | collective-permute-start | bytes 1179656 | tf_op jit(solution)/shard_map/ppermute | solution.py:76
  165.1 13.8 %collective-permute-start.36 = (bf16[2,96,768]{2,1,0:T(8,128)(2,1)S(1)}, bf16[2,96,768]{2,1,0:T(8,128)(2,1)S(1)}, u32[]{:S(2)}, u32[]{:S(2)}) collective-permute-start(bf16[2,96,768]{2,1,0:T(8,128)(2,1)S(1)} %slice.123), channel_id=1, source_target_pairs={{0,4},{1,5},{2,6},{3,7},{4,0},{5,1},{6,2},{7,3},{8,12},{9,13},{10,... | collective-permute-start | bytes 884744 | tf_op jit(solution)/shard_map/ppermute | solution.py:76
  165.1 13.7 %collective-permute-start.37 = (bf16[1,256,768]{2,1,0:T(8,128)(2,1)S(1)}, bf16[1,256,768]{2,1,0:T(8,128)(2,1)S(1)}, u32[]{:S(2)}, u32[]{:S(2)}) collective-permute-start(bf16[1,256,768]{2,1,0:T(8,128)(2,1)S(1)} %get-tuple-element.222), channel_id=1, source_target_pairs={{0,1},{1,0},{2,3},{3,2},{4,5},{5,4},{6,7},{7,6},{8,9},{9,8},{10,11... | collective-permute-start | bytes 1179656 | tf_op jit(solution)/shard_map/ppermute | solution.py:76
  167.4 7.7 %collective-permute-start.35 = (bf16[24,3200]{1,0:T(8,128)(2,1)S(1)}, bf16[24,3200]{1,0:T(8,128)(2,1)S(1)}, u32[]{:S(2)}, u32[]{:S(2)}) collective-permute-start(bf16[24,3200]{1,0:T(8,128)(2,1)S(1)} %get-tuple-element.246), channel_id=1, source_target_pairs={{0,24},{1,25},{2,26},{3,27},{4,28},{5,29},{6,30},{7,31},{8,0},{9,1... | collective-permute-start | bytes 460808 | tf_op jit(solution)/shard_map/ppermute | solution.py:76
  168.8 10.0 %collective-permute-start.34 = (bf16[24,3200]{1,0:T(8,128)(2,1)S(1)}, bf16[24,3200]{1,0:T(8,128)(2,1)S(1)}, u32[]{:S(2)}, u32[]{:S(2)}) collective-permute-start(bf16[24,3200]{1,0:T(8,128)(2,1)S(1)} %get-tuple-element.247), channel_id=1, source_target_pairs={{0,16},{1,17},{2,18},{3,19},{4,20},{5,21},{6,22},{7,23},{8,24},{9,... | collective-permute-start | bytes 460808 | tf_op jit(solution)/shard_map/ppermute | solution.py:76
  179.7 8.1 %collective-permute-start.39 = (bf16[24,3200]{1,0:T(8,128)(2,1)S(1)}, bf16[24,3200]{1,0:T(8,128)(2,1)S(1)}, u32[]{:S(2)}, u32[]{:S(2)}) collective-permute-start(bf16[24,3200]{1,0:T(8,128)(2,1)S(1)} %fusion.7), channel_id=1, source_target_pairs={{0,8},{1,9},{2,10},{3,11},{4,12},{5,13},{6,14},{7,15},{8,16},{9,17... | collective-permute-start | bytes 460808 | tf_op jit(solution)/shard_map/ppermute | solution.py:76
  (21 other events, 157.2 us)

commit v3 on v2

--- a/solution.py
+++ b/solution.py
@@ -509,20 +509,20 @@
     def group(xx, yy):
         return jnp.where(place_ref[3] == yy, 0, 1) + jnp.where(place_ref[1] == xx, 0, 2)
 
-    def step(j, carry):
-        t, xx = j // 2, lax.rem(j, 2)
+    def step(t, carry):
         block = lax.rem(place_ref[0] + 7 - first - t, 4)
-        cut = pl.ds(pl.multiple_of(lax.rem(block, 2) * columns + xx * (columns // 2), LANES), columns // 2)
+        cut = pl.ds(pl.multiple_of(lax.rem(block, 2) * columns, LANES), columns)
         act = jnp.where(block >= 2, act_1_ref[:, cut], act_0_ref[:, cut])
         total = dot_tn(act, low_ref[...])
-        for yy in range(2):
-            one = total[yy * rows : (yy + 1) * rows]
-            two = total[(2 + yy) * rows : (3 + yy) * rows]
-            send_ref[t, group(xx, yy)] = jnp.where(c == 0, two, one).astype(BF16)
-            keep_ref[t, group(xx, yy)] = jnp.where(c == 0, one, two).astype(BF16)
+        for xx in range(2):
+            for yy in range(2):
+                at = (4 * xx + yy) * rows
+                one, two = total[at : at + rows], total[at + 2 * rows : at + 3 * rows]
+                send_ref[t, group(xx, yy)] = jnp.where(c == 0, two, one).astype(BF16)
+                keep_ref[t, group(xx, yy)] = jnp.where(c == 0, one, two).astype(BF16)
         return carry
 
-    lax.fori_loop(0, 2 * send_ref.shape[0], step, 0)
+    lax.fori_loop(0, send_ref.shape[0], step, 0)
 
 
 def grad_out(place, acts, d_low, nearby, rows, first, steps):
@@ -532,7 +532,7 @@
         functools.partial(grad_out_kernel, first=first),
         "grad_w_out",
         [(shape, BF16), (shape, BF16)],
-        6,
+        9,
         cost(16 * steps * count * rows * width, 16 * steps * count * rows),
         places=1,
     )(place, *acts, d_low, nearby)
@@ -603,17 +603,18 @@
     send_ref[:, :, :, :, split:] = jnp.zeros(send_ref.shape[:4] + (LANES,), BF16)
     keep_ref[:, :, :, :, split:] = jnp.zeros(keep_ref.shape[:4] + (LANES,), BF16)
     rows = send_ref.shape[3]
-    columns = split // 2
-    for z in range(4):
-        for cut in (slice(0, columns), slice(columns, split)):
-            total = dot(low_ref[8 * z * rows : 8 * (z + 1) * rows, :], pre_ref[:, cut])
+    columns = 768
+    for cut in (slice(at, at + columns) for at in range(0, split, columns)):
+        total = dot(low_ref[...], pre_ref[:, cut])
+        for z in range(4):
             for xx in range(2):
                 for yy in range(2):
-                    at = (4 * xx + yy) * rows
+                    at = (8 * z + 4 * xx + yy) * rows
                     first, second = total[at : at + rows], total[at + 2 * rows : at + 3 * rows]
                     away, stay = slot(place_ref, xx, yy, 1 - c), slot(place_ref, xx, yy, c)
                     send_ref[away[0], z, away[1], :, cut] = jnp.where(c == 0, second, first).astype(BF16)
                     keep_ref[stay[0], z, stay[1], :, cut] = jnp.where(c == 0, first, second).astype(BF16)
+    for z in range(4):
         for xx in range(2):
             for yy in range(2):
                 at = 8 * z + 4 * xx + yy

time: 189 us -> 188 us (level)
  no operation moved by 1% of the time
where the time goes in v3:
time: 188 us
  waiting for transfers between devices  71 us (38%)
  Pallas kernels  70.6 us (38%)
  starting transfers between devices  40.2 us (21%)
  local copies, waits for them, and re-layouts  2.31 us (1%)
  other arithmetic  2.14 us (1%)
    ppermute x40, waiting for transfers between devices, send(): return lax.ppermute(value, AXES, perm)  71 us
    pallas_call x13, Pallas kernels, call(): pl.pallas_call(kernel, name=name, in_specs=[pl.BlockSpec(memory_space=plt...  70.6 us
    ppermute x40, starting transfers between devices, send(): return lax.ppermute(value, AXES, perm)  40.2 us
  transfers between devices with their start and end apart: 40, of which 18 were waited for; matrix products, arithmetic and copies ran while one was open for 1% of the time, Pallas kernels for 34%

profile of v3, /device:TPU:0, one launch (start us, length us, event | category | flops | bytes accessed | tf_op | source)
XLA Modules:
  0.0 187.5 jit_solution(16768703132165281609)
XLA Ops:
  2.2 3.0 %collective-permute-start.4 = (bf16[2,256,768]{2,1,0:T(8,128)(2,1)S(1)}, bf16[2,256,768]{2,1,0:T(8,128)(2,1)S(1)}, u32[]{:S(2)}, u32[]{:S(2)}) collective-permute-start(bf16[2,256,768]{2,1,0:T(8,128)(2,1)S(1)} %constant_dynamic-slice_fusion.1), channel_id=1, source_target_pairs={{0,1},{1,0},{2,3},{3,2},{4,5},{5,4},{6,7},{7,6},{8,9},{9,8},{10,11... | collective-permute-start | bytes 2359304 | tf_op jit(solution)/shard_map/ppermute | solution.py:76
  5.4 3.7 %collective-permute-start.2 = (bf16[24,3200]{1,0:T(8,128)(2,1)S(1)}, bf16[24,3200]{1,0:T(8,128)(2,1)S(1)}, u32[]{:S(2)}, u32[]{:S(2)}) collective-permute-start(bf16[24,3200]{1,0:T(8,128)(2,1)S(1)} %pad_maximum_fusion.4), channel_id=1, source_target_pairs={{0,24},{1,25},{2,26},{3,27},{4,28},{5,29},{6,30},{7,31},{8,0},{9,1... | collective-permute-start | bytes 460808 | tf_op jit(solution)/shard_map/ppermute | solution.py:76
  11.6 3.7 %collective-permute-done.3 = bf16[96,768]{1,0:T(8,128)(2,1)S(1)} collective-permute-done((bf16[96,768]{1,0:T(8,128)(2,1)S(1)}, bf16[96,768]{1,0:T(8,128)(2,1)S(1)}, u32[]{:S(2)}, u32[]{:S(2)}) %collective-permute-start.3) | collective-permute-done | bytes 147488 | tf_op jit(solution)/shard_map/ppermute | solution.py:76
  15.3 6.6 %collective-permute-done.1 = bf16[24,3200]{1,0:T(8,128)(2,1)S(1)} collective-permute-done((bf16[24,3200]{1,0:T(8,128)(2,1)S(1)}, bf16[24,3200]{1,0:T(8,128)(2,1)S(1)}, u32[]{:S(2)}, u32[]{:S(2)}) %collective-permute-start.1) | collective-permute-done | bytes 153632 | tf_op jit(solution)/shard_map/ppermute | solution.py:76
  23.0 1.8 collective-permute-start.5
  27.9 6.6 %mix_norm.1 = (f32[1024,768]{1,0:T(8,128)S(1)}, f32[1024,1]{1,0:T(8,128)S(1)}) custom-call(s32[4]{0:T(128)S(1)} %pad_add_fusion.place_ref, bf16[4,256,768]{2,1,0:T(8,128)(2,1)S(1)} %copy-done.1, bf16[2,256,768]{2,1,0:T(8,128)(2,1)S(1)} %collective-permute-done.4.other_ref, bf16[1024,512]{1,0:T(8,128)(2,1)S(1)} %copy-done.4, bf16[1536,768]{1,0:T(8,128)(2,1)} %constant.108.hid_hbm), custom_call_target="tpu_custom_call" | custom-call | flops 4026531840 | bytes 7864320 | tf_op jit(solution)/shard_map/mix_norm/pallas_call | solution.py:150
  36.2 1.6 collective-permute-start.9
  38.2 14.2 %collective-permute-done.10.refs_3_ = bf16[4,96,768]{2,1,0:T(8,128)(2,1)S(1)} collective-permute-done((bf16[4,96,768]{2,1,0:T(8,128)(2,1)S(1)}, bf16[4,96,768]{2,1,0:T(8,128)(2,1)S(1)}, u32[]{:S(2)}, u32[]{:S(2)}) %collective-permute-start.10) | collective-permute-done | bytes 589856 | tf_op jit(solution)/shard_map/ppermute | solution.py:76
  53.0 2.6 %collective-permute-start.12 = (bf16[8,24,3200]{2,1,0:T(8,128)(2,1)S(1)}, bf16[8,24,3200]{2,1,0:T(8,128)(2,1)S(1)}, u32[]{:S(2)}, u32[]{:S(2)}) collective-permute-start(bf16[8,24,3200]{2,1,0:T(8,128)(2,1)S(1)} %collective-permute-done.9.refs_2_), channel_id=1, source_target_pairs={{0,2},{1,3},{2,0},{3,1},{4,6},{5,7},{6,4},{7,5},{8,10},{9,11},{10,... | collective-permute-start | bytes 3686408 | tf_op jit(solution)/shard_map/ppermute | solution.py:76
  56.3 2.2 %collective-permute-start.13 = (bf16[4,96,768]{2,1,0:T(8,128)(2,1)S(1)}, bf16[4,96,768]{2,1,0:T(8,128)(2,1)S(1)}, u32[]{:S(2)}, u32[]{:S(2)}) collective-permute-start(bf16[4,96,768]{2,1,0:T(8,128)(2,1)S(1)} %collective-permute-done.10.refs_3_), channel_id=1, source_target_pairs={{0,8},{1,9},{2,10},{3,11},{4,12},{5,13},{6,14},{7,15},{8,16},{9,17... | collective-permute-start | bytes 1769480 | tf_op jit(solution)/shard_map/ppermute | solution.py:76
  59.0 2.4 %first_weight.1 = (bf16[768,3072]{1,0:T(8,128)(2,1)S(1)}, f32[1,3072]{1,0:T(1,128)S(1)}, f32[8,768]{1,0:T(8,128)S(1)}, bf16[1024,768]{1,0:T(8,128)(2,1)S(1)}, bf16[768,1024]{1,0:T(8,128)(2,1)S(1)}) custom-call(s32[4]{0:T(128)S(1)} %pad_add_fusion.place_ref, f32[1024,768]{1,0:T(8,128)S(1)} %get-tuple-element.142.xhat_ref.refs_4_, ...), custom_call_target="tpu_custom_call" | custom-call | flops 1572864 | bytes 9830400 | tf_op jit(solution)/shard_map/first_weight/pallas_call | solution.py:150
  63.1 7.5 %ffn_in_gelu.1 = (bf16[1024,1536]{1,0:T(8,128)(2,1)S(1)}, bf16[1024,1536]{1,0:T(8,128)(2,1)S(1)}) custom-call(bf16[1024,768]{1,0:T(8,128)(2,1)S(1)} %get-tuple-element.160.low_ref, bf16[768,3072]{1,0:T(8,128)(2,1)S(1)} %get-tuple-element.152.w_ref.w_in_ref, f32[1,3072]{1,0:T(1,128)S(1)} %get-tuple-element.153.bias_ref), custom_call_target="tpu_custom_call" | custom-call | flops 2415919104 | bytes 6291456 | tf_op jit(solution)/shard_map/ffn_in_gelu/pallas_call | solution.py:150
  70.6 3.8 %collective-permute-done.13.refs_4_ = bf16[4,96,768]{2,1,0:T(8,128)(2,1)S(1)} collective-permute-done((bf16[4,96,768]{2,1,0:T(8,128)(2,1)S(1)}, bf16[4,96,768]{2,1,0:T(8,128)(2,1)S(1)}, u32[]{:S(2)}, u32[]{:S(2)}) %collective-permute-start.13) | collective-permute-done | bytes 589856 | tf_op jit(solution)/shard_map/ppermute | solution.py:76
  76.9 12.4 %ffn_in_out.1 = (bf16[1024,1536]{1,0:T(8,128)(2,1)S(1)}, bf16[1024,1536]{1,0:T(8,128)(2,1)S(1)}, bf16[3072,768]{1,0:T(8,128)(2,1)S(1)}, f32[1024,768]{1,0:T(8,128)S(1)}) custom-call(s32[4]{0:T(128)S(1)} %pad_add_fusion.place_ref, bf16[1024,768]{1,0:T(8,128)(2,1)S(1)} %get-tuple-element.160.low_ref, bf16[768,3072]{1,0:T(8,128)(2,1)S(1)} %get-tuple-element.152.w_ref.w_in_ref, ...), custom_call_target="tpu_custom_call" | custom-call | flops 6039797760 | bytes 12582912 | tf_op jit(solution)/shard_map/ffn_in_out/pallas_call | solution.py:150
  91.0 4.7 %ffn_out_norm.1 = (bf16[3072,768]{1,0:T(8,128)(2,1)S(1)}, bf16[2,256,768]{2,1,0:T(8,128)(2,1)S(1)}, bf16[2,256,768]{2,1,0:T(8,128)(2,1)S(1)}, f32[1024,768]{1,0:...) custom-call(s32[4]{0:T(128)S(1)} %pad_add_fusion.place_ref, ...), custom_call_target="tpu_custom_call", output_to_operand_aliasing={{0}: (3, {})} | custom-call | flops 1207959552 | bytes 23592960 | tf_op jit(solution)/shard_map/ffn_out_norm/pallas_call | solution.py:150
  95.7 2.0 %grad_w_out.2 = (bf16[1,4,96,768]{3,2,1,0:T(8,128)(2,1)S(1)}, bf16[1,4,96,768]{3,2,1,0:T(8,128)(2,1)S(1)}) custom-call(s32[4]{0:T(128)S(1)} %pad_add_fusion.place_ref, bf16[1024,1536]{1,0:T(8,128)(2,1)S(1)} %get-tuple-element.159.act_0_ref.refs_0_, bf16[1024,1536]{1,0:T(8,128)(2,1)S(1)} %get-tuple-element.166.refs_1_.act_1_ref, ...), custom_call_target="tpu_custom_call" | custom-call | flops 1207959552 | bytes 1572864 | tf_op jit(solution)/shard_map/grad_w_out/pallas_call | solution.py:150
  97.9 5.1 %grad_w_out.3 = (bf16[3,4,96,768]{3,2,1,0:T(8,128)(2,1)S(1)}, bf16[3,4,96,768]{3,2,1,0:T(8,128)(2,1)S(1)}) custom-call(s32[4]{0:T(128)S(1)} %pad_add_fusion.place_ref, bf16[1024,1536]{1,0:T(8,128)(2,1)S(1)} %get-tuple-element.159.act_0_ref.refs_0_, bf16[1024,1536]{1,0:T(8,128)(2,1)S(1)} %get-tuple-element.166.refs_1_.act_1_ref, ...), custom_call_target="tpu_custom_call" | custom-call | flops 3623878656 | bytes 4718592 | tf_op jit(solution)/shard_map/grad_w_out/pallas_call | solution.py:150
  103.6 1.6 collective-permute-start.25
  105.8 18.9 %ffn_back.1 = (bf16[1024,768]{1,0:T(8,128)(2,1)S(1)}, f32[1024,768]{1,0:T(8,128)S(1)}, bf16[2,4,2,24,3200]{4,3,2,1,0:T(8,128)(2,1)S(1)}, bf16[2,4,2,24,3200]{4,3,2,1,0:T(8,128)(2,1)S(1)}) custom-call(s32[4]{0:T(128)S(1)} %pad_add_fusion.place_ref, bf16[1024,768]{1,0:T(8,128)(2,1)S(1)} %get-tuple-element.189.low_ref, ...), custom_call_target="tpu_custom_call" | custom-call | flops 14495514624 | bytes 28311552 | tf_op jit(solution)/shard_map/ffn_back/pallas_call | solution.py:150
  125.7 2.2 %collective-permute-done.27 = bf16[4,2,24,3200]{3,2,0,1:T(8,128)(2,1)S(1)} collective-permute-done((bf16[4,2,24,3200]{3,2,0,1:T(8,128)(2,1)S(1)}, bf16[4,2,24,3200]{3,2,0,1:T(8,128)(2,1)S(1)}, u32[]{:S(2)}, u32[]{:S(2)}) %collective-permute-start.27) | collective-permute-done | bytes 1228832 | tf_op jit(solution)/shard_map/ppermute | solution.py:76
  131.3 1.7 join_rows.3
  133.3 5.0 %mix_back.1 = (bf16[2,256,768]{2,1,0:T(8,128)(2,1)S(1)}, f32[2,256,768]{2,1,0:T(8,128)S(1)}) custom-call(s32[4]{0:T(128)S(1)} %pad_add_fusion.place_ref, bf16[1024,768]{1,0:T(8,128)(2,1)S(1)} %get-tuple-element.209.low_ref, f32[1024,768]{1,0:T(8,128)S(1)} %get-tuple-element.210.one_ref, bf16[768,1536]{1,0:T(8,128)(2,1)S(1)} %copy-done.2, ...), custom_call_target="tpu_custom_call" | custom-call | flops 4026531840 | bytes 7864320 | tf_op jit(solution)/shard_map/mix_back/pallas_call | solution.py:150
  138.3 8.5 %collective-permute-done.29 = bf16[4,96,768]{2,1,0:T(8,128)(2,1)S(1)} collective-permute-done((bf16[4,96,768]{2,1,0:T(8,128)(2,1)S(1)}, bf16[4,96,768]{2,1,0:T(8,128)(2,1)S(1)}, u32[]{:S(2)}, u32[]{:S(2)}) %collective-permute-start.29) | collective-permute-done | bytes 589856 | tf_op jit(solution)/shard_map/ppermute | solution.py:76
  149.1 1.6 collective-permute-start.33
  150.7 10.5 %collective-permute-done.33.refs_1_ = bf16[1,256,768]{2,1,0:T(8,128)(2,1)S(1)} collective-permute-done((bf16[1,256,768]{2,1,0:T(8,128)(2,1)S(1)}, bf16[1,256,768]{2,1,0:T(8,128)(2,1)S(1)}, u32[]{:S(2)}, u32[]{:S(2)}) %collective-permute-start.33) | collective-permute-done | bytes 393248 | tf_op jit(solution)/shard_map/ppermute | solution.py:76
  161.2 2.2 %collective-permute-done.32 = bf16[4,96,768]{2,1,0:T(8,128)(2,1)S(1)} collective-permute-done((bf16[4,96,768]{2,1,0:T(8,128)(2,1)S(1)}, bf16[4,96,768]{2,1,0:T(8,128)(2,1)S(1)}, u32[]{:S(2)}, u32[]{:S(2)}) %collective-permute-start.32) | collective-permute-done | bytes 589856 | tf_op jit(solution)/shard_map/ppermute | solution.py:76
  163.9 2.2 %collective-permute-start.37 = (bf16[1,256,768]{2,1,0:T(8,128)(2,1)S(1)}, bf16[1,256,768]{2,1,0:T(8,128)(2,1)S(1)}, u32[]{:S(2)}, u32[]{:S(2)}) collective-permute-start(bf16[1,256,768]{2,1,0:T(8,128)(2,1)S(1)} %get-tuple-element.222), channel_id=1, source_target_pairs={{0,1},{1,0},{2,3},{3,2},{4,5},{5,4},{6,7},{7,6},{8,9},{9,8},{10,11... | collective-permute-start | bytes 1179656 | tf_op jit(solution)/shard_map/ppermute | solution.py:76
  167.5 2.0 %join_rows.4.refs_1_ = f32[4,256,768]{2,1,0:T(8,128)} custom-call(s32[4]{0:T(128)S(1)} %pad_add_fusion.place_ref, f32[2,256,768]{2,1,0:T(8,128)S(1)} %get-tuple-element.223.refs_0_, bf16[1,256,768]{2,1,0:T(8,128)(2,1)S(1)} %collective-permute-done.33.refs_1_), custom_call_target="tpu_custom_call" | custom-call | bytes 6291456 | tf_op jit(solution)/shard_map/join_rows/pallas_call | solution.py:150
  169.5 4.3 %collective-permute-done.35.refs_1_ = bf16[24,3200]{1,0:T(8,128)(2,1)S(1)} collective-permute-done((bf16[24,3200]{1,0:T(8,128)(2,1)S(1)}, bf16[24,3200]{1,0:T(8,128)(2,1)S(1)}, u32[]{:S(2)}, u32[]{:S(2)}) %collective-permute-start.35) | collective-permute-done | bytes 153632 | tf_op jit(solution)/shard_map/ppermute | solution.py:76
  173.8 3.7 %collective-permute-done.34.refs_0_ = bf16[24,3200]{1,0:T(8,128)(2,1)S(1)} collective-permute-done((bf16[24,3200]{1,0:T(8,128)(2,1)S(1)}, bf16[24,3200]{1,0:T(8,128)(2,1)S(1)}, u32[]{:S(2)}, u32[]{:S(2)}) %collective-permute-start.34) | collective-permute-done | bytes 153632 | tf_op jit(solution)/shard_map/ppermute | solution.py:76
  180.6 3.7 %collective-permute-done.38.refs_4_ = bf16[96,768]{1,0:T(8,128)(2,1)S(1)} collective-permute-done((bf16[96,768]{1,0:T(8,128)(2,1)S(1)}, bf16[96,768]{1,0:T(8,128)(2,1)S(1)}, u32[]{:S(2)}, u32[]{:S(2)}) %collective-permute-start.38) | collective-permute-done | bytes 147488 | tf_op jit(solution)/shard_map/ppermute | solution.py:76
  184.4 2.2 %collective-permute-done.39.refs_2_ = bf16[24,3200]{1,0:T(8,128)(2,1)S(1)} collective-permute-done((bf16[24,3200]{1,0:T(8,128)(2,1)S(1)}, bf16[24,3200]{1,0:T(8,128)(2,1)S(1)}, u32[]{:S(2)}, u32[]{:S(2)}) %collective-permute-start.39) | collective-permute-done | bytes 153632 | tf_op jit(solution)/shard_map/ppermute | solution.py:76
  (116 shorter events, 32.2 us)
Async XLA Ops:
  2.2 20.6 %collective-permute-start.4 = (bf16[2,256,768]{2,1,0:T(8,128)(2,1)S(1)}, bf16[2,256,768]{2,1,0:T(8,128)(2,1)S(1)}, u32[]{:S(2)}, u32[]{:S(2)}) collective-permute-start(bf16[2,256,768]{2,1,0:T(8,128)(2,1)S(1)} %constant_dynamic-slice_fusion.1), channel_id=1, source_target_pairs={{0,1},{1,0},{2,3},{3,2},{4,5},{5,4},{6,7},{7,6},{8,9},{9,8},{10,11... | collective-permute-start | bytes 2359304 | tf_op jit(solution)/shard_map/ppermute | solution.py:76
  5.4 9.8 %collective-permute-start.2 = (bf16[24,3200]{1,0:T(8,128)(2,1)S(1)}, bf16[24,3200]{1,0:T(8,128)(2,1)S(1)}, u32[]{:S(2)}, u32[]{:S(2)}) collective-permute-start(bf16[24,3200]{1,0:T(8,128)(2,1)S(1)} %pad_maximum_fusion.4), channel_id=1, source_target_pairs={{0,24},{1,25},{2,26},{3,27},{4,28},{5,29},{6,30},{7,31},{8,0},{9,1... | collective-permute-start | bytes 460808 | tf_op jit(solution)/shard_map/ppermute | solution.py:76
  9.1 12.7 %collective-permute-start.1 = (bf16[24,3200]{1,0:T(8,128)(2,1)S(1)}, bf16[24,3200]{1,0:T(8,128)(2,1)S(1)}, u32[]{:S(2)}, u32[]{:S(2)}) collective-permute-start(bf16[24,3200]{1,0:T(8,128)(2,1)S(1)} %pad_maximum_fusion.4), channel_id=1, source_target_pairs={{0,16},{1,17},{2,18},{3,19},{4,20},{5,21},{6,22},{7,23},{8,24},{9,... | collective-permute-start | bytes 460808 | tf_op jit(solution)/shard_map/ppermute | solution.py:76
  9.1 12.7 %collective-permute-start = (bf16[24,3200]{1,0:T(8,128)(2,1)S(1)}, bf16[24,3200]{1,0:T(8,128)(2,1)S(1)}, u32[]{:S(2)}, u32[]{:S(2)}) collective-permute-start(bf16[24,3200]{1,0:T(8,128)(2,1)S(1)} %pad_maximum_fusion.4), channel_id=1, source_target_pairs={{0,8},{1,9},{2,10},{3,11},{4,12},{5,13},{6,14},{7,15},{8,16},{9,17... | collective-permute-start | bytes 460808 | tf_op jit(solution)/shard_map/ppermute | solution.py:76
  23.0 13.0 %collective-permute-start.8 = (bf16[4,24,3200]{2,1,0:T(8,128)(2,1)S(1)}, bf16[4,24,3200]{2,1,0:T(8,128)(2,1)S(1)}, u32[]{:S(2)}, u32[]{:S(2)}) collective-permute-start(bf16[4,24,3200]{2,1,0:T(8,128)(2,1)S(1)} %pad_maximum_fusion.1.refs_0_), channel_id=1, source_target_pairs={{0,2},{1,3},{2,0},{3,1},{4,6},{5,7},{6,4},{7,5},{8,10},{9,11},{10,... | collective-permute-start | bytes 1843208 | tf_op jit(solution)/shard_map/ppermute | solution.py:76
  23.0 13.0 %collective-permute-start.5 = (bf16[4,24,3200]{2,1,0:T(8,128)(2,1)S(1)}, bf16[4,24,3200]{2,1,0:T(8,128)(2,1)S(1)}, u32[]{:S(2)}, u32[]{:S(2)}) collective-permute-start(bf16[4,24,3200]{2,1,0:T(8,128)(2,1)S(1)} %pad_maximum_fusion.1.refs_0_), channel_id=1, source_target_pairs={{0,4},{1,5},{2,3},{3,2},{4,0},{5,1},{6,7},{7,6},{8,12},{9,13},{10,... | collective-permute-start | bytes 1843208 | tf_op jit(solution)/shard_map/ppermute | solution.py:76
  24.8 9.9 %collective-permute-start.7 = (bf16[2,96,768]{2,1,0:T(8,128)(2,1)S(1)}, bf16[2,96,768]{2,1,0:T(8,128)(2,1)S(1)}, u32[]{:S(2)}, u32[]{:S(2)}) collective-permute-start(bf16[2,96,768]{2,1,0:T(8,128)(2,1)S(1)} %pad_maximum_fusion.3.refs_0_), channel_id=1, source_target_pairs={{0,1},{1,0},{2,3},{3,2},{4,5},{5,4},{6,7},{7,6},{8,9},{9,8},{10,11... | collective-permute-start | bytes 884744 | tf_op jit(solution)/shard_map/ppermute | solution.py:76
  26.3 9.7 %collective-permute-start.6 = (bf16[2,96,768]{2,1,0:T(8,128)(2,1)S(1)}, bf16[2,96,768]{2,1,0:T(8,128)(2,1)S(1)}, u32[]{:S(2)}, u32[]{:S(2)}) collective-permute-start(bf16[2,96,768]{2,1,0:T(8,128)(2,1)S(1)} %pad_maximum_fusion.3.refs_0_), channel_id=1, source_target_pairs={{0,8},{1,9},{2,10},{3,11},{4,12},{5,13},{6,14},{7,15},{8,16},{9,17... | collective-permute-start | bytes 884744 | tf_op jit(solution)/shard_map/ppermute | solution.py:76
  36.2 16.8 %collective-permute-start.9 = (bf16[8,24,3200]{2,1,0:T(8,128)(2,1)S(1)}, bf16[8,24,3200]{2,1,0:T(8,128)(2,1)S(1)}, u32[]{:S(2)}, u32[]{:S(2)}) collective-permute-start(bf16[8,24,3200]{2,1,0:T(8,128)(2,1)S(1)} %pad_maximum_fusion), channel_id=1, source_target_pairs={{0,1},{1,0},{2,6},{3,7},{4,5},{5,4},{6,2},{7,3},{8,9},{9,8},{10,14... | collective-permute-start | bytes 3686408 | tf_op jit(solution)/shard_map/ppermute | solution.py:76
  37.8 14.6 %collective-permute-start.10 = (bf16[4,96,768]{2,1,0:T(8,128)(2,1)S(1)}, bf16[4,96,768]{2,1,0:T(8,128)(2,1)S(1)}, u32[]{:S(2)}, u32[]{:S(2)}) collective-permute-start(bf16[4,96,768]{2,1,0:T(8,128)(2,1)S(1)} %pad_maximum_fusion.2), channel_id=1, source_target_pairs={{0,8},{1,9},{2,10},{3,11},{4,12},{5,13},{6,14},{7,15},{8,16},{9,17... | collective-permute-start | bytes 1769480 | tf_op jit(solution)/shard_map/ppermute | solution.py:76
  55.7 6.9 %collective-permute-start.15 = (bf16[2,96,768]{2,1,0:T(8,128)(2,1)S(1)}, bf16[2,96,768]{2,1,0:T(8,128)(2,1)S(1)}, u32[]{:S(2)}, u32[]{:S(2)}) collective-permute-start(bf16[2,96,768]{2,1,0:T(8,128)(2,1)S(1)} %pad_maximum_fusion.3.refs_0_), channel_id=1, source_target_pairs={{0,2},{1,3},{2,0},{3,1},{4,6},{5,7},{6,4},{7,5},{8,10},{9,11},{10,... | collective-permute-start | bytes 884744 | tf_op jit(solution)/shard_map/ppermute | solution.py:76
  56.3 14.3 %collective-permute-start.18 = (bf16[4,96,768]{2,1,0:T(8,128)(2,1)S(1)}, bf16[4,96,768]{2,1,0:T(8,128)(2,1)S(1)}, u32[]{:S(2)}, u32[]{:S(2)}) collective-permute-start(bf16[4,96,768]{2,1,0:T(8,128)(2,1)S(1)} %collective-permute-done.10.refs_3_), channel_id=1, source_target_pairs={{0,2},{1,3},{2,0},{3,1},{4,6},{5,7},{6,4},{7,5},{8,10},{9,11},{10,... | collective-permute-start | bytes 1769480 | tf_op jit(solution)/shard_map/ppermute | solution.py:76
  56.3 18.1 %collective-permute-start.13 = (bf16[4,96,768]{2,1,0:T(8,128)(2,1)S(1)}, bf16[4,96,768]{2,1,0:T(8,128)(2,1)S(1)}, u32[]{:S(2)}, u32[]{:S(2)}) collective-permute-start(bf16[4,96,768]{2,1,0:T(8,128)(2,1)S(1)} %collective-permute-done.10.refs_3_), channel_id=1, source_target_pairs={{0,8},{1,9},{2,10},{3,11},{4,12},{5,13},{6,14},{7,15},{8,16},{9,17... | collective-permute-start | bytes 1769480 | tf_op jit(solution)/shard_map/ppermute | solution.py:76
  61.5 12.9 %collective-permute-start.14 = (bf16[1,256,768]{2,1,0:T(8,128)(2,1)S(1)}, bf16[1,256,768]{2,1,0:T(8,128)(2,1)S(1)}, u32[]{:S(2)}, u32[]{:S(2)}) collective-permute-start(bf16[1,256,768]{2,1,0:T(8,128)(2,1)S(1)} %get-tuple-element.251), channel_id=1, source_target_pairs={{0,1},{1,0},{2,3},{3,2},{4,5},{5,4},{6,7},{7,6},{8,9},{9,8},{10,11... | collective-permute-start | bytes 1179656 | tf_op jit(solution)/shard_map/ppermute | solution.py:76
  62.6 8.0 %collective-permute-start.16 = (bf16[2,96,768]{2,1,0:T(8,128)(2,1)S(1)}, bf16[2,96,768]{2,1,0:T(8,128)(2,1)S(1)}, u32[]{:S(2)}, u32[]{:S(2)}) collective-permute-start(bf16[2,96,768]{2,1,0:T(8,128)(2,1)S(1)} %collective-permute-done.7.refs_1_), channel_id=1, source_target_pairs={{0,2},{1,3},{2,0},{3,1},{4,6},{5,7},{6,4},{7,5},{8,10},{9,11},{10,... | collective-permute-start | bytes 884744 | tf_op jit(solution)/shard_map/ppermute | solution.py:76
  62.6 8.0 %collective-permute-start.17 = (bf16[2,96,768]{2,1,0:T(8,128)(2,1)S(1)}, bf16[2,96,768]{2,1,0:T(8,128)(2,1)S(1)}, u32[]{:S(2)}, u32[]{:S(2)}) collective-permute-start(bf16[2,96,768]{2,1,0:T(8,128)(2,1)S(1)} %collective-permute-done.6.refs_2_), channel_id=1, source_target_pairs={{0,2},{1,3},{2,0},{3,1},{4,6},{5,7},{6,4},{7,5},{8,10},{9,11},{10,... | collective-permute-start | bytes 884744 | tf_op jit(solution)/shard_map/ppermute | solution.py:76
  74.5 14.9 %collective-permute-start.20 = (bf16[2,96,768]{2,1,0:T(8,128)(2,1)S(1)}, bf16[2,96,768]{2,1,0:T(8,128)(2,1)S(1)}, u32[]{:S(2)}, u32[]{:S(2)}) collective-permute-start(bf16[2,96,768]{2,1,0:T(8,128)(2,1)S(1)} %slice.67), channel_id=1, source_target_pairs={{0,8},{1,9},{2,10},{3,11},{4,12},{5,13},{6,14},{7,15},{8,16},{9,17... | collective-permute-start | bytes 884744 | tf_op jit(solution)/shard_map/ppermute | solution.py:76
  75.4 14.0 %collective-permute-start.21 = (bf16[1,256,768]{2,1,0:T(8,128)(2,1)S(1)}, bf16[1,256,768]{2,1,0:T(8,128)(2,1)S(1)}, u32[]{:S(2)}, u32[]{:S(2)}) collective-permute-start(bf16[1,256,768]{2,1,0:T(8,128)(2,1)S(1)} %get-tuple-element.169), channel_id=1, source_target_pairs={{0,1},{1,0},{2,3},{3,2},{4,5},{5,4},{6,7},{7,6},{8,9},{9,8},{10,11... | collective-permute-start | bytes 1179656 | tf_op jit(solution)/shard_map/ppermute | solution.py:76
  103.2 21.5 %collective-permute-start.24 = (bf16[3,4,96,768]{3,2,1,0:T(8,128)(2,1)S(1)}, bf16[3,4,96,768]{3,2,1,0:T(8,128)(2,1)S(1)}, u32[]{:S(2)}, u32[]{:S(2)}) collective-permute-start(bf16[3,4,96,768]{3,2,1,0:T(8,128)(2,1)S(1)} %get-tuple-element.186), channel_id=1, source_target_pairs={{0,2},{1,3},{2,0},{3,1},{4,6},{5,7},{6,4},{7,5},{8,10},{9,11},{10,... | collective-permute-start | bytes 5308424 | tf_op jit(solution)/shard_map/ppermute | solution.py:76
  103.6 21.0 %collective-permute-start.25 = (bf16[4,96,768]{2,1,0:T(8,128)(2,1)S(1)}, bf16[4,96,768]{2,1,0:T(8,128)(2,1)S(1)}, u32[]{:S(2)}, u32[]{:S(2)}) collective-permute-start(bf16[4,96,768]{2,1,0:T(8,128)(2,1)S(1)} %add_bitcast_fusion), channel_id=1, source_target_pairs={{0,8},{1,9},{2,10},{3,11},{4,12},{5,13},{6,14},{7,15},{8,16},{9,17... | collective-permute-start | bytes 1769480 | tf_op jit(solution)/shard_map/ppermute | solution.py:76
  105.3 19.5 %collective-permute-start.26 = (bf16[2,256,768]{2,1,0:T(8,128)(2,1)S(1)}, bf16[2,256,768]{2,1,0:T(8,128)(2,1)S(1)}, u32[]{:S(2)}, u32[]{:S(2)}) collective-permute-start(bf16[2,256,768]{2,1,0:T(8,128)(2,1)S(1)} %get-tuple-element.188), channel_id=1, source_target_pairs={{0,1},{1,0},{2,3},{3,2},{4,5},{5,4},{6,7},{7,6},{8,9},{9,8},{10,11... | collective-permute-start | bytes 2359304 | tf_op jit(solution)/shard_map/ppermute | solution.py:76
  125.0 13.4 %collective-permute-start.30 = (bf16[4,2,24,3200]{3,2,0,1:T(8,128)(2,1)S(1)}, bf16[4,2,24,3200]{3,2,0,1:T(8,128)(2,1)S(1)}, u32[]{:S(2)}, u32[]{:S(2)}) collective-permute-start(bf16[4,2,24,3200]{3,2,0,1:T(8,128)(2,1)S(1)} %get-tuple-element.244), channel_id=1, source_target_pairs={{0,2},{1,3},{2,0},{3,1},{4,6},{5,7},{6,4},{7,5},{8,10},{9,11},{10,... | collective-permute-start | bytes 3686408 | tf_op jit(solution)/shard_map/ppermute | solution.py:76
  128.2 18.7 %collective-permute-start.28 = (bf16[4,2,24,3200]{3,2,0,1:T(8,128)(2,1)S(1)}, bf16[4,2,24,3200]{3,2,0,1:T(8,128)(2,1)S(1)}, u32[]{:S(2)}, u32[]{:S(2)}) collective-permute-start(bf16[4,2,24,3200]{3,2,0,1:T(8,128)(2,1)S(1)} %fusion.1), channel_id=1, source_target_pairs={{0,1},{1,0},{2,6},{3,7},{4,5},{5,4},{6,2},{7,3},{8,9},{9,8},{10,14... | collective-permute-start | bytes 3686408 | tf_op jit(solution)/shard_map/ppermute | solution.py:76
  129.8 17.1 %collective-permute-start.29 = (bf16[4,96,768]{2,1,0:T(8,128)(2,1)S(1)}, bf16[4,96,768]{2,1,0:T(8,128)(2,1)S(1)}, u32[]{:S(2)}, u32[]{:S(2)}) collective-permute-start(bf16[4,96,768]{2,1,0:T(8,128)(2,1)S(1)} %bitcast_add_fusion.2), channel_id=1, source_target_pairs={{0,8},{1,9},{2,10},{3,11},{4,12},{5,13},{6,14},{7,15},{8,16},{9,17... | collective-permute-start | bytes 1769480 | tf_op jit(solution)/shard_map/ppermute | solution.py:76
  147.1 16.3 %collective-permute-start.32 = (bf16[4,96,768]{2,1,0:T(8,128)(2,1)S(1)}, bf16[4,96,768]{2,1,0:T(8,128)(2,1)S(1)}, u32[]{:S(2)}, u32[]{:S(2)}) collective-permute-start(bf16[4,96,768]{2,1,0:T(8,128)(2,1)S(1)} %fusion.3), channel_id=1, source_target_pairs={{0,8},{1,9},{2,10},{3,11},{4,12},{5,13},{6,14},{7,15},{8,16},{9,17... | collective-permute-start | bytes 1769480 | tf_op jit(solution)/shard_map/ppermute | solution.py:76
  147.7 15.8 %collective-permute-start.31 = (bf16[4,24,3200]{2,1,0:T(8,128)(2,1)S(1)}, bf16[4,24,3200]{2,1,0:T(8,128)(2,1)S(1)}, u32[]{:S(2)}, u32[]{:S(2)}) collective-permute-start(bf16[4,24,3200]{2,1,0:T(8,128)(2,1)S(1)} %fusion.4), channel_id=1, source_target_pairs={{0,4},{1,5},{2,3},{3,2},{4,0},{5,1},{6,7},{7,6},{8,12},{9,13},{10,... | collective-permute-start | bytes 1843208 | tf_op jit(solution)/shard_map/ppermute | solution.py:76
  149.1 12.1 %collective-permute-start.33 = (bf16[1,256,768]{2,1,0:T(8,128)(2,1)S(1)}, bf16[1,256,768]{2,1,0:T(8,128)(2,1)S(1)}, u32[]{:S(2)}, u32[]{:S(2)}) collective-permute-start(bf16[1,256,768]{2,1,0:T(8,128)(2,1)S(1)} %get-tuple-element.249), channel_id=1, source_target_pairs={{0,1},{1,0},{2,3},{3,2},{4,5},{5,4},{6,7},{7,6},{8,9},{9,8},{10,11... | collective-permute-start | bytes 1179656 | tf_op jit(solution)/shard_map/ppermute | solution.py:76
  163.8 13.7 %collective-permute-start.36 = (bf16[2,96,768]{2,1,0:T(8,128)(2,1)S(1)}, bf16[2,96,768]{2,1,0:T(8,128)(2,1)S(1)}, u32[]{:S(2)}, u32[]{:S(2)}) collective-permute-start(bf16[2,96,768]{2,1,0:T(8,128)(2,1)S(1)} %slice.123), channel_id=1, source_target_pairs={{0,4},{1,5},{2,6},{3,7},{4,0},{5,1},{6,2},{7,3},{8,12},{9,13},{10,... | collective-permute-start | bytes 884744 | tf_op jit(solution)/shard_map/ppermute | solution.py:76
  163.9 13.7 %collective-permute-start.37 = (bf16[1,256,768]{2,1,0:T(8,128)(2,1)S(1)}, bf16[1,256,768]{2,1,0:T(8,128)(2,1)S(1)}, u32[]{:S(2)}, u32[]{:S(2)}) collective-permute-start(bf16[1,256,768]{2,1,0:T(8,128)(2,1)S(1)} %get-tuple-element.222), channel_id=1, source_target_pairs={{0,1},{1,0},{2,3},{3,2},{4,5},{5,4},{6,7},{7,6},{8,9},{9,8},{10,11... | collective-permute-start | bytes 1179656 | tf_op jit(solution)/shard_map/ppermute | solution.py:76
  166.1 7.7 %collective-permute-start.35 = (bf16[24,3200]{1,0:T(8,128)(2,1)S(1)}, bf16[24,3200]{1,0:T(8,128)(2,1)S(1)}, u32[]{:S(2)}, u32[]{:S(2)}) collective-permute-start(bf16[24,3200]{1,0:T(8,128)(2,1)S(1)} %get-tuple-element.246), channel_id=1, source_target_pairs={{0,24},{1,25},{2,26},{3,27},{4,28},{5,29},{6,30},{7,31},{8,0},{9,1... | collective-permute-start | bytes 460808 | tf_op jit(solution)/shard_map/ppermute | solution.py:76
  167.5 10.0 %collective-permute-start.34 = (bf16[24,3200]{1,0:T(8,128)(2,1)S(1)}, bf16[24,3200]{1,0:T(8,128)(2,1)S(1)}, u32[]{:S(2)}, u32[]{:S(2)}) collective-permute-start(bf16[24,3200]{1,0:T(8,128)(2,1)S(1)} %get-tuple-element.247), channel_id=1, source_target_pairs={{0,16},{1,17},{2,18},{3,19},{4,20},{5,21},{6,22},{7,23},{8,24},{9,... | collective-permute-start | bytes 460808 | tf_op jit(solution)/shard_map/ppermute | solution.py:76
  178.5 8.1 %collective-permute-start.39 = (bf16[24,3200]{1,0:T(8,128)(2,1)S(1)}, bf16[24,3200]{1,0:T(8,128)(2,1)S(1)}, u32[]{:S(2)}, u32[]{:S(2)}) collective-permute-start(bf16[24,3200]{1,0:T(8,128)(2,1)S(1)} %fusion.7), channel_id=1, source_target_pairs={{0,8},{1,9},{2,10},{3,11},{4,12},{5,13},{6,14},{7,15},{8,16},{9,17... | collective-permute-start | bytes 460808 | tf_op jit(solution)/shard_map/ppermute | solution.py:76
  (21 other events, 156.3 us)
